TPU v7x, 512 devices: a whole 4x8x8 slice. The times are simulated.
512 devices in a mesh: gx: 16 (over y, core), gy: 8 (over z), gz: 4 (over x).
Axes of the slice: x: 4, y: 8, z: 8, core: 2. Of those that a mesh axis runs over, the one named last changes fastest.
Arguments:
- source_field: float32 [2, 256, 128, 512], P(None, 'gx', 'gy', 'gz'), may hold values from -6 to 6
- mach_number: bfloat16 [256, 128, 512], P('gx', 'gy', 'gz'), may hold values from 0.14941406 to 0.59765625
Outputs:
- correction: float32 [2, 256, 128, 512], P(None, 'gx', 'gy', 'gz')
All inputs are finite; a program needn't handle non-finite values.
Results may differ from a plain program's by a relative error of at most 0.0003.
Values sent between devices are 32-bit elements; how exact they have to be, the bound alone decides.
No kernel may reach another device: no remote copies, remote signals or barrier semaphores. Data moves between devices by JAX's collectives and lax.ppermute only.
A program may use at most 128 MiB of HBM per device.

v0:
```python
import jax
import jax.numpy as jnp
from jax import lax
from jax.sharding import PartitionSpec as P

LEVELS = 5
POST = 2
COARSE_SWEEPS = 6


wave_step = 0.25
jacobi_weight = 0.5


def extended(block, sides, width):
    for axis, dim in sides:
        count = lax.axis_size(axis)
        forward = [(i, i + 1) for i in range(count - 1)]
        backward = [(target, source) for source, target in forward]
        low = lax.ppermute(
            lax.slice_in_dim(block, block.shape[dim] - width, None, axis=dim), axis, forward
        )
        high = lax.ppermute(lax.slice_in_dim(block, 0, width, axis=dim), axis, backward)
        block = jnp.concatenate([low, block, high], axis=dim)
    return block


def complex_times(values, factor):
    real_part = values[0] * factor[0] - values[1] * factor[1]
    imaginary = values[0] * factor[1] + values[1] * factor[0]
    return jnp.stack([real_part, imaginary])


def inverse_diagonal(mach_field, grid_level):
    diffusion_scale = 0.25**grid_level
    wave_square = wave_step * wave_step
    axial_weight = 1.0 - mach_field * mach_field
    diagonal_real = diffusion_scale * (2.0 * axial_weight + 4.0) - wave_square
    diagonal_imaginary = 0.5 * wave_square
    modulus = diagonal_real * diagonal_real + diagonal_imaginary * diagonal_imaginary
    return jnp.stack([diagonal_real / modulus, -diagonal_imaginary / modulus])


def operate(padded, mach_field, grid_level):
    centre = padded[:, 1:-1, 1:-1, 1:-1]
    east_cells = padded[:, 2:, 1:-1, 1:-1]
    west_cells = padded[:, :-2, 1:-1, 1:-1]
    north_cells = padded[:, 1:-1, 2:, 1:-1]
    south_cells = padded[:, 1:-1, :-2, 1:-1]
    upper_cells = padded[:, 1:-1, 1:-1, 2:]
    lower_cells = padded[:, 1:-1, 1:-1, :-2]
    diffusion_scale = 0.25**grid_level
    axial_weight = 1.0 - mach_field * mach_field
    spread = diffusion_scale * (
        axial_weight * (2.0 * centre - east_cells - west_cells)
        + (2.0 * centre - north_cells - south_cells)
        + (2.0 * centre - upper_cells - lower_cells)
    )
    advect = wave_step * 0.5**grid_level * mach_field
    axial_slope = east_cells - west_cells
    wave_square = wave_step * wave_step
    real_part = spread[0] + advect * axial_slope[1] - wave_square * (centre[0] + 0.5 * centre[1])
    imaginary = spread[1] - advect * axial_slope[0] - wave_square * (centre[1] - 0.5 * centre[0])
    return jnp.stack([real_part, imaginary])


def jacobi_step(solution, padded, source, mach_field, inverse, grid_level):
    return solution + jacobi_weight * complex_times(
        source - operate(padded, mach_field, grid_level), inverse
    )


def restrict(values):
    leading = values.shape[:-3]
    leading_rank = len(leading)
    first_length, second_length, third_length = values.shape[-3:]
    grouped = values.reshape(
        leading + (first_length // 2, 2, second_length // 2, 2, third_length // 2, 2)
    )
    return grouped.mean(axis=(leading_rank + 1, leading_rank + 3, leading_rank + 5))


def prolong(values):
    leading = values.shape[:-3]
    first_length, second_length, third_length = values.shape[-3:]
    expanded = values[..., :, None, :, None, :, None]
    expanded = jnp.broadcast_to(
        expanded, leading + (first_length, 2, second_length, 2, third_length, 2)
    )
    return expanded.reshape(leading + (2 * first_length, 2 * second_length, 2 * third_length))


def sweep_halo(solution):
    return extended(solution, (("gx", 1), ("gy", 2), ("gz", 3)), 1)


def coarse_solve(source, mach_field, grid_level):
    inverse = inverse_diagonal(mach_field, grid_level)
    solution = jacobi_weight * complex_times(source, inverse)
    for sweep_index in range(COARSE_SWEEPS - 1):
        padded = extended(solution, (("gx", 1), ("gy", 2), ("gz", 3)), 1)
        solution = jacobi_step(solution, padded, source, mach_field, inverse, grid_level)
    return solution


def multigrid(source, mach_levels, grid_level):
    mach_field = mach_levels[grid_level]
    if grid_level == LEVELS - 1:
        return coarse_solve(source, mach_field, grid_level)
    inverse = inverse_diagonal(mach_field, grid_level)
    solution = jacobi_weight * complex_times(source, inverse)
    solution = jacobi_step(solution, sweep_halo(solution), source, mach_field, inverse, grid_level)
    padded = extended(solution, (("gx", 1), ("gy", 2), ("gz", 3)), 1)
    residual = source - operate(padded, mach_field, grid_level)
    coarse = multigrid(restrict(residual), mach_levels, grid_level + 1)
    solution = solution + prolong(coarse)
    for sweep_index in range(POST):
        solution = jacobi_step(
            solution, sweep_halo(solution), source, mach_field, inverse, grid_level
        )
    return solution


def shards(source_field, mach_number):
    mach_levels = [mach_number.astype(jnp.float32)]
    for grid_level in range(1, LEVELS):
        mach_levels.append(restrict(mach_levels[-1]))
    return multigrid(source_field, mach_levels, 0)


def solution(mesh):
    return jax.shard_map(
        shards,
        mesh=mesh,
        in_specs=(P(None, "gx", "gy", "gz"), P("gx", "gy", "gz")),
        out_specs=P(None, "gx", "gy", "gz"),
        check_vma=False,
    )
```

profile of v0, /device:TPU:230, one launch (start us, length us, event | category | flops | bytes accessed | tf_op | source)
XLA Modules:
  0.0 619.5 jit_solution(9962739222145129856)
XLA Ops:
  11.3 5.5 collective-permute-start.3
  22.7 5.4 collective-permute-done.4
  43.2 5.1 collective-permute-start.9
  48.3 9.7 %reshape.1671 = f32[8,2,8,2,64,2]{5,4,3,2,1,0:T(8,128)} reshape(bf16[16,16,128]{2,1,0:T(8,128)(2,1)S(1)} %copy-done.1) | data formatting | bytes 196608 | tf_op jit(solution)/shard_map/reshape | solution.py:77
  66.0 5.2 collective-permute-done.10
  75.9 18.1 %reshape.1670 = f32[2,8,2,8,2,64,2]{6,5,4,3,2,1,0:T(8,128)} reshape(f32[2,16,16,128]{3,2,1,0:T(8,128)S(1)} %maximum_subtract_fusion.2) | data formatting | bytes 524288 | tf_op jit(solution)/shard_map/reshape | solution.py:77
  94.0 7.0 %reduce_sum.86 = f32[2,8,8,64]{3,2,1,0:T(8,128)S(1)} reduce(f32[2,8,2,8,2,64,2]{6,5,4,3,2,1,0:T(8,128)} %reshape.1670, f32[]{:T(128)} %constant.31.clone.1), dimensions={2,4,6}, to_apply=%region_0.0 | reduce | flops 57344 | bytes 294916 | tf_op jit(solution)/shard_map/reduce_sum | solution.py:80
  111.1 5.1 collective-permute-start.15
  123.0 4.4 collective-permute-done.17
  137.8 5.4 collective-permute-start.21
  152.0 4.4 collective-permute-done.23
  173.6 5.1 collective-permute-start.27
  183.8 4.3 collective-permute-done.29
  198.4 5.4 collective-permute-start.33
  208.8 4.3 collective-permute-done.35
  223.7 5.4 collective-permute-start.39
  233.8 4.2 collective-permute-done.41
  248.2 5.4 collective-permute-start.45
  258.4 4.2 collective-permute-done.47
  272.9 5.4 collective-permute-start.51
  283.0 4.2 collective-permute-done.53
  297.3 5.4 collective-permute-start.57
  307.4 4.2 collective-permute-done.59
  321.7 5.4 collective-permute-start.63
  331.8 4.2 collective-permute-done.65
  346.1 5.4 collective-permute-start.69
  356.2 4.2 collective-permute-done.71
  370.5 5.4 collective-permute-start.75
  380.6 4.2 collective-permute-done.77
  395.1 5.4 collective-permute-start.81
  405.3 4.2 collective-permute-done.83
  419.7 5.4 collective-permute-start.87
  429.8 4.2 collective-permute-done.89
  444.5 5.4 collective-permute-start.93
  455.0 4.3 collective-permute-done.95
  469.5 5.4 collective-permute-start.99
  480.0 4.3 collective-permute-done.101
  496.6 5.4 collective-permute-start.105
  508.3 4.4 collective-permute-done.107
  523.1 5.4 collective-permute-start.111
  534.7 4.4 collective-permute-done.113
  539.4 6.5 %broadcast_in_dim.17 = f32[2,8,2,8,2,64,2]{6,5,4,3,2,1,0:T(8,128)} broadcast(f32[2,8,8,64]{3,2,1,0:T(8,128)S(1)} %fusion.115), dimensions={0,1,3,5} | broadcast | bytes 294912 | tf_op jit(solution)/shard_map/broadcast_in_dim | solution.py:87
  545.9 12.7 %reshape.1674 = f32[2,16,16,128]{3,2,1,0:T(8,128)S(1)} reshape(f32[2,8,2,8,2,64,2]{6,5,4,3,2,1,0:T(8,128)} %broadcast_in_dim.17) | data formatting | bytes 524288 | tf_op jit(solution)/shard_map/reshape | solution.py:90
  568.9 5.4 collective-permute-start.117
  579.2 4.7 collective-permute-done.118
  583.9 4.2 collective-permute-done.119
  598.9 5.4 collective-permute-start.123
  609.3 4.7 collective-permute-done.124
  (496 shorter events, 353.5 us)
Async XLA Ops:
  9.3 7.4 %collective-permute-start.2 = (f32[2,18,1,128]{3,2,1,0:T(1,128)S(1)}, f32[2,18,1,128]{3,2,1,0:T(1,128)S(1)}, u32[]{:S(2)}, u32[]{:S(2)}) collective-permute-start(f32[2,18,1,128]{3,2,1,0:T(1,128)S(1)} %get-tuple-element.36), channel_id=1, source_target_pairs={{4,0},{8,4},{12,8},{16,12},{20,16},{24,20},{28,24},{5,1},{9,5},{13... | collective-permute-start | bytes 55304 | tf_op jit(solution)/shard_map/ppermute | solution.py:23
  11.3 6.9 %collective-permute-start.3 = (f32[2,18,1,128]{3,2,1,0:T(1,128)S(1)}, f32[2,18,1,128]{3,2,1,0:T(1,128)S(1)}, u32[]{:S(2)}, u32[]{:S(2)}) collective-permute-start(f32[2,18,1,128]{3,2,1,0:T(1,128)S(1)} %get-tuple-element.35), channel_id=1, source_target_pairs={{0,4},{4,8},{8,12},{12,16},{16,20},{20,24},{24,28},{1,5},{5,9},{9,... | collective-permute-start | bytes 55304 | tf_op jit(solution)/shard_map/ppermute | solution.py:20
  18.5 9.7 %collective-permute-start.4 = (f32[2,18,18,1]{3,2,1,0:T(8,128)S(1)}, f32[2,18,18,1]{3,2,1,0:T(8,128)S(1)}, u32[]{:S(2)}, u32[]{:S(2)}) collective-permute-start(f32[2,18,18,1]{3,2,1,0:T(8,128)S(1)} %get-tuple-element.19), channel_id=1, source_target_pairs={{1,0},{2,1},{3,2},{5,4},{6,5},{7,6},{9,8},{10,9},{11,10},{13,12},{... | collective-permute-start | bytes 7784 | tf_op jit(solution)/shard_map/ppermute | solution.py:23
  21.4 10.9 %collective-permute-start.5 = (f32[2,18,18,1]{3,2,1,0:T(8,128)S(1)}, f32[2,18,18,1]{3,2,1,0:T(8,128)S(1)}, u32[]{:S(2)}, u32[]{:S(2)}) collective-permute-start(f32[2,18,18,1]{3,2,1,0:T(8,128)S(1)} %get-tuple-element.20), channel_id=1, source_target_pairs={{0,1},{1,2},{2,3},{4,5},{5,6},{6,7},{8,9},{9,10},{10,11},{12,13},{... | collective-permute-start | bytes 7784 | tf_op jit(solution)/shard_map/ppermute | solution.py:20
  41.2 20.7 %collective-permute-start.8 = (f32[2,18,1,128]{3,2,1,0:T(1,128)S(1)}, f32[2,18,1,128]{3,2,1,0:T(1,128)S(1)}, u32[]{:S(2)}, u32[]{:S(2)}) collective-permute-start(f32[2,18,1,128]{3,2,1,0:T(1,128)S(1)} %get-tuple-element.34), channel_id=1, source_target_pairs={{4,0},{8,4},{12,8},{16,12},{20,16},{24,20},{28,24},{5,1},{9,5},{13... | collective-permute-start | bytes 55304 | tf_op jit(solution)/shard_map/ppermute | solution.py:23
  43.2 18.8 %collective-permute-start.9 = (f32[2,18,1,128]{3,2,1,0:T(1,128)S(1)}, f32[2,18,1,128]{3,2,1,0:T(1,128)S(1)}, u32[]{:S(2)}, u32[]{:S(2)}) collective-permute-start(f32[2,18,1,128]{3,2,1,0:T(1,128)S(1)} %get-tuple-element.33), channel_id=1, source_target_pairs={{0,4},{4,8},{8,12},{12,16},{16,20},{20,24},{24,28},{1,5},{5,9},{9,... | collective-permute-start | bytes 55304 | tf_op jit(solution)/shard_map/ppermute | solution.py:20
  62.3 9.0 %collective-permute-start.10 = (f32[2,18,18,1]{3,2,1,0:T(8,128)S(1)}, f32[2,18,18,1]{3,2,1,0:T(8,128)S(1)}, u32[]{:S(2)}, u32[]{:S(2)}) collective-permute-start(f32[2,18,18,1]{3,2,1,0:T(8,128)S(1)} %get-tuple-element.17), channel_id=1, source_target_pairs={{1,0},{2,1},{3,2},{5,4},{6,5},{7,6},{9,8},{10,9},{11,10},{13,12},{... | collective-permute-start | bytes 7784 | tf_op jit(solution)/shard_map/ppermute | solution.py:23
  64.7 10.7 %collective-permute-start.11 = (f32[2,18,18,1]{3,2,1,0:T(8,128)S(1)}, f32[2,18,18,1]{3,2,1,0:T(8,128)S(1)}, u32[]{:S(2)}, u32[]{:S(2)}) collective-permute-start(f32[2,18,18,1]{3,2,1,0:T(8,128)S(1)} %get-tuple-element.18), channel_id=1, source_target_pairs={{0,1},{1,2},{2,3},{4,5},{5,6},{6,7},{8,9},{9,10},{10,11},{12,13},{... | collective-permute-start | bytes 7784 | tf_op jit(solution)/shard_map/ppermute | solution.py:20
  109.2 7.1 %collective-permute-start.14 = (f32[2,10,1,64]{3,2,1,0:T(1,128)S(1)}, f32[2,10,1,64]{3,2,1,0:T(1,128)S(1)}, u32[]{:S(2)}, u32[]{:S(2)}) collective-permute-start(f32[2,10,1,64]{3,2,1,0:T(1,128)S(1)} %get-tuple-element.76), channel_id=1, source_target_pairs={{4,0},{8,4},{12,8},{16,12},{20,16},{24,20},{28,24},{5,1},{9,5},{13... | collective-permute-start | bytes 15368 | tf_op jit(solution)/shard_map/ppermute | solution.py:23
  120.2 7.2 %collective-permute-start.17 = (f32[2,10,10,1]{3,2,1,0:T(8,128)S(1)}, f32[2,10,10,1]{3,2,1,0:T(8,128)S(1)}, u32[]{:S(2)}, u32[]{:S(2)}) collective-permute-start(f32[2,10,10,1]{3,2,1,0:T(8,128)S(1)} %get-tuple-element.60), channel_id=1, source_target_pairs={{0,1},{1,2},{2,3},{4,5},{5,6},{6,7},{8,9},{9,10},{10,11},{12,13},{... | collective-permute-start | bytes 2408 | tf_op jit(solution)/shard_map/ppermute | solution.py:20
  135.9 10.8 %collective-permute-start.20 = (f32[2,10,1,64]{3,2,1,0:T(1,128)S(1)}, f32[2,10,1,64]{3,2,1,0:T(1,128)S(1)}, u32[]{:S(2)}, u32[]{:S(2)}) collective-permute-start(f32[2,10,1,64]{3,2,1,0:T(1,128)S(1)} %get-tuple-element.74), channel_id=1, source_target_pairs={{4,0},{8,4},{12,8},{16,12},{20,16},{24,20},{28,24},{5,1},{9,5},{13... | collective-permute-start | bytes 15368 | tf_op jit(solution)/shard_map/ppermute | solution.py:23
  137.8 8.9 %collective-permute-start.21 = (f32[2,10,1,64]{3,2,1,0:T(1,128)S(1)}, f32[2,10,1,64]{3,2,1,0:T(1,128)S(1)}, u32[]{:S(2)}, u32[]{:S(2)}) collective-permute-start(f32[2,10,1,64]{3,2,1,0:T(1,128)S(1)} %get-tuple-element.73), channel_id=1, source_target_pairs={{0,4},{4,8},{8,12},{12,16},{16,20},{20,24},{24,28},{1,5},{5,9},{9,... | collective-permute-start | bytes 15368 | tf_op jit(solution)/shard_map/ppermute | solution.py:20
  149.2 7.2 %collective-permute-start.23 = (f32[2,10,10,1]{3,2,1,0:T(8,128)S(1)}, f32[2,10,10,1]{3,2,1,0:T(8,128)S(1)}, u32[]{:S(2)}, u32[]{:S(2)}) collective-permute-start(f32[2,10,10,1]{3,2,1,0:T(8,128)S(1)} %get-tuple-element.58), channel_id=1, source_target_pairs={{0,1},{1,2},{2,3},{4,5},{5,6},{6,7},{8,9},{9,10},{10,11},{12,13},{... | collective-permute-start | bytes 2408 | tf_op jit(solution)/shard_map/ppermute | solution.py:20
  171.7 7.1 %collective-permute-start.26 = (f32[2,6,1,32]{3,2,1,0:T(1,128)S(1)}, f32[2,6,1,32]{3,2,1,0:T(1,128)S(1)}, u32[]{:S(2)}, u32[]{:S(2)}) collective-permute-start(f32[2,6,1,32]{3,2,1,0:T(1,128)S(1)} %get-tuple-element.117), channel_id=1, source_target_pairs={{4,0},{8,4},{12,8},{16,12},{20,16},{24,20},{28,24},{5,1},{9,5},{13... | collective-permute-start | bytes 4616 | tf_op jit(solution)/shard_map/ppermute | solution.py:23
  196.4 7.7 %collective-permute-start.32 = (f32[2,6,1,32]{3,2,1,0:T(1,128)S(1)}, f32[2,6,1,32]{3,2,1,0:T(1,128)S(1)}, u32[]{:S(2)}, u32[]{:S(2)}) collective-permute-start(f32[2,6,1,32]{3,2,1,0:T(1,128)S(1)} %get-tuple-element.113), channel_id=1, source_target_pairs={{4,0},{8,4},{12,8},{16,12},{20,16},{24,20},{28,24},{5,1},{9,5},{13... | collective-permute-start | bytes 4616 | tf_op jit(solution)/shard_map/ppermute | solution.py:23
  198.4 6.7 %collective-permute-start.33 = (f32[2,6,1,32]{3,2,1,0:T(1,128)S(1)}, f32[2,6,1,32]{3,2,1,0:T(1,128)S(1)}, u32[]{:S(2)}, u32[]{:S(2)}) collective-permute-start(f32[2,6,1,32]{3,2,1,0:T(1,128)S(1)} %get-tuple-element.112), channel_id=1, source_target_pairs={{0,4},{4,8},{8,12},{12,16},{16,20},{20,24},{24,28},{1,5},{5,9},{9,... | collective-permute-start | bytes 4616 | tf_op jit(solution)/shard_map/ppermute | solution.py:20
  221.7 7.4 %collective-permute-start.38 = (f32[2,4,1,16]{3,2,1,0:T(1,128)S(1)}, f32[2,4,1,16]{3,2,1,0:T(1,128)S(1)}, u32[]{:S(2)}, u32[]{:S(2)}) collective-permute-start(f32[2,4,1,16]{3,2,1,0:T(1,128)S(1)} %get-tuple-element.161), channel_id=1, source_target_pairs={{4,0},{8,4},{12,8},{16,12},{20,16},{24,20},{28,24},{5,1},{9,5},{13... | collective-permute-start | bytes 1544 | tf_op jit(solution)/shard_map/ppermute | solution.py:23
  223.7 6.7 %collective-permute-start.39 = (f32[2,4,1,16]{3,2,1,0:T(1,128)S(1)}, f32[2,4,1,16]{3,2,1,0:T(1,128)S(1)}, u32[]{:S(2)}, u32[]{:S(2)}) collective-permute-start(f32[2,4,1,16]{3,2,1,0:T(1,128)S(1)} %get-tuple-element.160), channel_id=1, source_target_pairs={{0,4},{4,8},{8,12},{12,16},{16,20},{20,24},{24,28},{1,5},{5,9},{9,... | collective-permute-start | bytes 1544 | tf_op jit(solution)/shard_map/ppermute | solution.py:20
  246.3 7.5 %collective-permute-start.44 = (f32[2,4,1,16]{3,2,1,0:T(1,128)S(1)}, f32[2,4,1,16]{3,2,1,0:T(1,128)S(1)}, u32[]{:S(2)}, u32[]{:S(2)}) collective-permute-start(f32[2,4,1,16]{3,2,1,0:T(1,128)S(1)} %get-tuple-element.159), channel_id=1, source_target_pairs={{4,0},{8,4},{12,8},{16,12},{20,16},{24,20},{28,24},{5,1},{9,5},{13... | collective-permute-start | bytes 1544 | tf_op jit(solution)/shard_map/ppermute | solution.py:23
  248.2 6.7 %collective-permute-start.45 = (f32[2,4,1,16]{3,2,1,0:T(1,128)S(1)}, f32[2,4,1,16]{3,2,1,0:T(1,128)S(1)}, u32[]{:S(2)}, u32[]{:S(2)}) collective-permute-start(f32[2,4,1,16]{3,2,1,0:T(1,128)S(1)} %get-tuple-element.158), channel_id=1, source_target_pairs={{0,4},{4,8},{8,12},{12,16},{16,20},{20,24},{24,28},{1,5},{5,9},{9,... | collective-permute-start | bytes 1544 | tf_op jit(solution)/shard_map/ppermute | solution.py:20
  270.9 7.3 %collective-permute-start.50 = (f32[2,3,1,8]{3,2,1,0:T(1,128)S(1)}, f32[2,3,1,8]{3,2,1,0:T(1,128)S(1)}, u32[]{:S(2)}, u32[]{:S(2)}) collective-permute-start(f32[2,3,1,8]{3,2,1,0:T(1,128)S(1)} %pad_maximum_fusion.356), channel_id=1, source_target_pairs={{4,0},{8,4},{12,8},{16,12},{20,16},{24,20},{28,24},{5,1},{9,5},{13... | collective-permute-start | bytes 584 | tf_op jit(solution)/shard_map/ppermute | solution.py:23
  272.9 6.7 %collective-permute-start.51 = (f32[2,3,1,8]{3,2,1,0:T(1,128)S(1)}, f32[2,3,1,8]{3,2,1,0:T(1,128)S(1)}, u32[]{:S(2)}, u32[]{:S(2)}) collective-permute-start(f32[2,3,1,8]{3,2,1,0:T(1,128)S(1)} %pad_maximum_fusion.356), channel_id=1, source_target_pairs={{0,4},{4,8},{8,12},{12,16},{16,20},{20,24},{24,28},{1,5},{5,9},{9,... | collective-permute-start | bytes 584 | tf_op jit(solution)/shard_map/ppermute | solution.py:20
  295.4 7.3 %collective-permute-start.56 = (f32[2,3,1,8]{3,2,1,0:T(1,128)S(1)}, f32[2,3,1,8]{3,2,1,0:T(1,128)S(1)}, u32[]{:S(2)}, u32[]{:S(2)}) collective-permute-start(f32[2,3,1,8]{3,2,1,0:T(1,128)S(1)} %pad_maximum_fusion.357), channel_id=1, source_target_pairs={{4,0},{8,4},{12,8},{16,12},{20,16},{24,20},{28,24},{5,1},{9,5},{13... | collective-permute-start | bytes 584 | tf_op jit(solution)/shard_map/ppermute | solution.py:23
  319.8 7.3 %collective-permute-start.62 = (f32[2,3,1,8]{3,2,1,0:T(1,128)S(1)}, f32[2,3,1,8]{3,2,1,0:T(1,128)S(1)}, u32[]{:S(2)}, u32[]{:S(2)}) collective-permute-start(f32[2,3,1,8]{3,2,1,0:T(1,128)S(1)} %pad_maximum_fusion.358), channel_id=1, source_target_pairs={{4,0},{8,4},{12,8},{16,12},{20,16},{24,20},{28,24},{5,1},{9,5},{13... | collective-permute-start | bytes 584 | tf_op jit(solution)/shard_map/ppermute | solution.py:23
  344.2 7.3 %collective-permute-start.68 = (f32[2,3,1,8]{3,2,1,0:T(1,128)S(1)}, f32[2,3,1,8]{3,2,1,0:T(1,128)S(1)}, u32[]{:S(2)}, u32[]{:S(2)}) collective-permute-start(f32[2,3,1,8]{3,2,1,0:T(1,128)S(1)} %pad_maximum_fusion.359), channel_id=1, source_target_pairs={{4,0},{8,4},{12,8},{16,12},{20,16},{24,20},{28,24},{5,1},{9,5},{13... | collective-permute-start | bytes 584 | tf_op jit(solution)/shard_map/ppermute | solution.py:23
  368.6 7.3 %collective-permute-start.74 = (f32[2,3,1,8]{3,2,1,0:T(1,128)S(1)}, f32[2,3,1,8]{3,2,1,0:T(1,128)S(1)}, u32[]{:S(2)}, u32[]{:S(2)}) collective-permute-start(f32[2,3,1,8]{3,2,1,0:T(1,128)S(1)} %pad_maximum_fusion.360), channel_id=1, source_target_pairs={{4,0},{8,4},{12,8},{16,12},{20,16},{24,20},{28,24},{5,1},{9,5},{13... | collective-permute-start | bytes 584 | tf_op jit(solution)/shard_map/ppermute | solution.py:23
  393.2 7.3 %collective-permute-start.80 = (f32[2,4,1,16]{3,2,1,0:T(1,128)S(1)}, f32[2,4,1,16]{3,2,1,0:T(1,128)S(1)}, u32[]{:S(2)}, u32[]{:S(2)}) collective-permute-start(f32[2,4,1,16]{3,2,1,0:T(1,128)S(1)} %get-tuple-element.157), channel_id=1, source_target_pairs={{4,0},{8,4},{12,8},{16,12},{20,16},{24,20},{28,24},{5,1},{9,5},{13... | collective-permute-start | bytes 1544 | tf_op jit(solution)/shard_map/ppermute | solution.py:23
  395.1 6.7 %collective-permute-start.81 = (f32[2,4,1,16]{3,2,1,0:T(1,128)S(1)}, f32[2,4,1,16]{3,2,1,0:T(1,128)S(1)}, u32[]{:S(2)}, u32[]{:S(2)}) collective-permute-start(f32[2,4,1,16]{3,2,1,0:T(1,128)S(1)} %get-tuple-element.156), channel_id=1, source_target_pairs={{0,4},{4,8},{8,12},{12,16},{16,20},{20,24},{24,28},{1,5},{5,9},{9,... | collective-permute-start | bytes 1544 | tf_op jit(solution)/shard_map/ppermute | solution.py:20
  417.7 7.3 %collective-permute-start.86 = (f32[2,4,1,16]{3,2,1,0:T(1,128)S(1)}, f32[2,4,1,16]{3,2,1,0:T(1,128)S(1)}, u32[]{:S(2)}, u32[]{:S(2)}) collective-permute-start(f32[2,4,1,16]{3,2,1,0:T(1,128)S(1)} %get-tuple-element.155), channel_id=1, source_target_pairs={{4,0},{8,4},{12,8},{16,12},{20,16},{24,20},{28,24},{5,1},{9,5},{13... | collective-permute-start | bytes 1544 | tf_op jit(solution)/shard_map/ppermute | solution.py:23
  419.7 6.7 %collective-permute-start.87 = (f32[2,4,1,16]{3,2,1,0:T(1,128)S(1)}, f32[2,4,1,16]{3,2,1,0:T(1,128)S(1)}, u32[]{:S(2)}, u32[]{:S(2)}) collective-permute-start(f32[2,4,1,16]{3,2,1,0:T(1,128)S(1)} %get-tuple-element.154), channel_id=1, source_target_pairs={{0,4},{4,8},{8,12},{12,16},{16,20},{20,24},{24,28},{1,5},{5,9},{9,... | collective-permute-start | bytes 1544 | tf_op jit(solution)/shard_map/ppermute | solution.py:20
  442.6 7.3 %collective-permute-start.92 = (f32[2,6,1,32]{3,2,1,0:T(1,128)S(1)}, f32[2,6,1,32]{3,2,1,0:T(1,128)S(1)}, u32[]{:S(2)}, u32[]{:S(2)}) collective-permute-start(f32[2,6,1,32]{3,2,1,0:T(1,128)S(1)} %get-tuple-element.111), channel_id=1, source_target_pairs={{4,0},{8,4},{12,8},{16,12},{20,16},{24,20},{28,24},{5,1},{9,5},{13... | collective-permute-start | bytes 4616 | tf_op jit(solution)/shard_map/ppermute | solution.py:23
  444.5 6.7 %collective-permute-start.93 = (f32[2,6,1,32]{3,2,1,0:T(1,128)S(1)}, f32[2,6,1,32]{3,2,1,0:T(1,128)S(1)}, u32[]{:S(2)}, u32[]{:S(2)}) collective-permute-start(f32[2,6,1,32]{3,2,1,0:T(1,128)S(1)} %get-tuple-element.110), channel_id=1, source_target_pairs={{0,4},{4,8},{8,12},{12,16},{16,20},{20,24},{24,28},{1,5},{5,9},{9,... | collective-permute-start | bytes 4616 | tf_op jit(solution)/shard_map/ppermute | solution.py:20
  467.6 7.3 %collective-permute-start.98 = (f32[2,6,1,32]{3,2,1,0:T(1,128)S(1)}, f32[2,6,1,32]{3,2,1,0:T(1,128)S(1)}, u32[]{:S(2)}, u32[]{:S(2)}) collective-permute-start(f32[2,6,1,32]{3,2,1,0:T(1,128)S(1)} %get-tuple-element.107), channel_id=1, source_target_pairs={{4,0},{8,4},{12,8},{16,12},{20,16},{24,20},{28,24},{5,1},{9,5},{13... | collective-permute-start | bytes 4616 | tf_op jit(solution)/shard_map/ppermute | solution.py:23
  469.5 6.7 %collective-permute-start.99 = (f32[2,6,1,32]{3,2,1,0:T(1,128)S(1)}, f32[2,6,1,32]{3,2,1,0:T(1,128)S(1)}, u32[]{:S(2)}, u32[]{:S(2)}) collective-permute-start(f32[2,6,1,32]{3,2,1,0:T(1,128)S(1)} %get-tuple-element.106), channel_id=1, source_target_pairs={{0,4},{4,8},{8,12},{12,16},{16,20},{20,24},{24,28},{1,5},{5,9},{9,... | collective-permute-start | bytes 4616 | tf_op jit(solution)/shard_map/ppermute | solution.py:20
  494.7 7.3 %collective-permute-start.104 = (f32[2,10,1,64]{3,2,1,0:T(1,128)S(1)}, f32[2,10,1,64]{3,2,1,0:T(1,128)S(1)}, u32[]{:S(2)}, u32[]{:S(2)}) collective-permute-start(f32[2,10,1,64]{3,2,1,0:T(1,128)S(1)} %get-tuple-element.72), channel_id=1, source_target_pairs={{4,0},{8,4},{12,8},{16,12},{20,16},{24,20},{28,24},{5,1},{9,5},{13... | collective-permute-start | bytes 15368 | tf_op jit(solution)/shard_map/ppermute | solution.py:23
  496.6 6.8 %collective-permute-start.105 = (f32[2,10,1,64]{3,2,1,0:T(1,128)S(1)}, f32[2,10,1,64]{3,2,1,0:T(1,128)S(1)}, u32[]{:S(2)}, u32[]{:S(2)}) collective-permute-start(f32[2,10,1,64]{3,2,1,0:T(1,128)S(1)} %get-tuple-element.71), channel_id=1, source_target_pairs={{0,4},{4,8},{8,12},{12,16},{16,20},{20,24},{24,28},{1,5},{5,9},{9,... | collective-permute-start | bytes 15368 | tf_op jit(solution)/shard_map/ppermute | solution.py:20
  505.5 7.2 %collective-permute-start.107 = (f32[2,10,10,1]{3,2,1,0:T(8,128)S(1)}, f32[2,10,10,1]{3,2,1,0:T(8,128)S(1)}, u32[]{:S(2)}, u32[]{:S(2)}) collective-permute-start(f32[2,10,10,1]{3,2,1,0:T(8,128)S(1)} %get-tuple-element.56), channel_id=1, source_target_pairs={{0,1},{1,2},{2,3},{4,5},{5,6},{6,7},{8,9},{9,10},{10,11},{12,13},{... | collective-permute-start | bytes 2408 | tf_op jit(solution)/shard_map/ppermute | solution.py:20
  521.1 7.3 %collective-permute-start.110 = (f32[2,10,1,64]{3,2,1,0:T(1,128)S(1)}, f32[2,10,1,64]{3,2,1,0:T(1,128)S(1)}, u32[]{:S(2)}, u32[]{:S(2)}) collective-permute-start(f32[2,10,1,64]{3,2,1,0:T(1,128)S(1)} %get-tuple-element.70), channel_id=1, source_target_pairs={{4,0},{8,4},{12,8},{16,12},{20,16},{24,20},{28,24},{5,1},{9,5},{13... | collective-permute-start | bytes 15368 | tf_op jit(solution)/shard_map/ppermute | solution.py:23
  523.1 6.8 %collective-permute-start.111 = (f32[2,10,1,64]{3,2,1,0:T(1,128)S(1)}, f32[2,10,1,64]{3,2,1,0:T(1,128)S(1)}, u32[]{:S(2)}, u32[]{:S(2)}) collective-permute-start(f32[2,10,1,64]{3,2,1,0:T(1,128)S(1)} %get-tuple-element.69), channel_id=1, source_target_pairs={{0,4},{4,8},{8,12},{12,16},{16,20},{20,24},{24,28},{1,5},{5,9},{9,... | collective-permute-start | bytes 15368 | tf_op jit(solution)/shard_map/ppermute | solution.py:20
  531.9 7.2 %collective-permute-start.113 = (f32[2,10,10,1]{3,2,1,0:T(8,128)S(1)}, f32[2,10,10,1]{3,2,1,0:T(8,128)S(1)}, u32[]{:S(2)}, u32[]{:S(2)}) collective-permute-start(f32[2,10,10,1]{3,2,1,0:T(8,128)S(1)} %get-tuple-element.54), channel_id=1, source_target_pairs={{0,1},{1,2},{2,3},{4,5},{5,6},{6,7},{8,9},{9,10},{10,11},{12,13},{... | collective-permute-start | bytes 2408 | tf_op jit(solution)/shard_map/ppermute | solution.py:20
  566.9 7.3 %collective-permute-start.116 = (f32[2,18,1,128]{3,2,1,0:T(1,128)S(1)}, f32[2,18,1,128]{3,2,1,0:T(1,128)S(1)}, u32[]{:S(2)}, u32[]{:S(2)}) collective-permute-start(f32[2,18,1,128]{3,2,1,0:T(1,128)S(1)} %get-tuple-element.32), channel_id=1, source_target_pairs={{4,0},{8,4},{12,8},{16,12},{20,16},{24,20},{28,24},{5,1},{9,5},{13... | collective-permute-start | bytes 55304 | tf_op jit(solution)/shard_map/ppermute | solution.py:23
  568.9 6.9 %collective-permute-start.117 = (f32[2,18,1,128]{3,2,1,0:T(1,128)S(1)}, f32[2,18,1,128]{3,2,1,0:T(1,128)S(1)}, u32[]{:S(2)}, u32[]{:S(2)}) collective-permute-start(f32[2,18,1,128]{3,2,1,0:T(1,128)S(1)} %get-tuple-element.31), channel_id=1, source_target_pairs={{0,4},{4,8},{8,12},{12,16},{16,20},{20,24},{24,28},{1,5},{5,9},{9,... | collective-permute-start | bytes 55304 | tf_op jit(solution)/shard_map/ppermute | solution.py:20
  576.0 7.9 %collective-permute-start.118 = (f32[2,18,18,1]{3,2,1,0:T(8,128)S(1)}, f32[2,18,18,1]{3,2,1,0:T(8,128)S(1)}, u32[]{:S(2)}, u32[]{:S(2)}) collective-permute-start(f32[2,18,18,1]{3,2,1,0:T(8,128)S(1)} %get-tuple-element.15), channel_id=1, source_target_pairs={{1,0},{2,1},{3,2},{5,4},{6,5},{7,6},{9,8},{10,9},{11,10},{13,12},{... | collective-permute-start | bytes 7784 | tf_op jit(solution)/shard_map/ppermute | solution.py:23
  577.9 10.2 %collective-permute-start.119 = (f32[2,18,18,1]{3,2,1,0:T(8,128)S(1)}, f32[2,18,18,1]{3,2,1,0:T(8,128)S(1)}, u32[]{:S(2)}, u32[]{:S(2)}) collective-permute-start(f32[2,18,18,1]{3,2,1,0:T(8,128)S(1)} %get-tuple-element.16), channel_id=1, source_target_pairs={{0,1},{1,2},{2,3},{4,5},{5,6},{6,7},{8,9},{9,10},{10,11},{12,13},{... | collective-permute-start | bytes 7784 | tf_op jit(solution)/shard_map/ppermute | solution.py:20
  597.0 7.4 %collective-permute-start.122 = (f32[2,18,1,128]{3,2,1,0:T(1,128)S(1)}, f32[2,18,1,128]{3,2,1,0:T(1,128)S(1)}, u32[]{:S(2)}, u32[]{:S(2)}) collective-permute-start(f32[2,18,1,128]{3,2,1,0:T(1,128)S(1)} %get-tuple-element.30), channel_id=1, source_target_pairs={{4,0},{8,4},{12,8},{16,12},{20,16},{24,20},{28,24},{5,1},{9,5},{13... | collective-permute-start | bytes 55304 | tf_op jit(solution)/shard_map/ppermute | solution.py:23
  598.9 6.9 %collective-permute-start.123 = (f32[2,18,1,128]{3,2,1,0:T(1,128)S(1)}, f32[2,18,1,128]{3,2,1,0:T(1,128)S(1)}, u32[]{:S(2)}, u32[]{:S(2)}) collective-permute-start(f32[2,18,1,128]{3,2,1,0:T(1,128)S(1)} %get-tuple-element.29), channel_id=1, source_target_pairs={{0,4},{4,8},{8,12},{12,16},{16,20},{20,24},{24,28},{1,5},{5,9},{9,... | collective-permute-start | bytes 55304 | tf_op jit(solution)/shard_map/ppermute | solution.py:20
  606.0 7.9 %collective-permute-start.124 = (f32[2,18,18,1]{3,2,1,0:T(8,128)S(1)}, f32[2,18,18,1]{3,2,1,0:T(8,128)S(1)}, u32[]{:S(2)}, u32[]{:S(2)}) collective-permute-start(f32[2,18,18,1]{3,2,1,0:T(8,128)S(1)} %get-tuple-element.13), channel_id=1, source_target_pairs={{1,0},{2,1},{3,2},{5,4},{6,5},{7,6},{9,8},{10,9},{11,10},{13,12},{... | collective-permute-start | bytes 7784 | tf_op jit(solution)/shard_map/ppermute | solution.py:23
  608.0 10.2 %collective-permute-start.125 = (f32[2,18,18,1]{3,2,1,0:T(8,128)S(1)}, f32[2,18,18,1]{3,2,1,0:T(8,128)S(1)}, u32[]{:S(2)}, u32[]{:S(2)}) collective-permute-start(f32[2,18,18,1]{3,2,1,0:T(8,128)S(1)} %get-tuple-element.14), channel_id=1, source_target_pairs={{0,1},{1,2},{2,3},{4,5},{5,6},{6,7},{8,9},{9,10},{10,11},{12,13},{... | collective-permute-start | bytes 7784 | tf_op jit(solution)/shard_map/ppermute | solution.py:20
  (102 other events, 1214.4 us)
where the time goes:
time: 623 us; the launch traced here: 619 us
  starting transfers between devices  314 us (50%)
  waiting for transfers between devices  220 us (35%)
  local copies, waits for them, and re-layouts  60.1 us (10%)
  other arithmetic  22.3 us (4%)
    ppermute x63, waiting for transfers between devices, extended(): lax.ppermute(lax.slice_in_dim(block, block.shape[dim] - width, None, axis...  192 us
    ppermute x63, starting transfers between devices, extended(): lax.ppermute(lax.slice_in_dim(block, block.shape[dim] - width, None, axis...  191 us
    ppermute x63, starting transfers between devices, extended(): lax.ppermute(lax.slice_in_dim(block, 0, width, axis=dim), axis, backward)  123 us
    ppermute x63, waiting for transfers between devices, extended(): lax.ppermute(lax.slice_in_dim(block, 0, width, axis=dim), axis, backward)  28.4 us
    reshape x2, local copies, waits for them, and re-layouts, restrict(): values.reshape(leading + (first_length // 2, 2, second_length // 2, 2, th...  27.7 us
    reshape x3, local copies, waits for them, and re-layouts, prolong(): expanded.reshape(leading + (2 * first_length, 2 * second_length, 2 * thir...  14.5 us
    reduce_sum x10, other arithmetic, restrict(): grouped.mean(axis=(leading_rank + 1, leading_rank + 3, leading_rank + 5))  13.2 us
  transfers between devices with their start and end apart: 126, of which 82 were waited for; matrix products, arithmetic and copies ran while one was open for 3% of the time, Pallas kernels for 0%

commit v1 on v0

v1 whole, which is shorter than its diff:
```python
import functools

import jax
import jax.numpy as jnp
from jax import lax
from jax.experimental import pallas as pl
from jax.experimental.pallas import tpu as pltpu
from jax.sharding import PartitionSpec as P

F32, BF16 = jnp.float32, jnp.bfloat16
WAVE = 0.0625
DIAG_I = 0.5 * WAVE

X0, Y0, L0 = 22, 24, 256
X1, Y1, L1 = 16, 16, 128
X2, Y2 = 12, 32
X3, Y3, PAD3 = 32, 16, 4
X4, Y4 = 16, 8


def iota(shape, dim):
    return lax.broadcasted_iota(jnp.int32, shape, dim)


def split(x):
    high = x.astype(BF16)
    rest = x - high.astype(F32)
    middle = rest.astype(BF16)
    return high, middle, (rest - middle.astype(F32)).astype(BF16)


def select(x, matrix, dims=(((1,), (0,)), ((), ()))):
    parts = [lax.dot_general(p, matrix, dims, preferred_element_type=F32) for p in split(x)]
    return parts[0] + (parts[1] + parts[2])


def coefficients(mach, level):
    scale = 0.25**level
    axial = scale * (1.0 - mach * mach)
    advect = (0.25 * 0.5**level) * mach
    diagonal = 2.0 * axial + (4.0 * scale - WAVE)
    return axial, advect, diagonal


def half_inverse(mach, level):
    diagonal = coefficients(mach, level)[2]
    scale = 0.5 / (diagonal * diagonal + DIAG_I * DIAG_I)
    inside = mach > 0.0
    return jnp.where(inside, diagonal * scale, 0.0), jnp.where(inside, -DIAG_I * scale, 0.0)


def transverse(c, ymask, zmask):
    rows, lanes = c.shape
    north, south = pltpu.roll(c, rows - 1, 0), pltpu.roll(c, 1, 0)
    upper, lower = pltpu.roll(c, lanes - 1, 1), pltpu.roll(c, 1, 1)
    if ymask:
        at = iota(c.shape, 0)
        north = jnp.where(at == rows - 1, 0.0, north)
        south = jnp.where(at == 0, 0.0, south)
    if zmask:
        at = iota(c.shape, 1)
        upper = jnp.where(at == lanes - 1, 0.0, upper)
        lower = jnp.where(at == 0, 0.0, lower)
    return (north + south) + (upper + lower)


def balance(g_r, g_i, mach, v, i, level, ymask, zmask):
    axial, advect, diagonal = coefficients(mach, level)
    scale = 0.25**level
    c_r, c_i = v[0, i], v[1, i]
    e_r, w_r, e_i, w_i = v[0, i + 1], v[0, i - 1], v[1, i + 1], v[1, i - 1]
    t_r = g_r + axial * (e_r + w_r) - advect * (e_i - w_i)
    t_i = g_i + axial * (e_i + w_i) + advect * (e_r - w_r)
    return (
        t_r + scale * transverse(c_r, ymask, zmask),
        t_i + scale * transverse(c_i, ymask, zmask),
        c_r,
        c_i,
        diagonal,
    )


def first_loop(lo, hi, g, hd, v, level):
    def body(i, _):
        h_r, h_i = half_inverse(g[2, i], level)
        hd[0, i], hd[1, i] = h_r, h_i
        g_r, g_i = g[0, i], g[1, i]
        v[0, i] = h_r * g_r - h_i * g_i
        v[1, i] = h_r * g_i + h_i * g_r
        return 0

    lax.fori_loop(lo, hi, body, 0)


def relax_loop(lo, count, g, hd, v, write, level, ymask=False, zmask=False):
    def body(j, _):
        i = lo + j
        t_r, t_i, c_r, c_i, _d = balance(g[0, i], g[1, i], g[2, i], v, i, level, ymask, zmask)
        h_r, h_i = hd[0, i], hd[1, i]
        write(j, i, 0.5 * c_r + (h_r * t_r - h_i * t_i), 0.5 * c_i + (h_r * t_i + h_i * t_r))
        return 0

    lax.fori_loop(0, count, body, 0)


def writer(out):
    def write(j, i, re, im):
        out[0, i], out[1, i] = re, im

    return write


def residual(g, v, i, level, ymask=False, zmask=False):
    t_r, t_i, c_r, c_i, d = balance(g[0, i], g[1, i], g[2, i], v, i, level, ymask, zmask)
    return t_r - (d * c_r - DIAG_I * c_i), t_i - (d * c_i + DIAG_I * c_r)


def residual_pair(g, v, i, level, ymask=False, zmask=False):
    a = residual(g, v, i, level, ymask, zmask)
    b = residual(g, v, i + 1, level, ymask, zmask)
    return a[0] + b[0], a[1] + b[1], g[2, i] + g[2, i + 1]


def pair_rows(ref, rows):
    return ref[pl.ds(0, rows // 2, stride=2), :] + ref[pl.ds(1, rows // 2, stride=2), :]


def twin_rows(ref, value):
    rows = value.shape[0]
    ref[pl.ds(0, rows, stride=2), :] = value
    ref[pl.ds(1, rows, stride=2), :] = value


def matrix(rows, lanes, rule, value=1.0):
    shape = (rows, lanes)
    return jnp.where(rule(iota(shape, 0), iota(shape, 1)), value, 0.0).astype(BF16)


def gather_kernel(own_lanes, width, own, ylo, yhi, xlo, xhi, f, packed):
    count = own.shape[1]
    rows = own.shape[2]
    hx = xlo.shape[1]
    for c in range(3):
        f[c, 0:hx] = xlo[c]
        f[c, hx : hx + count, 0:4] = ylo[c]
        f[c, hx : hx + count, 4 : 4 + rows] = own[c]
        f[c, hx : hx + count, 4 + rows :] = yhi[c]
        f[c, hx + count :] = xhi[c]
    edge = matrix(
        8,
        128,
        lambda r, l: ((r < 4) & (l == r)) | ((r >= 4) & (l == own_lanes - 8 + r)),
    )
    flat = f[...].reshape(-1, 128)
    total = None
    for part in split(flat):
        term = lax.dot_general(edge, part, (((1,), (1,)), ((), ())), preferred_element_type=F32)
        total = term if total is None else total + term
    packed[...] = total


def unpack_lanes(lower, upper, lower_start, upper_start):
    both = jnp.concatenate([upper[...], lower[...]], axis=0)
    place = matrix(
        16,
        128,
        lambda r, l: ((r < 4) & (l == upper_start + r)) | ((r >= 12) & (l == lower_start + r - 12)),
    )
    return select(both, place, (((0,), (0,)), ((), ())))


def down0_kernel(f, lower, upper, g, hd, v2, coarse, v1, sums):
    tail = unpack_lanes(lower, upper, 124, 0).reshape(3, X0, Y0, 128)
    g[:, :, :, 0:128] = f[...]
    g[:, :, :, 128:256] = tail
    first_loop(0, X0, g, hd, v1, 0)
    relax_loop(1, X0 - 2, g, hd, v1, writer(v2), 0)

    def body(k, _):
        parts = residual_pair(g, v2, 3 + 2 * k, 0)
        for c in range(3):
            row = pl.multiple_of((c * 8 + k) * 16, 16)
            sums[pl.ds(row, 16), :] = parts[c][4:20, 0:128]
        return 0

    lax.fori_loop(0, 8, body, 0)
    halve = matrix(128, 128, lambda r, l: r // 2 == l, 0.125)
    coarse[...] = select(pair_rows(sums, 384), halve).reshape(3, 8, 8, 128)


def down1_kernel(f, lower, upper, g, hd, v2, chunk, v1, sums, g2, hd2, va, vb):
    tail = unpack_lanes(lower, upper, 124, 64).reshape(3, X1, Y1, 128)
    g[...] = f[...] + tail
    first_loop(0, X1, g, hd, v1, 1)
    relax_loop(1, X1 - 2, g, hd, v1, writer(v2), 1)

    def body(k, _):
        parts = residual_pair(g, v2, 2 + 2 * k, 1)
        for c in range(3):
            row = pl.multiple_of((c * 6 + k) * 16, 16)
            sums[pl.ds(row, 16), :] = parts[c]
        return 0

    lax.fori_loop(0, 6, body, 0)
    halve = matrix(
        128,
        128,
        lambda r, l: ((r < 66) & (r // 2 == l)) | ((r >= 124) & (r // 2 + 64 == l)),
        0.125,
    )
    g2[...] = select(pair_rows(sums, 288), halve).reshape(3, 6, 8, 128)
    first_loop(0, 6, g2, hd2, va, 2)
    relax_loop(1, 4, g2, hd2, va, writer(vb), 2)
    lane = iota((8, 128), 1) // 32
    chunk[...] = jnp.zeros_like(chunk)
    for c in range(5):
        source = (lambda x: g2[c, x]) if c < 3 else (lambda x: vb[c - 3, x])
        total = source(1)
        for x in range(1, 4):
            total = jnp.where(lane == x, pltpu.roll(source(1 + x), 32 * x, 1), total)
        chunk[4 * c : 4 * c + 4, :] = total[2:6, :]


def down2_kernel(own, left, right, a, chunk, planes, sums):
    lane = iota((Y2, 128), 1) // 32
    for p, piece in enumerate((left, own, right)):

        def body(c, _):
            for gz in range(4):
                for gy in range(8):
                    planes[gz, 4 * gy : 4 * gy + 4, :] = piece[gy * 4 + gz, pl.ds(4 * c, 4), :]
            for x in range(4):
                total = None
                for gz in range(4):
                    value = planes[gz]
                    if gz != x:
                        value = pltpu.roll(value, (32 * (gz - x)) % 128, 1)
                    total = value if total is None else jnp.where(lane == gz, value, total)
                a[c, 4 * p + x] = total
            return 0

        lax.fori_loop(0, 5, body, 0)
    v = a.at[3:5]
    for k in range(2):
        parts = residual_pair(a, v, 4 + 2 * k, 2, True, True)
        for c in range(3):
            sums[k, Y2 * c : Y2 * (c + 1), :] = parts[c]
    total = None
    for k in range(2):
        halve = matrix(128, 128, lambda r, l: r // 2 + 64 * k == l, 0.125)
        term = select(pair_rows(sums.at[k], 3 * Y2), halve)
        total = term if total is None else total + term
    chunk[...] = total


def up_kernel(
    index, parts3, a, g1, hd1, v21, g0, hd0, v20, out,
    g3, hd3, va3, vb3, s3, g4, hd4, va4, vb4, t4, w3, t3, hd2, va2, vb2, w2, t2, va1, vb1, t1, va0, vb0,
):
    gx, gy, gz = index[0], index[1], index[2]
    zero3 = jnp.zeros((Y3, 128), F32)
    for ref in (g3, hd3, va3, vb3):
        for c in range(ref.shape[0]):
            for i in range(PAD3):
                ref[c, i] = zero3
                ref[c, PAD3 + X3 + i] = zero3
    low = iota((Y3, 128), 1) < 64

    def spread(s, _):
        for c in range(3):
            value = parts3[s, Y3 * c : Y3 * (c + 1), :]
            g3[c, PAD3 + 2 * s] = jnp.where(low, value, 0.0)
            g3[c, PAD3 + 2 * s + 1] = jnp.where(low, pltpu.roll(value, 64, 1), 0.0)
        return 0

    lax.fori_loop(0, 16, spread, 0)
    first_loop(PAD3, PAD3 + X3, g3, hd3, va3, 3)
    relax_loop(PAD3, X3, g3, hd3, va3, writer(vb3), 3, True)

    def body3(k, _):
        parts = residual_pair(g3, vb3, PAD3 + 2 * k, 3, True)
        for c in range(3):
            s3[pl.ds(pl.multiple_of((c * X4 + k) * Y3, Y3), Y3), :] = parts[c]
        return 0

    lax.fori_loop(0, X4, body3, 0)
    halve = matrix(128, 128, lambda r, l: (r // 2 == l) & (r < 64), 0.125)
    g4[:, 1 : 1 + X4] = select(pair_rows(s3, 3 * X4 * Y3), halve).reshape(3, X4, Y4, 128)
    for ref in (va4, vb4):
        for c in range(2):
            ref[c, 0] = jnp.zeros((Y4, 128), F32)
            ref[c, X4 + 1] = jnp.zeros((Y4, 128), F32)
    first_loop(1, X4 + 1, g4, hd4, va4, 4)
    src, dst = va4, vb4
    for _ in range(5):
        relax_loop(1, X4, g4, hd4, src, writer(dst), 4, True)
        src, dst = dst, src
    double = matrix(128, 128, lambda r, l: l // 2 == r)
    twin_rows(t4, select(src[:, 1 : 1 + X4].reshape(2 * X4 * Y4, 128), double))

    def add3(k, _):
        for c in range(2):
            value = t4[pl.ds(pl.multiple_of((c * X4 + k) * Y3, Y3), Y3), :]
            vb3[c, PAD3 + 2 * k] = vb3[c, PAD3 + 2 * k] + value
            vb3[c, PAD3 + 2 * k + 1] = vb3[c, PAD3 + 2 * k + 1] + value
        return 0

    lax.fori_loop(0, X4, add3, 0)
    base = PAD3 + 2 * gx
    relax_loop(base - 3, 8, g3, hd3, vb3, writer(va3), 3, True)

    def write3(j, i, re, im):
        w3[0, j], w3[1, j] = re, im

    relax_loop(base - 2, 6, g3, hd3, va3, write3, 3, True)
    twin_rows(t3, select(w3[...].reshape(2 * 6 * Y3, 128), double))

    def start2(i, _):
        hd2[0, i], hd2[1, i] = half_inverse(a[2, i], 2)
        for c in range(2):
            row = pl.multiple_of((c * 6 + i // 2) * Y2, Y2)
            va2[c, i] = a[3 + c, i] + jnp.where(a[2, i] > 0.0, t3[pl.ds(row, Y2), :], 0.0)
        return 0

    lax.fori_loop(0, X2, start2, 0)
    relax_loop(1, X2 - 2, a, hd2, va2, writer(vb2), 2, True, True)
    w2[...] = jnp.zeros_like(w2)

    def write2(j, i, re, im):
        w2[0, j, 8 : 8 + Y2], w2[1, j, 8 : 8 + Y2] = re, im

    relax_loop(2, X2 - 4, a, hd2, vb2, write2, 2, True, True)
    rows = w2[:, :, pl.ds(4 * gy + 6, 8), :].reshape(2 * 8 * 8, 128)

    def place1(r, l):
        at = jnp.where(l < 96, l, l - 128)
        return r == 32 * gz + (at + 128) // 2 - 64

    twin_rows(t2, select(rows, matrix(128, 128, place1)))

    def start1(i, _):
        for c in range(2):
            row = pl.multiple_of((c * 8 + i // 2) * Y1, Y1)
            va1[c, i] = v21[c, i] + t2[pl.ds(row, Y1), :]
        return 0

    lax.fori_loop(1, X1 - 1, start1, 0)
    relax_loop(2, X1 - 4, g1, hd1, va1, writer(vb1), 1)
    relax_loop(3, X1 - 6, g1, hd1, vb1, writer(va1), 1)
    own = va1[:, 3:13].reshape(2 * 10 * Y1, 128)
    for half in range(2):
        place = matrix(128, 128, lambda r, l: r == (l + 128 * half) // 2)
        twin_rows(t1.at[half], select(own, place))

    def start0(k, _):
        for c in range(2):
            row = (c * 10 + k) * 32 + 4
            for half in range(2):
                lanes = slice(128 * half, 128 * half + 128)
                value = t1[half, pl.ds(row, Y0), :]
                for i in range(2):
                    va0[c, 2 * k + 1 + i, :, lanes] = v20[c, 2 * k + 1 + i, :, lanes] + value
        return 0

    lax.fori_loop(0, 10, start0, 0)
    relax_loop(2, X0 - 4, g0, hd0, va0, writer(vb0), 0)

    def write0(j, i, re, im):
        out[0, j], out[1, j] = re[4:20, 0:128], im[4:20, 0:128]

    relax_loop(3, X0 - 6, g0, hd0, vb0, write0, 0)


def vmem(*shape):
    return pltpu.VMEM(shape, F32)


def call(kernel, outs, scratch, *args, smem_first=False):
    spec = pl.BlockSpec(memory_space=pltpu.VMEM)
    specs = [spec] * len(args)
    if smem_first:
        specs[0] = pl.BlockSpec(memory_space=pltpu.SMEM)
    return pl.pallas_call(
        kernel,
        out_shape=[jax.ShapeDtypeStruct(s, F32) for s in outs],
        in_specs=specs,
        out_specs=[spec] * len(outs),
        scratch_shapes=[vmem(*s) for s in scratch],
        compiler_params=pltpu.CompilerParams(vmem_limit_bytes=48 << 20),
    )(*args)


def shift(block, axis, step):
    count = lax.axis_size(axis)
    pairs = [(i, i + step) for i in range(count) if 0 <= i + step < count]
    return lax.ppermute(block, axis, pairs)


def with_halos(own, hx, own_lanes):
    rows = own.shape[2]
    count = own.shape[1]
    ylo = shift(own[:, :, rows - 4 :], "gy", 1)
    yhi = shift(own[:, :, :4], "gy", -1)

    def edge(at):
        return jnp.concatenate([x[:, at : at + hx] for x in (ylo, own, yhi)], axis=2)

    xlo = shift(edge(count - hx), "gx", 1)
    xhi = shift(edge(0), "gx", -1)
    shape = (3, count + 2 * hx, rows + 8, 128)
    flat = shape[0] * shape[1] * shape[2]
    f, packed = call(
        functools.partial(gather_kernel, own_lanes, None), [shape, (8, flat)], [], own, ylo, yhi, xlo, xhi
    )
    return f, shift(packed, "gz", 1), shift(packed, "gz", -1)


def everyone(block, axes):
    count = lax.axis_size(axes)
    return lax.all_to_all(jnp.broadcast_to(block, (count,) + block.shape), axes, 0, 0)


def shards(source_field, mach_number):
    own0 = jnp.concatenate([source_field, mach_number.astype(F32)[None]], axis=0)
    f0, lower0, upper0 = with_halos(own0, 3, 128)
    full0 = (X0, Y0, L0)
    g0, hd0, v20, own1 = call(
        down0_kernel,
        [(3,) + full0, (2,) + full0, (2,) + full0, (3, 8, 8, 128)],
        [(2,) + full0, (384, 128)],
        f0, lower0, upper0,
    )
    f1, lower1, upper1 = with_halos(own1, 4, 64)
    full1 = (X1, Y1, L1)
    g1, hd1, v21, chunk2 = call(
        down1_kernel,
        [(3,) + full1, (2,) + full1, (2,) + full1, (24, 128)],
        [(2,) + full1, (288, 128), (3, 6, 8, 128)] + [(2, 6, 8, 128)] * 3,
        f1, lower1, upper1,
    )
    own2 = everyone(chunk2, ("gy", "gz"))
    left2 = shift(own2, "gx", 1)
    right2 = shift(own2, "gx", -1)
    a, chunk3 = call(
        down2_kernel,
        [(5, X2, Y2, 128), (48, 128)],
        [(4, Y2, 128), (2, 96, 128)],
        own2, left2, right2,
    )
    parts3 = everyone(chunk3, "gx")
    index = jnp.stack([lax.axis_index(n) for n in ("gx", "gy", "gz")]).astype(jnp.int32)
    wide3 = (X3 + 2 * PAD3, Y3, 128)
    wide4 = (X4 + 2, Y4, 128)
    scratch = [(3,) + wide3, (2,) + wide3, (2,) + wide3, (2,) + wide3, (3 * X4 * Y3, 128)]
    scratch += [(3,) + wide4, (2,) + wide4, (2,) + wide4, (2,) + wide4, (2 * X4 * Y3, 128)]
    scratch += [(2, 6, Y3, 128), (2 * 6 * Y2, 128)] + [(2, X2, Y2, 128)] * 3
    scratch += [(2, 8, Y2 + 16, 128), (2 * 8 * Y1, 128), (2,) + full1, (2,) + full1]
    scratch += [(2, 2 * 10 * 32, 128), (2,) + full0, (2,) + full0]
    return call(
        up_kernel,
        [(2, 16, 16, 128)],
        scratch,
        index, parts3, a, g1, hd1, v21, g0, hd0, v20,
        smem_first=True,
    )[0]


def solution(mesh):
    return jax.shard_map(
        shards,
        mesh=mesh,
        in_specs=(P(None, "gx", "gy", "gz"), P("gx", "gy", "gz")),
        out_specs=P(None, "gx", "gy", "gz"),
        check_vma=False,
    )
```

time: 623 us -> 162 us (0.26)
  the two profiles are of different devices: /device:TPU:230 before, /device:TPU:1 now
where the time goes in v1:
time: 162 us; the launch traced here: 161 us
  starting transfers between devices  52.3 us (32%)
  waiting for transfers between devices  41.5 us (26%)
  Pallas kernels  35.1 us (22%)
  blocking collectives  21.1 us (13%)
  local copies, waits for them, and re-layouts  7.78 us (5%)
  other arithmetic  2.93 us (2%)
    ppermute x14, starting transfers between devices, shift(): return lax.ppermute(block, axis, pairs)  43.4 us
    pallas_call x6, Pallas kernels, call(): pl.pallas_call(kernel, out_shape=[jax.ShapeDtypeStruct(s, F32) for s in o...  35.1 us
    ppermute x14, waiting for transfers between devices, shift(): return lax.ppermute(block, axis, pairs)  27 us
    all_to_all x1, blocking collectives, everyone(): lax.all_to_all(jnp.broadcast_to(block, (count,) + block.shape), axes, 0, 0)  21.1 us
    all_to_all x1, waiting for transfers between devices, everyone(): lax.all_to_all(jnp.broadcast_to(block, (count,) + block.shape), axes, 0, 0)  14.5 us
    all_to_all x1, starting transfers between devices, everyone(): lax.all_to_all(jnp.broadcast_to(block, (count,) + block.shape), axes, 0, 0)  8.92 us
    unnamed x18, local copies, waits for them, and re-layouts  6.93 us
  transfers between devices with their start and end apart: 15, of which 10 were waited for; matrix products, arithmetic and copies ran while one was open for 1% of the time, Pallas kernels for 0%

profile of v1, /device:TPU:1, one launch (start us, length us, event | category | flops | bytes accessed | tf_op | source)
XLA Modules:
  0.0 160.9 jit_solution(13360534768801589137)
XLA Ops:
  0.0 0.9 bitcast_convert_fusion
  0.9 1.0 fusion.1
  1.9 4.8 %collective-permute-start = (f32[3,16,4,128]{3,2,1,0:T(4,128)S(1)}, f32[3,16,4,128]{3,2,1,0:T(4,128)S(1)}, u32[]{:S(2)}, u32[]{:S(2)}) collective-permute-start(f32[3,16,4,128]{3,2,1,0:T(4,128)S(1)} %get-tuple-element.36), channel_id=1, source_target_pairs={{0,4},{4,8},{8,12},{12,16},{16,20},{20,24},{24,28},{1,5},{5,9},{9,... | collective-permute-start | bytes 294920 | tf_op jit(solution)/shard_map/ppermute | solution.py:396
  6.8 1.3 collective-permute-start.1
  8.1 0.8 fusion.3
  8.9 0.0 collective-permute-done.ylo
  8.9 3.8 %collective-permute-done.1.yhi = f32[3,16,4,128]{3,2,1,0:T(4,128)S(1)} collective-permute-done((f32[3,16,4,128]{3,2,1,0:T(4,128)S(1)}, f32[3,16,4,128]{3,2,1,0:T(4,128)S(1)}, u32[]{:S(2)}, u32[]{:S(2)}) %collective-permute-start.1) | collective-permute-done | bytes 98336 | tf_op jit(solution)/shard_map/ppermute | solution.py:396
  12.8 5.8 %collective-permute-start.3 = (f32[3,3,24,128]{3,2,1,0:T(8,128)S(1)}, f32[3,3,24,128]{3,2,1,0:T(8,128)S(1)}, u32[]{:S(2)}, u32[]{:S(2)}) collective-permute-start(f32[3,3,24,128]{3,2,1,0:T(8,128)S(1)} %pad_maximum_fusion.2), channel_id=1, source_target_pairs={{32,0},{64,32},{96,64},{128,96},{160,128},{192,160},{224,192},{256... | collective-permute-start | bytes 331784 | tf_op jit(solution)/shard_map/ppermute | solution.py:396
  18.6 1.9 %collective-permute-start.2 = (f32[3,3,24,128]{3,2,1,0:T(8,128)S(1)}, f32[3,3,24,128]{3,2,1,0:T(8,128)S(1)}, u32[]{:S(2)}, u32[]{:S(2)}) collective-permute-start(f32[3,3,24,128]{3,2,1,0:T(8,128)S(1)} %pad_maximum_fusion.1), channel_id=1, source_target_pairs={{0,32},{32,64},{64,96},{96,128},{128,160},{160,192},{192,224},{224... | collective-permute-start | bytes 331784 | tf_op jit(solution)/shard_map/ppermute | solution.py:396
  20.6 0.0 collective-permute-done.3.xhi
  20.6 1.7 %collective-permute-done.2.xlo = f32[3,3,24,128]{3,2,1,0:T(8,128)S(1)} collective-permute-done((f32[3,3,24,128]{3,2,1,0:T(8,128)S(1)}, f32[3,3,24,128]{3,2,1,0:T(8,128)S(1)}, u32[]{:S(2)}, u32[]{:S(2)}) %collective-permute-start.2) | collective-permute-done | bytes 110624 | tf_op jit(solution)/shard_map/ppermute | solution.py:396
  22.2 0.5 shard_map.28
  22.8 2.3 %collective-permute-start.4 = (f32[8,1584]{1,0:T(8,128)S(1)}, f32[8,1584]{1,0:T(8,128)S(1)}, u32[]{:S(2)}, u32[]{:S(2)}) collective-permute-start(f32[8,1584]{1,0:T(8,128)S(1)} %get-tuple-element.20), channel_id=1, source_target_pairs={{0,1},{1,2},{2,3},{4,5},{5,6},{6,7},{8,9},{9,10},{10,11},{12,13},{... | collective-permute-start | bytes 152072 | tf_op jit(solution)/shard_map/ppermute | solution.py:396
  25.0 1.3 collective-permute-start.5
  26.3 0.0 collective-permute-done.4.lower
  26.4 3.6 %collective-permute-done.5.upper = f32[8,1584]{1,0:T(8,128)S(1)} collective-permute-done((f32[8,1584]{1,0:T(8,128)S(1)}, f32[8,1584]{1,0:T(8,128)S(1)}, u32[]{:S(2)}, u32[]{:S(2)}) %collective-permute-start.5) | collective-permute-done | bytes 50720 | tf_op jit(solution)/shard_map/ppermute | solution.py:396
  29.9 4.7 %shard_map.29 = (f32[3,22,24,256]{3,2,1,0:T(8,128)S(1)}, f32[2,22,24,256]{3,2,1,0:T(8,128)S(1)}, f32[2,22,24,256]{3,2,1,0:T(8,128)S(1)}, f32[3,8,8,128]{3,2,1,0:T(8,128)S(1)}) custom-call(f32[3,22,24,128]{3,2,1,0:T(8,128)S(1)} %get-tuple-element.19.f, f32[8,1584]{1,0:T(8,128)S(1)} %collective-permute-done.4.lower, f32[8,1584]{1,0:T(8,128)S(1)} %collective-permute-done.5.upper), custom_call_target="tpu_custom_call" | custom-call | tf_op jit(solution)/shard_map/pallas_call | solution.py:383
  34.7 1.0 copy-done
  35.7 4.0 %collective-permute-start.6 = (f32[3,8,4,128]{3,2,1,0:T(4,128)S(1)}, f32[3,8,4,128]{3,2,1,0:T(4,128)S(1)}, u32[]{:S(2)}, u32[]{:S(2)}) collective-permute-start(f32[3,8,4,128]{3,2,1,0:T(4,128)S(1)} %get-tuple-element.40), channel_id=1, source_target_pairs={{0,4},{4,8},{8,12},{12,16},{16,20},{20,24},{24,28},{1,5},{5,9},{9,... | collective-permute-start | bytes 147464 | tf_op jit(solution)/shard_map/ppermute | solution.py:396
  39.7 1.3 collective-permute-start.7
  41.0 5.9 %collective-permute-done.7.yhi = f32[3,8,4,128]{3,2,1,0:T(4,128)S(1)} collective-permute-done((f32[3,8,4,128]{3,2,1,0:T(4,128)S(1)}, f32[3,8,4,128]{3,2,1,0:T(4,128)S(1)}, u32[]{:S(2)}, u32[]{:S(2)}) %collective-permute-start.7) | collective-permute-done | bytes 49184 | tf_op jit(solution)/shard_map/ppermute | solution.py:396
  46.9 2.6 %collective-permute-start.9 = (f32[3,4,16,128]{3,2,1,0:T(8,128)S(1)}, f32[3,4,16,128]{3,2,1,0:T(8,128)S(1)}, u32[]{:S(2)}, u32[]{:S(2)}) collective-permute-start(f32[3,4,16,128]{3,2,1,0:T(8,128)S(1)} %pad_maximum_fusion.4), channel_id=1, source_target_pairs={{32,0},{64,32},{96,64},{128,96},{160,128},{192,160},{224,192},{256... | collective-permute-start | bytes 294920 | tf_op jit(solution)/shard_map/ppermute | solution.py:396
  49.6 5.7 %collective-permute-start.8 = (f32[3,4,16,128]{3,2,1,0:T(8,128)S(1)}, f32[3,4,16,128]{3,2,1,0:T(8,128)S(1)}, u32[]{:S(2)}, u32[]{:S(2)}) collective-permute-start(f32[3,4,16,128]{3,2,1,0:T(8,128)S(1)} %pad_maximum_fusion.3), channel_id=1, source_target_pairs={{0,32},{32,64},{64,96},{96,128},{128,160},{160,192},{192,224},{224... | collective-permute-start | bytes 294920 | tf_op jit(solution)/shard_map/ppermute | solution.py:396
  55.3 0.3 collective-permute-done.9.xhi
  55.6 1.3 collective-permute-done.8.xlo
  56.9 0.3 shard_map.30
  57.2 3.1 %collective-permute-start.10 = (f32[8,768]{1,0:T(8,128)S(1)}, f32[8,768]{1,0:T(8,128)S(1)}, u32[]{:S(2)}, u32[]{:S(2)}) collective-permute-start(f32[8,768]{1,0:T(8,128)S(1)} %get-tuple-element.23), channel_id=1, source_target_pairs={{0,1},{1,2},{2,3},{4,5},{5,6},{6,7},{8,9},{9,10},{10,11},{12,13},{... | collective-permute-start | bytes 73736 | tf_op jit(solution)/shard_map/ppermute | solution.py:396
  60.3 1.3 collective-permute-start.11
  61.6 3.3 %collective-permute-done.11.upper = f32[8,768]{1,0:T(8,128)S(1)} collective-permute-done((f32[8,768]{1,0:T(8,128)S(1)}, f32[8,768]{1,0:T(8,128)S(1)}, u32[]{:S(2)}, u32[]{:S(2)}) %collective-permute-start.11) | collective-permute-done | bytes 24608 | tf_op jit(solution)/shard_map/ppermute | solution.py:396
  64.9 3.2 %shard_map.31 = (f32[3,16,16,128]{3,2,1,0:T(8,128)S(1)}, f32[2,16,16,128]{3,2,1,0:T(8,128)S(1)}, f32[2,16,16,128]{3,2,1,0:T(8,128)S(1)}, f32[24,128]{1,0:T(8,128)S(1)}) custom-call(f32[3,16,16,128]{3,2,1,0:T(8,128)S(1)} %get-tuple-element.22.f, f32[8,768]{1,0:T(8,128)S(1)} %collective-permute-done.10.lower, f32[8,768]{1,0:T(8,128)S(1)} %collective-permute-done.11.upper), custom_call_target="tpu_custom_call" | custom-call | tf_op jit(solution)/shard_map/pallas_call | solution.py:383
  68.1 0.0 copy-start.4
  68.2 0.7 copy-done.4
  68.8 21.1 %all_to_all.10.own = f32[32,24,128]{2,1,0:T(8,128)S(1)} all-to-all(f32[32,24,128]{2,1,0:T(8,128)S(1)} %broadcast_in_dim.14), channel_id=1, replica_groups=mesh['gx'=16,'gy'=8,'gz'=4] {'gy','gz'}, dimensions={0} | all-to-all | bytes 786432 | tf_op jit(solution)/shard_map/all_to_all | solution.py:420
  89.9 6.1 %collective-permute-start.12 = (f32[32,24,128]{2,1,0:T(8,128)S(1)}, f32[32,24,128]{2,1,0:T(8,128)S(1)}, u32[]{:S(2)}, u32[]{:S(2)}) collective-permute-start(f32[32,24,128]{2,1,0:T(8,128)S(1)} %all_to_all.10.own), channel_id=1, source_target_pairs={{0,32},{32,64},{64,96},{96,128},{128,160},{160,192},{192,224},{224... | collective-permute-start | bytes 1179656 | tf_op jit(solution)/shard_map/ppermute | solution.py:396
  96.0 1.9 %collective-permute-start.13 = (f32[32,24,128]{2,1,0:T(8,128)S(1)}, f32[32,24,128]{2,1,0:T(8,128)S(1)}, u32[]{:S(2)}, u32[]{:S(2)}) collective-permute-start(f32[32,24,128]{2,1,0:T(8,128)S(1)} %all_to_all.10.own), channel_id=1, source_target_pairs={{32,0},{64,32},{96,64},{128,96},{160,128},{192,160},{224,192},{256... | collective-permute-start | bytes 1179656 | tf_op jit(solution)/shard_map/ppermute | solution.py:396
  97.9 2.8 %collective-permute-done.12.left = f32[32,24,128]{2,1,0:T(8,128)S(1)} collective-permute-done((f32[32,24,128]{2,1,0:T(8,128)S(1)}, f32[32,24,128]{2,1,0:T(8,128)S(1)}, u32[]{:S(2)}, u32[]{:S(2)}) %collective-permute-start.12) | collective-permute-done | bytes 393248 | tf_op jit(solution)/shard_map/ppermute | solution.py:396
  100.7 4.4 %collective-permute-done.13.right = f32[32,24,128]{2,1,0:T(8,128)S(1)} collective-permute-done((f32[32,24,128]{2,1,0:T(8,128)S(1)}, f32[32,24,128]{2,1,0:T(8,128)S(1)}, u32[]{:S(2)}, u32[]{:S(2)}) %collective-permute-start.13) | collective-permute-done | bytes 393248 | tf_op jit(solution)/shard_map/ppermute | solution.py:396
  105.1 2.3 %shard_map.32 = (f32[5,12,32,128]{3,2,1,0:T(8,128)S(1)}, f32[48,128]{1,0:T(8,128)S(1)}) custom-call(f32[32,24,128]{2,1,0:T(8,128)S(1)} %all_to_all.10.own, f32[32,24,128]{2,1,0:T(8,128)S(1)} %collective-permute-done.12.left, f32[32,24,128]{2,1,0:T(8,128)S(1)} %collective-permute-done.13.right), custom_call_target="tpu_custom_call" | custom-call | tf_op jit(solution)/shard_map/pallas_call | solution.py:383
  107.3 0.9 copy-done.2
  108.3 0.8 broadcast_in_dim.15
  109.1 8.9 %all-to-all-start.1 = ((f32[16,48,128]{2,1,0:T(8,128)}), f32[16,48,128]{2,1,0:T(8,128)S(1)}, u32[]{:S(2)}, u32[]{:S(2)}) async-start(f32[16,48,128]{2,1,0:T(8,128)} %broadcast_in_dim.15), calls=%async_computation.1 | async-start | bytes 786432 | tf_op jit(solution)/shard_map/all_to_all | solution.py:420
  118.0 0.1 pad_add_fusion.index
  118.1 14.5 %all-to-all-done.1.parts3 = f32[16,48,128]{2,1,0:T(8,128)S(1)} async-done(((f32[16,48,128]{2,1,0:T(8,128)}), f32[16,48,128]{2,1,0:T(8,128)S(1)}, u32[]{:S(2)}, u32[]{:S(2)}) %all-to-all-start.1) | async-done | bytes 393248 | tf_op jit(solution)/shard_map/all_to_all | solution.py:420
  132.5 1.2 copy-done.1
  133.8 1.2 copy-done.3
  135.0 0.9 copy-done.5
  135.9 0.9 copy-done.7
  136.9 24.1 %shard_map.33 = f32[2,16,16,128]{3,2,1,0:T(8,128)} custom-call(s32[3]{0:T(128)S(1)} %pad_add_fusion.index, f32[16,48,128]{2,1,0:T(8,128)S(1)} %all-to-all-done.1.parts3, f32[5,12,32,128]{3,2,1,0:T(8,128)S(1)} %copy-done.3, f32[3,16,16,128]{3,2,1,0:T(8,128)S(1)} %get-tuple-element.27.g1, f32[2,16,16,128]{3,2,1,0:T(8,128)S(1)} %copy-done.5, ...), custom_call_target="tpu_custom_call" | custom-call | tf_op jit(solution)/shard_map/pallas_call | solution.py:383
  (24 shorter events, 0.2 us)
Async XLA Ops:
  0.0 20.5 %copy-start.8 = (f32[2,16,16,128]{3,2,1,0:T(8,128)S(1)}, f32[2,16,16,128]{3,2,1,0:T(8,128)}, u32[]{:S(2)}) copy-start(f32[2,16,16,128]{3,2,1,0:T(8,128)} %param.2) | copy-start | bytes 786436
  1.9 7.0 %collective-permute-start = (f32[3,16,4,128]{3,2,1,0:T(4,128)S(1)}, f32[3,16,4,128]{3,2,1,0:T(4,128)S(1)}, u32[]{:S(2)}, u32[]{:S(2)}) collective-permute-start(f32[3,16,4,128]{3,2,1,0:T(4,128)S(1)} %get-tuple-element.36), channel_id=1, source_target_pairs={{0,4},{4,8},{8,12},{12,16},{16,20},{20,24},{24,28},{1,5},{5,9},{9,... | collective-permute-start | bytes 294920 | tf_op jit(solution)/shard_map/ppermute | solution.py:396
  6.8 6.0 %collective-permute-start.1 = (f32[3,16,4,128]{3,2,1,0:T(4,128)S(1)}, f32[3,16,4,128]{3,2,1,0:T(4,128)S(1)}, u32[]{:S(2)}, u32[]{:S(2)}) collective-permute-start(f32[3,16,4,128]{3,2,1,0:T(4,128)S(1)} %get-tuple-element.35), channel_id=1, source_target_pairs={{4,0},{8,4},{12,8},{16,12},{20,16},{24,20},{28,24},{5,1},{9,5},{13... | collective-permute-start | bytes 294920 | tf_op jit(solution)/shard_map/ppermute | solution.py:396
  12.8 7.8 %collective-permute-start.3 = (f32[3,3,24,128]{3,2,1,0:T(8,128)S(1)}, f32[3,3,24,128]{3,2,1,0:T(8,128)S(1)}, u32[]{:S(2)}, u32[]{:S(2)}) collective-permute-start(f32[3,3,24,128]{3,2,1,0:T(8,128)S(1)} %pad_maximum_fusion.2), channel_id=1, source_target_pairs={{32,0},{64,32},{96,64},{128,96},{160,128},{192,160},{224,192},{256... | collective-permute-start | bytes 331784 | tf_op jit(solution)/shard_map/ppermute | solution.py:396
  18.6 3.7 %collective-permute-start.2 = (f32[3,3,24,128]{3,2,1,0:T(8,128)S(1)}, f32[3,3,24,128]{3,2,1,0:T(8,128)S(1)}, u32[]{:S(2)}, u32[]{:S(2)}) collective-permute-start(f32[3,3,24,128]{3,2,1,0:T(8,128)S(1)} %pad_maximum_fusion.1), channel_id=1, source_target_pairs={{0,32},{32,64},{64,96},{96,128},{128,160},{160,192},{192,224},{224... | collective-permute-start | bytes 331784 | tf_op jit(solution)/shard_map/ppermute | solution.py:396
  22.8 3.6 %collective-permute-start.4 = (f32[8,1584]{1,0:T(8,128)S(1)}, f32[8,1584]{1,0:T(8,128)S(1)}, u32[]{:S(2)}, u32[]{:S(2)}) collective-permute-start(f32[8,1584]{1,0:T(8,128)S(1)} %get-tuple-element.20), channel_id=1, source_target_pairs={{0,1},{1,2},{2,3},{4,5},{5,6},{6,7},{8,9},{9,10},{10,11},{12,13},{... | collective-permute-start | bytes 152072 | tf_op jit(solution)/shard_map/ppermute | solution.py:396
  25.0 4.9 %collective-permute-start.5 = (f32[8,1584]{1,0:T(8,128)S(1)}, f32[8,1584]{1,0:T(8,128)S(1)}, u32[]{:S(2)}, u32[]{:S(2)}) collective-permute-start(f32[8,1584]{1,0:T(8,128)S(1)} %get-tuple-element.20), channel_id=1, source_target_pairs={{1,0},{2,1},{3,2},{5,4},{6,5},{7,6},{9,8},{10,9},{11,10},{13,12},{... | collective-permute-start | bytes 152072 | tf_op jit(solution)/shard_map/ppermute | solution.py:396
  34.6 1.0 copy-start
  35.7 5.3 %collective-permute-start.6 = (f32[3,8,4,128]{3,2,1,0:T(4,128)S(1)}, f32[3,8,4,128]{3,2,1,0:T(4,128)S(1)}, u32[]{:S(2)}, u32[]{:S(2)}) collective-permute-start(f32[3,8,4,128]{3,2,1,0:T(4,128)S(1)} %get-tuple-element.40), channel_id=1, source_target_pairs={{0,4},{4,8},{8,12},{12,16},{16,20},{20,24},{24,28},{1,5},{5,9},{9,... | collective-permute-start | bytes 147464 | tf_op jit(solution)/shard_map/ppermute | solution.py:396
  39.7 7.2 %collective-permute-start.7 = (f32[3,8,4,128]{3,2,1,0:T(4,128)S(1)}, f32[3,8,4,128]{3,2,1,0:T(4,128)S(1)}, u32[]{:S(2)}, u32[]{:S(2)}) collective-permute-start(f32[3,8,4,128]{3,2,1,0:T(4,128)S(1)} %get-tuple-element.39), channel_id=1, source_target_pairs={{4,0},{8,4},{12,8},{16,12},{20,16},{24,20},{28,24},{5,1},{9,5},{13... | collective-permute-start | bytes 147464 | tf_op jit(solution)/shard_map/ppermute | solution.py:396
  46.9 8.7 %collective-permute-start.9 = (f32[3,4,16,128]{3,2,1,0:T(8,128)S(1)}, f32[3,4,16,128]{3,2,1,0:T(8,128)S(1)}, u32[]{:S(2)}, u32[]{:S(2)}) collective-permute-start(f32[3,4,16,128]{3,2,1,0:T(8,128)S(1)} %pad_maximum_fusion.4), channel_id=1, source_target_pairs={{32,0},{64,32},{96,64},{128,96},{160,128},{192,160},{224,192},{256... | collective-permute-start | bytes 294920 | tf_op jit(solution)/shard_map/ppermute | solution.py:396
  49.6 7.3 %collective-permute-start.8 = (f32[3,4,16,128]{3,2,1,0:T(8,128)S(1)}, f32[3,4,16,128]{3,2,1,0:T(8,128)S(1)}, u32[]{:S(2)}, u32[]{:S(2)}) collective-permute-start(f32[3,4,16,128]{3,2,1,0:T(8,128)S(1)} %pad_maximum_fusion.3), channel_id=1, source_target_pairs={{0,32},{32,64},{64,96},{96,128},{128,160},{160,192},{192,224},{224... | collective-permute-start | bytes 294920 | tf_op jit(solution)/shard_map/ppermute | solution.py:396
  57.2 4.4 %collective-permute-start.10 = (f32[8,768]{1,0:T(8,128)S(1)}, f32[8,768]{1,0:T(8,128)S(1)}, u32[]{:S(2)}, u32[]{:S(2)}) collective-permute-start(f32[8,768]{1,0:T(8,128)S(1)} %get-tuple-element.23), channel_id=1, source_target_pairs={{0,1},{1,2},{2,3},{4,5},{5,6},{6,7},{8,9},{9,10},{10,11},{12,13},{... | collective-permute-start | bytes 73736 | tf_op jit(solution)/shard_map/ppermute | solution.py:396
  60.3 4.6 %collective-permute-start.11 = (f32[8,768]{1,0:T(8,128)S(1)}, f32[8,768]{1,0:T(8,128)S(1)}, u32[]{:S(2)}, u32[]{:S(2)}) collective-permute-start(f32[8,768]{1,0:T(8,128)S(1)} %get-tuple-element.23), channel_id=1, source_target_pairs={{1,0},{2,1},{3,2},{5,4},{6,5},{7,6},{9,8},{10,9},{11,10},{13,12},{... | collective-permute-start | bytes 73736 | tf_op jit(solution)/shard_map/ppermute | solution.py:396
  68.1 0.7 copy-start.4
  68.1 39.2 %copy-start.6 = (f32[2,16,16,128]{3,2,1,0:T(8,128)}, f32[2,16,16,128]{3,2,1,0:T(8,128)S(1)}, u32[]{:S(2)}) copy-start(f32[2,16,16,128]{3,2,1,0:T(8,128)S(1)} %get-tuple-element.29.v21) | copy-start | bytes 786436
  89.9 10.8 %collective-permute-start.12 = (f32[32,24,128]{2,1,0:T(8,128)S(1)}, f32[32,24,128]{2,1,0:T(8,128)S(1)}, u32[]{:S(2)}, u32[]{:S(2)}) collective-permute-start(f32[32,24,128]{2,1,0:T(8,128)S(1)} %all_to_all.10.own), channel_id=1, source_target_pairs={{0,32},{32,64},{64,96},{96,128},{128,160},{160,192},{192,224},{224... | collective-permute-start | bytes 1179656 | tf_op jit(solution)/shard_map/ppermute | solution.py:396
  96.0 9.1 %collective-permute-start.13 = (f32[32,24,128]{2,1,0:T(8,128)S(1)}, f32[32,24,128]{2,1,0:T(8,128)S(1)}, u32[]{:S(2)}, u32[]{:S(2)}) collective-permute-start(f32[32,24,128]{2,1,0:T(8,128)S(1)} %all_to_all.10.own), channel_id=1, source_target_pairs={{32,0},{64,32},{96,64},{128,96},{160,128},{192,160},{224,192},{256... | collective-permute-start | bytes 1179656 | tf_op jit(solution)/shard_map/ppermute | solution.py:396
  107.3 0.9 copy-start.2
  109.1 23.5 %all-to-all-start.1 = ((f32[16,48,128]{2,1,0:T(8,128)}), f32[16,48,128]{2,1,0:T(8,128)S(1)}, u32[]{:S(2)}, u32[]{:S(2)}) async-start(f32[16,48,128]{2,1,0:T(8,128)} %broadcast_in_dim.15), calls=%async_computation.1 | async-start | bytes 786432 | tf_op jit(solution)/shard_map/all_to_all | solution.py:420
  132.5 1.2 copy-start.1
  133.8 1.2 copy-start.3
  135.0 0.9 copy-start.5
  135.9 0.9 copy-start.7

commit v2 on v1

--- a/solution.py
+++ b/solution.py
@@ -10,8 +10,10 @@
 F32, BF16 = jnp.float32, jnp.bfloat16
 WAVE = 0.0625
 DIAG_I = 0.5 * WAVE
+MOST = (2, 7, 5, 8, 16)
 
 X0, Y0, L0 = 22, 24, 256
+HZ = 10
 X1, Y1, L1 = 16, 16, 128
 X2, Y2 = 12, 32
 X3, Y3, PAD3 = 32, 16, 4
@@ -80,27 +82,43 @@
     )
 
 
+def blocks(count, most, compute, store):
+    unit = max(u for u in range(1, most + 1) if count % u == 0)
+
+    def body(k, _):
+        steps = [k * unit + u for u in range(unit)]
+        for j, value in zip(steps, [compute(j) for j in steps]):
+            store(j, value)
+        return 0
+
+    if count == unit:
+        body(0, 0)
+    else:
+        lax.fori_loop(0, count // unit, body, 0)
+
+
 def first_loop(lo, hi, g, hd, v, level):
-    def body(i, _):
+    def compute(j):
+        i = lo + j
         h_r, h_i = half_inverse(g[2, i], level)
-        hd[0, i], hd[1, i] = h_r, h_i
         g_r, g_i = g[0, i], g[1, i]
-        v[0, i] = h_r * g_r - h_i * g_i
-        v[1, i] = h_r * g_i + h_i * g_r
-        return 0
-
-    lax.fori_loop(lo, hi, body, 0)
+        return h_r, h_i, h_r * g_r - h_i * g_i, h_r * g_i + h_i * g_r
+
+    def store(j, value):
+        i = lo + j
+        hd[0, i], hd[1, i], v[0, i], v[1, i] = value
+
+    blocks(hi - lo, MOST[level], compute, store)
 
 
 def relax_loop(lo, count, g, hd, v, write, level, ymask=False, zmask=False):
-    def body(j, _):
+    def compute(j):
         i = lo + j
-        t_r, t_i, c_r, c_i, _d = balance(g[0, i], g[1, i], g[2, i], v, i, level, ymask, zmask)
+        t_r, t_i, c_r, c_i, _ = balance(g[0, i], g[1, i], g[2, i], v, i, level, ymask, zmask)
         h_r, h_i = hd[0, i], hd[1, i]
-        write(j, i, 0.5 * c_r + (h_r * t_r - h_i * t_i), 0.5 * c_i + (h_r * t_i + h_i * t_r))
-        return 0
-
-    lax.fori_loop(0, count, body, 0)
+        return 0.5 * c_r + (h_r * t_r - h_i * t_i), 0.5 * c_i + (h_r * t_i + h_i * t_r)
+
+    blocks(count, MOST[level], compute, lambda j, value: write(j, lo + j, *value))
 
 
 def writer(out):
@@ -136,72 +154,77 @@
     return jnp.where(rule(iota(shape, 0), iota(shape, 1)), value, 0.0).astype(BF16)
 
 
-def gather_kernel(own_lanes, width, own, ylo, yhi, xlo, xhi, f, packed):
-    count = own.shape[1]
-    rows = own.shape[2]
-    hx = xlo.shape[1]
+def assemble(own, ylo, yhi, xlo, xhi, f):
+    count, rows, hx = own.shape[1], own.shape[2], xlo.shape[1]
     for c in range(3):
         f[c, 0:hx] = xlo[c]
         f[c, hx : hx + count, 0:4] = ylo[c]
         f[c, hx : hx + count, 4 : 4 + rows] = own[c]
         f[c, hx : hx + count, 4 + rows :] = yhi[c]
         f[c, hx + count :] = xhi[c]
-    edge = matrix(
-        8,
-        128,
-        lambda r, l: ((r < 4) & (l == r)) | ((r >= 4) & (l == own_lanes - 8 + r)),
-    )
-    flat = f[...].reshape(-1, 128)
-    total = None
-    for part in split(flat):
-        term = lax.dot_general(edge, part, (((1,), (1,)), ((), ())), preferred_element_type=F32)
-        total = term if total is None else total + term
-    packed[...] = total
-
-
-def unpack_lanes(lower, upper, lower_start, upper_start):
+
+
+def views(kept):
+    return kept.at[0:3], kept.at[3:5], kept.at[5:7]
+
+
+def gather0_kernel(own, ylo, yhi, xlo, xhi, f, low_lanes, high_lanes):
+    assemble(own, ylo, yhi, xlo, xhi, f)
+    parts = split(f[...].reshape(-1, 128))
+    for out, start in ((low_lanes, 0), (high_lanes, 118)):
+        edge = matrix(16, 128, lambda r, l: (r < HZ) & (l == start + r))
+        dims = (((1,), (1,)), ((), ()))
+        terms = [lax.dot_general(edge, p, dims, preferred_element_type=F32) for p in parts]
+        out[...] = terms[0] + (terms[1] + terms[2])
+
+
+def smooth0(f, lower, upper, g, hd, v2, v1):
     both = jnp.concatenate([upper[...], lower[...]], axis=0)
-    place = matrix(
-        16,
-        128,
-        lambda r, l: ((r < 4) & (l == upper_start + r)) | ((r >= 12) & (l == lower_start + r - 12)),
-    )
-    return select(both, place, (((0,), (0,)), ((), ())))
-
-
-def down0_kernel(f, lower, upper, g, hd, v2, coarse, v1, sums):
-    tail = unpack_lanes(lower, upper, 124, 0).reshape(3, X0, Y0, 128)
+    place = matrix(32, 128, lambda r, l: ((r < HZ) & (l == r)) | ((r >= 16) & (l == r + 102)))
+    tail = select(both, place, (((0,), (0,)), ((), ())))
     g[:, :, :, 0:128] = f[...]
-    g[:, :, :, 128:256] = tail
+    g[:, :, :, 128:256] = tail.reshape(3, X0, Y0, 128)
     first_loop(0, X0, g, hd, v1, 0)
     relax_loop(1, X0 - 2, g, hd, v1, writer(v2), 0)
 
-    def body(k, _):
-        parts = residual_pair(g, v2, 3 + 2 * k, 0)
+
+def keep0_kernel(f, lower, upper, kept, v1):
+    smooth0(f, lower, upper, *views(kept), v1)
+
+
+def down0_kernel(f, lower, upper, coarse, g, hd, v2, v1, sums):
+    smooth0(f, lower, upper, g, hd, v2, v1)
+
+    def store(k, parts):
         for c in range(3):
             row = pl.multiple_of((c * 8 + k) * 16, 16)
-            sums[pl.ds(row, 16), :] = parts[c][4:20, 0:128]
-        return 0
-
-    lax.fori_loop(0, 8, body, 0)
-    halve = matrix(128, 128, lambda r, l: r // 2 == l, 0.125)
-    coarse[...] = select(pair_rows(sums, 384), halve).reshape(3, 8, 8, 128)
-
-
-def down1_kernel(f, lower, upper, g, hd, v2, chunk, v1, sums, g2, hd2, va, vb):
-    tail = unpack_lanes(lower, upper, 124, 64).reshape(3, X1, Y1, 128)
-    g[...] = f[...] + tail
+            for half in range(2):
+                sums[half, pl.ds(row, 16), :] = parts[c][4:20, 128 * half : 128 * half + 128]
+
+    blocks(8, 1, lambda k: residual_pair(g, v2, 3 + 2 * k, 0), store)
+    own = matrix(128, 128, lambda r, l: r // 2 == l, 0.125)
+    rest = matrix(
+        128,
+        128,
+        lambda r, l: ((r < 8) & (r // 2 + 64 == l)) | ((r >= 120) & (r // 2 + 64 == l)),
+        0.125,
+    )
+    total = select(pair_rows(sums.at[0], 384), own) + select(pair_rows(sums.at[1], 384), rest)
+    coarse[...] = total.reshape(3, 8, 8, 128)
+
+
+def down1_kernel(own, ylo, yhi, xlo, xhi, kept, chunk, v1, sums, g2, hd2, va, vb):
+    g, hd, v2 = views(kept)
+    assemble(own, ylo, yhi, xlo, xhi, g)
     first_loop(0, X1, g, hd, v1, 1)
     relax_loop(1, X1 - 2, g, hd, v1, writer(v2), 1)
 
-    def body(k, _):
-        parts = residual_pair(g, v2, 2 + 2 * k, 1)
+    def store(k, parts):
         for c in range(3):
             row = pl.multiple_of((c * 6 + k) * 16, 16)
             sums[pl.ds(row, 16), :] = parts[c]
-        return 0
-
-    lax.fori_loop(0, 6, body, 0)
+
+    blocks(6, 3, lambda k: residual_pair(g, v2, 2 + 2 * k, 1), store)
     halve = matrix(
         128,
         128,
@@ -212,13 +235,12 @@
     first_loop(0, 6, g2, hd2, va, 2)
     relax_loop(1, 4, g2, hd2, va, writer(vb), 2)
     lane = iota((8, 128), 1) // 32
-    chunk[...] = jnp.zeros_like(chunk)
     for c in range(5):
         source = (lambda x: g2[c, x]) if c < 3 else (lambda x: vb[c - 3, x])
         total = source(1)
         for x in range(1, 4):
             total = jnp.where(lane == x, pltpu.roll(source(1 + x), 32 * x, 1), total)
-        chunk[4 * c : 4 * c + 4, :] = total[2:6, :]
+        chunk[c] = total[2:6, :]
 
 
 def down2_kernel(own, left, right, a, chunk, planes, sums):
@@ -228,7 +250,7 @@
         def body(c, _):
             for gz in range(4):
                 for gy in range(8):
-                    planes[gz, 4 * gy : 4 * gy + 4, :] = piece[gy * 4 + gz, pl.ds(4 * c, 4), :]
+                    planes[gz, 4 * gy : 4 * gy + 4, :] = piece[gy * 4 + gz, c]
             for x in range(4):
                 total = None
                 for gz in range(4):
@@ -254,10 +276,12 @@
 
 
 def up_kernel(
-    index, parts3, a, g1, hd1, v21, g0, hd0, v20, out,
+    index, parts3, a, kept1, kept0, out,
     g3, hd3, va3, vb3, s3, g4, hd4, va4, vb4, t4, w3, t3, hd2, va2, vb2, w2, t2, va1, vb1, t1, va0, vb0,
 ):
     gx, gy, gz = index[0], index[1], index[2]
+    g1, hd1, v21 = views(kept1)
+    g0, hd0, v20 = views(kept0)
     zero3 = jnp.zeros((Y3, 128), F32)
     for ref in (g3, hd3, va3, vb3):
         for c in range(ref.shape[0]):
@@ -277,13 +301,11 @@
     first_loop(PAD3, PAD3 + X3, g3, hd3, va3, 3)
     relax_loop(PAD3, X3, g3, hd3, va3, writer(vb3), 3, True)
 
-    def body3(k, _):
-        parts = residual_pair(g3, vb3, PAD3 + 2 * k, 3, True)
+    def keep3(k, parts):
         for c in range(3):
             s3[pl.ds(pl.multiple_of((c * X4 + k) * Y3, Y3), Y3), :] = parts[c]
-        return 0
-
-    lax.fori_loop(0, X4, body3, 0)
+
+    blocks(X4, 4, lambda k: residual_pair(g3, vb3, PAD3 + 2 * k, 3, True), keep3)
     halve = matrix(128, 128, lambda r, l: (r // 2 == l) & (r < 64), 0.125)
     g4[:, 1 : 1 + X4] = select(pair_rows(s3, 3 * X4 * Y3), halve).reshape(3, X4, Y4, 128)
     for ref in (va4, vb4):
@@ -371,22 +393,17 @@
     relax_loop(3, X0 - 6, g0, hd0, vb0, write0, 0)
 
 
-def vmem(*shape):
-    return pltpu.VMEM(shape, F32)
-
-
-def call(kernel, outs, scratch, *args, smem_first=False):
-    spec = pl.BlockSpec(memory_space=pltpu.VMEM)
-    specs = [spec] * len(args)
-    if smem_first:
-        specs[0] = pl.BlockSpec(memory_space=pltpu.SMEM)
+def call(kernel, outs, scratch, *args, limit=12, memory="", cost=None):
+    memory = memory or "v" * (len(args) + len(outs))
+    specs = [pl.BlockSpec(memory_space=pltpu.SMEM if m == "s" else pltpu.VMEM) for m in memory]
     return pl.pallas_call(
         kernel,
         out_shape=[jax.ShapeDtypeStruct(s, F32) for s in outs],
-        in_specs=specs,
-        out_specs=[spec] * len(outs),
-        scratch_shapes=[vmem(*s) for s in scratch],
-        compiler_params=pltpu.CompilerParams(vmem_limit_bytes=48 << 20),
+        in_specs=specs[: len(args)],
+        out_specs=specs[len(args) :],
+        scratch_shapes=[pltpu.VMEM(s, F32) for s in scratch],
+        compiler_params=pltpu.CompilerParams(vmem_limit_bytes=limit << 20),
+        cost_estimate=cost and pl.CostEstimate(cost[0], 0, cost[1]),
     )(*args)
 
 
@@ -396,23 +413,15 @@
     return lax.ppermute(block, axis, pairs)
 
 
-def with_halos(own, hx, own_lanes):
-    rows = own.shape[2]
-    count = own.shape[1]
+def halos(own, hx):
+    count, rows = own.shape[1], own.shape[2]
     ylo = shift(own[:, :, rows - 4 :], "gy", 1)
     yhi = shift(own[:, :, :4], "gy", -1)
 
     def edge(at):
         return jnp.concatenate([x[:, at : at + hx] for x in (ylo, own, yhi)], axis=2)
 
-    xlo = shift(edge(count - hx), "gx", 1)
-    xhi = shift(edge(0), "gx", -1)
-    shape = (3, count + 2 * hx, rows + 8, 128)
-    flat = shape[0] * shape[1] * shape[2]
-    f, packed = call(
-        functools.partial(gather_kernel, own_lanes, None), [shape, (8, flat)], [], own, ylo, yhi, xlo, xhi
-    )
-    return f, shift(packed, "gz", 1), shift(packed, "gz", -1)
+    return own, ylo, yhi, shift(edge(count - hx), "gx", 1), shift(edge(0), "gx", -1)
 
 
 def everyone(block, axes):
@@ -422,32 +431,29 @@
 
 def shards(source_field, mach_number):
     own0 = jnp.concatenate([source_field, mach_number.astype(F32)[None]], axis=0)
-    f0, lower0, upper0 = with_halos(own0, 3, 128)
-    full0 = (X0, Y0, L0)
-    g0, hd0, v20, own1 = call(
-        down0_kernel,
-        [(3,) + full0, (2,) + full0, (2,) + full0, (3, 8, 8, 128)],
-        [(2,) + full0, (384, 128)],
-        f0, lower0, upper0,
-    )
-    f1, lower1, upper1 = with_halos(own1, 4, 64)
-    full1 = (X1, Y1, L1)
-    g1, hd1, v21, chunk2 = call(
+    flat = (16, 3 * X0 * Y0)
+    f0, low, high = call(gather0_kernel, [(3, X0, Y0, 128), flat, flat], [], *halos(own0, 3))
+    full0, full1 = (X0, Y0, L0), (X1, Y1, L1)
+    block0 = (f0, shift(high, "gz", 1), shift(low, "gz", -1))
+    smoothed0 = [(3,) + full0] + [(2,) + full0] * 3
+    (own1,) = call(
+        down0_kernel, [(3, 8, 8, 128)], smoothed0 + [(2, 384, 128)], *block0
+    )
+    kept1, chunk2 = call(
         down1_kernel,
-        [(3,) + full1, (2,) + full1, (2,) + full1, (24, 128)],
+        [(7,) + full1, (5, 4, 128)],
         [(2,) + full1, (288, 128), (3, 6, 8, 128)] + [(2, 6, 8, 128)] * 3,
-        f1, lower1, upper1,
+        *halos(own1, 4),
     )
     own2 = everyone(chunk2, ("gy", "gz"))
-    left2 = shift(own2, "gx", 1)
-    right2 = shift(own2, "gx", -1)
     a, chunk3 = call(
         down2_kernel,
         [(5, X2, Y2, 128), (48, 128)],
         [(4, Y2, 128), (2, 96, 128)],
-        own2, left2, right2,
+        own2, shift(own2, "gx", 1), shift(own2, "gx", -1),
     )
     parts3 = everyone(chunk3, "gx")
+    (kept0,) = call(keep0_kernel, [(7,) + full0], [(2,) + full0], *block0, cost=(60 << 20, 8 << 20))
     index = jnp.stack([lax.axis_index(n) for n in ("gx", "gy", "gz")]).astype(jnp.int32)
     wide3 = (X3 + 2 * PAD3, Y3, 128)
     wide4 = (X4 + 2, Y4, 128)
@@ -460,8 +466,9 @@
         up_kernel,
         [(2, 16, 16, 128)],
         scratch,
-        index, parts3, a, g1, hd1, v21, g0, hd0, v20,
-        smem_first=True,
+        index, parts3, a, kept1, kept0,
+        limit=16,
+        memory="svvvvv",
     )[0]
 
 

time: 162 us -> 131 us (0.81)
  Pallas kernels: 35.1 us -> 20.6 us
  waiting for transfers between devices: 41.5 us -> 32.6 us
  starting transfers between devices: 52.3 us -> 47.5 us
  local copies, waits for them, and re-layouts: 7.78 us -> 4.75 us
    pallas_call x6, Pallas kernels: 35.1 us -> 20.6 us  [call(): pl.pallas_call(kernel, out_shape=[jax.ShapeDtypeStruct(s, F32) for s in o...]
    ppermute x14 -> x12, starting transfers between devices: 43.4 us -> 38.9 us  [shift(): return lax.ppermute(block, axis, pairs)]
    all_to_all x1, waiting for transfers between devices: 14.5 us -> 9.99 us  [everyone(): lax.all_to_all(jnp.broadcast_to(block, (count,) + block.shape), axes, 0, 0)]
    ppermute x14 -> x12, waiting for transfers between devices: 27 us -> 22.6 us  [shift(): return lax.ppermute(block, axis, pairs)]
    unnamed x18 -> x4, local copies, waits for them, and re-layouts: 6.93 us -> 3.88 us
  transfers between devices with their start and end apart: 15 -> 13, of which waited for: 10 -> 10; matrix products, arithmetic and copies ran while one was open for 1% -> 2% of each run, Pallas kernels for 0% -> 2%
where the time goes in v2:
time: 131 us
  starting transfers between devices  47.5 us (36%)
  waiting for transfers between devices  32.6 us (25%)
  blocking collectives  20.9 us (16%)
  Pallas kernels  20.6 us (16%)
  local copies, waits for them, and re-layouts  4.75 us (4%)
  other arithmetic  3.83 us (3%)
    ppermute x12, starting transfers between devices, shift(): return lax.ppermute(block, axis, pairs)  38.9 us
    ppermute x12, waiting for transfers between devices, shift(): return lax.ppermute(block, axis, pairs)  22.6 us
    all_to_all x1, blocking collectives, everyone(): lax.all_to_all(jnp.broadcast_to(block, (count,) + block.shape), axes, 0, 0)  20.9 us
    pallas_call x6, Pallas kernels, call(): pl.pallas_call(kernel, out_shape=[jax.ShapeDtypeStruct(s, F32) for s in o...  20.6 us
    all_to_all x1, waiting for transfers between devices, everyone(): lax.all_to_all(jnp.broadcast_to(block, (count,) + block.shape), axes, 0, 0)  9.99 us
    all_to_all x1, starting transfers between devices, everyone(): lax.all_to_all(jnp.broadcast_to(block, (count,) + block.shape), axes, 0, 0)  8.63 us
    unnamed x4, local copies, waits for them, and re-layouts  3.88 us
    concatenate x3, other arithmetic, shards(): jnp.concatenate([source_field, mach_number.astype(F32)[None]], axis=0)  2.83 us
  transfers between devices with their start and end apart: 13, of which 10 were waited for; matrix products, arithmetic and copies ran while one was open for 2% of the time, Pallas kernels for 2%

profile of v2, /device:TPU:1, one launch (start us, length us, event | category | flops | bytes accessed | tf_op | source)
XLA Modules:
  0.0 130.5 jit_solution(9536649639671810321)
XLA Ops:
  0.0 0.8 bitcast_convert_fusion
  0.9 1.0 fusion.1
  1.9 4.8 %collective-permute-start = (f32[3,16,4,128]{3,2,1,0:T(4,128)S(1)}, f32[3,16,4,128]{3,2,1,0:T(4,128)S(1)}, u32[]{:S(2)}, u32[]{:S(2)}) collective-permute-start(f32[3,16,4,128]{3,2,1,0:T(4,128)S(1)} %get-tuple-element.22), channel_id=1, source_target_pairs={{0,4},{4,8},{8,12},{12,16},{16,20},{20,24},{24,28},{1,5},{5,9},{9,... | collective-permute-start | bytes 294920 | tf_op jit(solution)/shard_map/ppermute | solution.py:413
  6.7 1.3 collective-permute-start.1
  8.0 0.8 fusion.3
  8.8 0.0 collective-permute-done.ylo
  8.9 3.8 %collective-permute-done.1.yhi = f32[3,16,4,128]{3,2,1,0:T(4,128)S(1)} collective-permute-done((f32[3,16,4,128]{3,2,1,0:T(4,128)S(1)}, f32[3,16,4,128]{3,2,1,0:T(4,128)S(1)}, u32[]{:S(2)}, u32[]{:S(2)}) %collective-permute-start.1) | collective-permute-done | bytes 98336 | tf_op jit(solution)/shard_map/ppermute | solution.py:413
  12.7 5.8 %collective-permute-start.3 = (f32[3,3,24,128]{3,2,1,0:T(8,128)S(1)}, f32[3,3,24,128]{3,2,1,0:T(8,128)S(1)}, u32[]{:S(2)}, u32[]{:S(2)}) collective-permute-start(f32[3,3,24,128]{3,2,1,0:T(8,128)S(1)} %pad_maximum_fusion.2), channel_id=1, source_target_pairs={{32,0},{64,32},{96,64},{128,96},{160,128},{192,160},{224,192},{256... | collective-permute-start | bytes 331784 | tf_op jit(solution)/shard_map/ppermute | solution.py:413
  18.5 1.9 %collective-permute-start.2 = (f32[3,3,24,128]{3,2,1,0:T(8,128)S(1)}, f32[3,3,24,128]{3,2,1,0:T(8,128)S(1)}, u32[]{:S(2)}, u32[]{:S(2)}) collective-permute-start(f32[3,3,24,128]{3,2,1,0:T(8,128)S(1)} %pad_maximum_fusion.1), channel_id=1, source_target_pairs={{0,32},{32,64},{64,96},{96,128},{128,160},{160,192},{192,224},{224... | collective-permute-start | bytes 331784 | tf_op jit(solution)/shard_map/ppermute | solution.py:413
  20.5 1.0 pad_maximum_fusion.own
  21.4 0.0 collective-permute-done.3.xhi
  21.5 0.7 collective-permute-done.2.xlo
  22.2 0.8 shard_map.28
  23.0 2.3 %collective-permute-start.4 = (f32[16,1584]{1,0:T(8,128)S(1)}, f32[16,1584]{1,0:T(8,128)S(1)}, u32[]{:S(2)}, u32[]{:S(2)}) collective-permute-start(f32[16,1584]{1,0:T(8,128)S(1)} %get-tuple-element.13), channel_id=1, source_target_pairs={{0,1},{1,2},{2,3},{4,5},{5,6},{6,7},{8,9},{9,10},{10,11},{12,13},{... | collective-permute-start | bytes 304136 | tf_op jit(solution)/shard_map/ppermute | solution.py:413
  25.3 1.3 collective-permute-start.5
  26.6 0.5 collective-permute-done.4.lower
  27.1 4.1 %collective-permute-done.5.upper = f32[16,1584]{1,0:T(8,128)S(1)} collective-permute-done((f32[16,1584]{1,0:T(8,128)S(1)}, f32[16,1584]{1,0:T(8,128)S(1)}, u32[]{:S(2)}, u32[]{:S(2)}) %collective-permute-start.5) | collective-permute-done | bytes 101408 | tf_op jit(solution)/shard_map/ppermute | solution.py:413
  31.2 4.1 %shard_map.29.own = f32[3,8,8,128]{3,2,1,0:T(8,128)S(1)} custom-call(f32[3,22,24,128]{3,2,1,0:T(8,128)S(1)} %get-tuple-element.12.f, f32[16,1584]{1,0:T(8,128)S(1)} %collective-permute-done.4.lower, f32[16,1584]{1,0:T(8,128)S(1)} %collective-permute-done.5.upper), custom_call_target="tpu_custom_call" | custom-call | tf_op jit(solution)/shard_map/pallas_call | solution.py:399
  35.3 4.0 %collective-permute-start.6 = (f32[3,8,4,128]{3,2,1,0:T(4,128)S(1)}, f32[3,8,4,128]{3,2,1,0:T(4,128)S(1)}, u32[]{:S(2)}, u32[]{:S(2)}) collective-permute-start(f32[3,8,4,128]{3,2,1,0:T(4,128)S(1)} %get-tuple-element.26), channel_id=1, source_target_pairs={{0,4},{4,8},{8,12},{12,16},{16,20},{20,24},{24,28},{1,5},{5,9},{9,... | collective-permute-start | bytes 147464 | tf_op jit(solution)/shard_map/ppermute | solution.py:413
  39.4 1.3 collective-permute-start.7
  40.7 0.0 collective-permute-done.6.ylo
  40.7 5.4 %collective-permute-done.7.yhi = f32[3,8,4,128]{3,2,1,0:T(4,128)S(1)} collective-permute-done((f32[3,8,4,128]{3,2,1,0:T(4,128)S(1)}, f32[3,8,4,128]{3,2,1,0:T(4,128)S(1)}, u32[]{:S(2)}, u32[]{:S(2)}) %collective-permute-start.7) | collective-permute-done | bytes 49184 | tf_op jit(solution)/shard_map/ppermute | solution.py:413
  46.1 3.1 %collective-permute-start.9 = (f32[3,4,16,128]{3,2,1,0:T(8,128)S(1)}, f32[3,4,16,128]{3,2,1,0:T(8,128)S(1)}, u32[]{:S(2)}, u32[]{:S(2)}) collective-permute-start(f32[3,4,16,128]{3,2,1,0:T(8,128)S(1)} %pad_maximum_fusion.4), channel_id=1, source_target_pairs={{32,0},{64,32},{96,64},{128,96},{160,128},{192,160},{224,192},{256... | collective-permute-start | bytes 294920 | tf_op jit(solution)/shard_map/ppermute | solution.py:413
  49.3 5.2 %collective-permute-start.8 = (f32[3,4,16,128]{3,2,1,0:T(8,128)S(1)}, f32[3,4,16,128]{3,2,1,0:T(8,128)S(1)}, u32[]{:S(2)}, u32[]{:S(2)}) collective-permute-start(f32[3,4,16,128]{3,2,1,0:T(8,128)S(1)} %pad_maximum_fusion.3), channel_id=1, source_target_pairs={{0,32},{32,64},{64,96},{96,128},{128,160},{160,192},{192,224},{224... | collective-permute-start | bytes 294920 | tf_op jit(solution)/shard_map/ppermute | solution.py:413
  54.5 0.3 collective-permute-done.9.xhi
  54.8 1.3 collective-permute-done.8.xlo
  56.1 1.1 shard_map.30
  57.2 20.9 %all_to_all.10.own = f32[32,5,4,128]{3,2,1,0:T(4,128)S(1)} all-to-all(f32[32,5,4,128]{3,2,1,0:T(4,128)S(1)} %broadcast_in_dim.14), channel_id=1, replica_groups=mesh['gx'=16,'gy'=8,'gz'=4] {'gy','gz'}, dimensions={0} | all-to-all | bytes 655360 | tf_op jit(solution)/shard_map/all_to_all | solution.py:429
  78.2 6.0 %collective-permute-start.10 = (f32[32,5,4,128]{3,2,1,0:T(4,128)S(1)}, f32[32,5,4,128]{3,2,1,0:T(4,128)S(1)}, u32[]{:S(2)}, u32[]{:S(2)}) collective-permute-start(f32[32,5,4,128]{3,2,1,0:T(4,128)S(1)} %all_to_all.10.own), channel_id=1, source_target_pairs={{0,32},{32,64},{64,96},{96,128},{128,160},{160,192},{192,224},{224... | collective-permute-start | bytes 983048 | tf_op jit(solution)/shard_map/ppermute | solution.py:413
  84.2 1.9 %collective-permute-start.11 = (f32[32,5,4,128]{3,2,1,0:T(4,128)S(1)}, f32[32,5,4,128]{3,2,1,0:T(4,128)S(1)}, u32[]{:S(2)}, u32[]{:S(2)}) collective-permute-start(f32[32,5,4,128]{3,2,1,0:T(4,128)S(1)} %all_to_all.10.own), channel_id=1, source_target_pairs={{32,0},{64,32},{96,64},{128,96},{160,128},{192,160},{224,192},{256... | collective-permute-start | bytes 983048 | tf_op jit(solution)/shard_map/ppermute | solution.py:413
  86.1 2.1 %collective-permute-done.10.left = f32[32,5,4,128]{3,2,1,0:T(4,128)S(1)} collective-permute-done((f32[32,5,4,128]{3,2,1,0:T(4,128)S(1)}, f32[32,5,4,128]{3,2,1,0:T(4,128)S(1)}, u32[]{:S(2)}, u32[]{:S(2)}) %collective-permute-start.10) | collective-permute-done | bytes 327712 | tf_op jit(solution)/shard_map/ppermute | solution.py:413
  88.2 4.4 %collective-permute-done.11.right = f32[32,5,4,128]{3,2,1,0:T(4,128)S(1)} collective-permute-done((f32[32,5,4,128]{3,2,1,0:T(4,128)S(1)}, f32[32,5,4,128]{3,2,1,0:T(4,128)S(1)}, u32[]{:S(2)}, u32[]{:S(2)}) %collective-permute-start.11) | collective-permute-done | bytes 327712 | tf_op jit(solution)/shard_map/ppermute | solution.py:413
  92.5 2.2 %shard_map.31 = (f32[5,12,32,128]{3,2,1,0:T(8,128)S(1)}, f32[48,128]{1,0:T(8,128)S(1)}) custom-call(f32[32,5,4,128]{3,2,1,0:T(4,128)S(1)} %all_to_all.10.own, f32[32,5,4,128]{3,2,1,0:T(4,128)S(1)} %collective-permute-done.10.left, f32[32,5,4,128]{3,2,1,0:T(4,128)S(1)} %collective-permute-done.11.right), custom_call_target="tpu_custom_call" | custom-call | tf_op jit(solution)/shard_map/pallas_call | solution.py:399
  94.8 0.8 broadcast_in_dim.15
  95.6 8.6 %all-to-all-start.1 = ((f32[16,48,128]{2,1,0:T(8,128)}), f32[16,48,128]{2,1,0:T(8,128)S(1)}, u32[]{:S(2)}, u32[]{:S(2)}) async-start(f32[16,48,128]{2,1,0:T(8,128)} %broadcast_in_dim.15), calls=%async_computation.1 | async-start | bytes 786432 | tf_op jit(solution)/shard_map/all_to_all | solution.py:429
  104.2 0.1 pad_add_fusion.index
  104.3 2.7 %shard_map.32.kept0 = f32[7,22,24,256]{3,2,1,0:T(8,128)S(1)} custom-call(f32[3,22,24,128]{3,2,1,0:T(8,128)S(1)} %get-tuple-element.12.f, f32[16,1584]{1,0:T(8,128)S(1)} %collective-permute-done.4.lower, f32[16,1584]{1,0:T(8,128)S(1)} %collective-permute-done.5.upper), custom_call_target="tpu_custom_call" | custom-call | flops 62914560 | bytes 8388608 | tf_op jit(solution)/shard_map/pallas_call | solution.py:399
  106.9 0.0 copy-start
  106.9 1.8 %copy-done = f32[7,22,24,256]{3,2,1,0:T(8,128)} copy-done((f32[7,22,24,256]{3,2,1,0:T(8,128)}, f32[7,22,24,256]{3,2,1,0:T(8,128)S(1)}, u32[]{:S(2)}) %copy-start) | copy-done | bytes 3784728
  108.7 10.0 %all-to-all-done.1.parts3 = f32[16,48,128]{2,1,0:T(8,128)S(1)} async-done(((f32[16,48,128]{2,1,0:T(8,128)}), f32[16,48,128]{2,1,0:T(8,128)S(1)}, u32[]{:S(2)}, u32[]{:S(2)}) %all-to-all-start.1) | async-done | bytes 393248 | tf_op jit(solution)/shard_map/all_to_all | solution.py:429
  118.7 0.0 copy-start.1
  118.7 2.1 %copy-done.1 = f32[7,22,24,256]{3,2,1,0:T(8,128)S(1)} copy-done((f32[7,22,24,256]{3,2,1,0:T(8,128)S(1)}, f32[7,22,24,256]{3,2,1,0:T(8,128)}, u32[]{:S(2)}) %copy-start.1) | copy-done | bytes 3784728
  120.8 9.7 %shard_map.33 = f32[2,16,16,128]{3,2,1,0:T(8,128)} custom-call(s32[3]{0:T(128)S(1)} %pad_add_fusion.index, f32[16,48,128]{2,1,0:T(8,128)S(1)} %all-to-all-done.1.parts3, f32[5,12,32,128]{3,2,1,0:T(8,128)S(1)} %get-tuple-element.17.a, f32[7,16,16,128]{3,2,1,0:T(8,128)S(1)} %get-tuple-element.18.kept1, f32[7,22,24,256]{3,2,1,0:T(8,128)S(1)} %copy-done.1), custom_call_target="tpu_custom_call" | custom-call | tf_op jit(solution)/shard_map/pallas_call | solution.py:399
  (11 shorter events, 0.2 us)
Async XLA Ops:
  1.9 7.0 %collective-permute-start = (f32[3,16,4,128]{3,2,1,0:T(4,128)S(1)}, f32[3,16,4,128]{3,2,1,0:T(4,128)S(1)}, u32[]{:S(2)}, u32[]{:S(2)}) collective-permute-start(f32[3,16,4,128]{3,2,1,0:T(4,128)S(1)} %get-tuple-element.22), channel_id=1, source_target_pairs={{0,4},{4,8},{8,12},{12,16},{16,20},{20,24},{24,28},{1,5},{5,9},{9,... | collective-permute-start | bytes 294920 | tf_op jit(solution)/shard_map/ppermute | solution.py:413
  6.7 6.0 %collective-permute-start.1 = (f32[3,16,4,128]{3,2,1,0:T(4,128)S(1)}, f32[3,16,4,128]{3,2,1,0:T(4,128)S(1)}, u32[]{:S(2)}, u32[]{:S(2)}) collective-permute-start(f32[3,16,4,128]{3,2,1,0:T(4,128)S(1)} %get-tuple-element.21), channel_id=1, source_target_pairs={{4,0},{8,4},{12,8},{16,12},{20,16},{24,20},{28,24},{5,1},{9,5},{13... | collective-permute-start | bytes 294920 | tf_op jit(solution)/shard_map/ppermute | solution.py:413
  12.7 8.7 %collective-permute-start.3 = (f32[3,3,24,128]{3,2,1,0:T(8,128)S(1)}, f32[3,3,24,128]{3,2,1,0:T(8,128)S(1)}, u32[]{:S(2)}, u32[]{:S(2)}) collective-permute-start(f32[3,3,24,128]{3,2,1,0:T(8,128)S(1)} %pad_maximum_fusion.2), channel_id=1, source_target_pairs={{32,0},{64,32},{96,64},{128,96},{160,128},{192,160},{224,192},{256... | collective-permute-start | bytes 331784 | tf_op jit(solution)/shard_map/ppermute | solution.py:413
  18.5 3.7 %collective-permute-start.2 = (f32[3,3,24,128]{3,2,1,0:T(8,128)S(1)}, f32[3,3,24,128]{3,2,1,0:T(8,128)S(1)}, u32[]{:S(2)}, u32[]{:S(2)}) collective-permute-start(f32[3,3,24,128]{3,2,1,0:T(8,128)S(1)} %pad_maximum_fusion.1), channel_id=1, source_target_pairs={{0,32},{32,64},{64,96},{96,128},{128,160},{160,192},{192,224},{224... | collective-permute-start | bytes 331784 | tf_op jit(solution)/shard_map/ppermute | solution.py:413
  23.0 4.1 %collective-permute-start.4 = (f32[16,1584]{1,0:T(8,128)S(1)}, f32[16,1584]{1,0:T(8,128)S(1)}, u32[]{:S(2)}, u32[]{:S(2)}) collective-permute-start(f32[16,1584]{1,0:T(8,128)S(1)} %get-tuple-element.13), channel_id=1, source_target_pairs={{0,1},{1,2},{2,3},{4,5},{5,6},{6,7},{8,9},{9,10},{10,11},{12,13},{... | collective-permute-start | bytes 304136 | tf_op jit(solution)/shard_map/ppermute | solution.py:413
  25.3 5.9 %collective-permute-start.5 = (f32[16,1584]{1,0:T(8,128)S(1)}, f32[16,1584]{1,0:T(8,128)S(1)}, u32[]{:S(2)}, u32[]{:S(2)}) collective-permute-start(f32[16,1584]{1,0:T(8,128)S(1)} %get-tuple-element.14), channel_id=1, source_target_pairs={{1,0},{2,1},{3,2},{5,4},{6,5},{7,6},{9,8},{10,9},{11,10},{13,12},{... | collective-permute-start | bytes 304136 | tf_op jit(solution)/shard_map/ppermute | solution.py:413
  35.3 5.3 %collective-permute-start.6 = (f32[3,8,4,128]{3,2,1,0:T(4,128)S(1)}, f32[3,8,4,128]{3,2,1,0:T(4,128)S(1)}, u32[]{:S(2)}, u32[]{:S(2)}) collective-permute-start(f32[3,8,4,128]{3,2,1,0:T(4,128)S(1)} %get-tuple-element.26), channel_id=1, source_target_pairs={{0,4},{4,8},{8,12},{12,16},{16,20},{20,24},{24,28},{1,5},{5,9},{9,... | collective-permute-start | bytes 147464 | tf_op jit(solution)/shard_map/ppermute | solution.py:413
  39.4 6.7 %collective-permute-start.7 = (f32[3,8,4,128]{3,2,1,0:T(4,128)S(1)}, f32[3,8,4,128]{3,2,1,0:T(4,128)S(1)}, u32[]{:S(2)}, u32[]{:S(2)}) collective-permute-start(f32[3,8,4,128]{3,2,1,0:T(4,128)S(1)} %get-tuple-element.25), channel_id=1, source_target_pairs={{4,0},{8,4},{12,8},{16,12},{20,16},{24,20},{28,24},{5,1},{9,5},{13... | collective-permute-start | bytes 147464 | tf_op jit(solution)/shard_map/ppermute | solution.py:413
  46.1 8.7 %collective-permute-start.9 = (f32[3,4,16,128]{3,2,1,0:T(8,128)S(1)}, f32[3,4,16,128]{3,2,1,0:T(8,128)S(1)}, u32[]{:S(2)}, u32[]{:S(2)}) collective-permute-start(f32[3,4,16,128]{3,2,1,0:T(8,128)S(1)} %pad_maximum_fusion.4), channel_id=1, source_target_pairs={{32,0},{64,32},{96,64},{128,96},{160,128},{192,160},{224,192},{256... | collective-permute-start | bytes 294920 | tf_op jit(solution)/shard_map/ppermute | solution.py:413
  49.3 6.8 %collective-permute-start.8 = (f32[3,4,16,128]{3,2,1,0:T(8,128)S(1)}, f32[3,4,16,128]{3,2,1,0:T(8,128)S(1)}, u32[]{:S(2)}, u32[]{:S(2)}) collective-permute-start(f32[3,4,16,128]{3,2,1,0:T(8,128)S(1)} %pad_maximum_fusion.3), channel_id=1, source_target_pairs={{0,32},{32,64},{64,96},{96,128},{128,160},{160,192},{192,224},{224... | collective-permute-start | bytes 294920 | tf_op jit(solution)/shard_map/ppermute | solution.py:413
  78.2 10.0 %collective-permute-start.10 = (f32[32,5,4,128]{3,2,1,0:T(4,128)S(1)}, f32[32,5,4,128]{3,2,1,0:T(4,128)S(1)}, u32[]{:S(2)}, u32[]{:S(2)}) collective-permute-start(f32[32,5,4,128]{3,2,1,0:T(4,128)S(1)} %all_to_all.10.own), channel_id=1, source_target_pairs={{0,32},{32,64},{64,96},{96,128},{128,160},{160,192},{192,224},{224... | collective-permute-start | bytes 983048 | tf_op jit(solution)/shard_map/ppermute | solution.py:413
  84.2 8.4 %collective-permute-start.11 = (f32[32,5,4,128]{3,2,1,0:T(4,128)S(1)}, f32[32,5,4,128]{3,2,1,0:T(4,128)S(1)}, u32[]{:S(2)}, u32[]{:S(2)}) collective-permute-start(f32[32,5,4,128]{3,2,1,0:T(4,128)S(1)} %all_to_all.10.own), channel_id=1, source_target_pairs={{32,0},{64,32},{96,64},{128,96},{160,128},{192,160},{224,192},{256... | collective-permute-start | bytes 983048 | tf_op jit(solution)/shard_map/ppermute | solution.py:413
  95.6 23.2 %all-to-all-start.1 = ((f32[16,48,128]{2,1,0:T(8,128)}), f32[16,48,128]{2,1,0:T(8,128)S(1)}, u32[]{:S(2)}, u32[]{:S(2)}) async-start(f32[16,48,128]{2,1,0:T(8,128)} %broadcast_in_dim.15), calls=%async_computation.1 | async-start | bytes 786432 | tf_op jit(solution)/shard_map/all_to_all | solution.py:429
  106.9 1.8 %copy-start = (f32[7,22,24,256]{3,2,1,0:T(8,128)}, f32[7,22,24,256]{3,2,1,0:T(8,128)S(1)}, u32[]{:S(2)}) copy-start(f32[7,22,24,256]{3,2,1,0:T(8,128)S(1)} %shard_map.32.kept0) | copy-start | bytes 11354116
  118.7 2.1 %copy-start.1 = (f32[7,22,24,256]{3,2,1,0:T(8,128)S(1)}, f32[7,22,24,256]{3,2,1,0:T(8,128)}, u32[]{:S(2)}) copy-start(f32[7,22,24,256]{3,2,1,0:T(8,128)} %copy-done) | copy-start | bytes 11354116

commit v3 on v2

--- a/solution.py
+++ b/solution.py
@@ -10,12 +10,14 @@
 F32, BF16 = jnp.float32, jnp.bfloat16
 WAVE = 0.0625
 DIAG_I = 0.5 * WAVE
-MOST = (2, 7, 5, 8, 16)
+MOST = (2, 5, 6, 8, 16)
 
 X0, Y0, L0 = 22, 24, 256
-HZ = 10
+HZ = 14
+X1D, Y1D = 20, 24
 X1, Y1, L1 = 16, 16, 128
-X2, Y2 = 12, 32
+X2D, Y2 = 8, 16
+X2 = 12
 X3, Y3, PAD3 = 32, 16, 4
 X4, Y4 = 16, 8
 
@@ -66,13 +68,15 @@
     return (north + south) + (upper + lower)
 
 
-def balance(g_r, g_i, mach, v, i, level, ymask, zmask):
+def balance(source, mach, v, i, level, ymask, zmask):
     axial, advect, diagonal = coefficients(mach, level)
     scale = 0.25**level
     c_r, c_i = v[0, i], v[1, i]
     e_r, w_r, e_i, w_i = v[0, i + 1], v[0, i - 1], v[1, i + 1], v[1, i - 1]
-    t_r = g_r + axial * (e_r + w_r) - advect * (e_i - w_i)
-    t_i = g_i + axial * (e_i + w_i) + advect * (e_r - w_r)
+    t_r = axial * (e_r + w_r) - advect * (e_i - w_i)
+    t_i = axial * (e_i + w_i) + advect * (e_r - w_r)
+    if source is not None:
+        t_r, t_i = t_r + source[0], t_i + source[1]
     return (
         t_r + scale * transverse(c_r, ymask, zmask),
         t_i + scale * transverse(c_i, ymask, zmask),
@@ -114,8 +118,18 @@
 def relax_loop(lo, count, g, hd, v, write, level, ymask=False, zmask=False):
     def compute(j):
         i = lo + j
-        t_r, t_i, c_r, c_i, _ = balance(g[0, i], g[1, i], g[2, i], v, i, level, ymask, zmask)
+        t_r, t_i, c_r, c_i, _ = balance((g[0, i], g[1, i]), g[2, i], v, i, level, ymask, zmask)
         h_r, h_i = hd[0, i], hd[1, i]
+        return 0.5 * c_r + (h_r * t_r - h_i * t_i), 0.5 * c_i + (h_r * t_i + h_i * t_r)
+
+    blocks(count, MOST[level], compute, lambda j, value: write(j, lo + j, *value))
+
+
+def free_loop(lo, count, coef, v, write, level):
+    def compute(j):
+        i = lo + j
+        t_r, t_i, c_r, c_i, _ = balance(None, coef[0, i - 2], v, i, level, False, False)
+        h_r, h_i = coef[1, i - 2], coef[2, i - 2]
         return 0.5 * c_r + (h_r * t_r - h_i * t_i), 0.5 * c_i + (h_r * t_i + h_i * t_r)
 
     blocks(count, MOST[level], compute, lambda j, value: write(j, lo + j, *value))
@@ -129,7 +143,7 @@
 
 
 def residual(g, v, i, level, ymask=False, zmask=False):
-    t_r, t_i, c_r, c_i, d = balance(g[0, i], g[1, i], g[2, i], v, i, level, ymask, zmask)
+    t_r, t_i, c_r, c_i, d = balance((g[0, i], g[1, i]), g[2, i], v, i, level, ymask, zmask)
     return t_r - (d * c_r - DIAG_I * c_i), t_i - (d * c_i + DIAG_I * c_r)
 
 
@@ -155,23 +169,19 @@
 
 
 def assemble(own, ylo, yhi, xlo, xhi, f):
-    count, rows, hx = own.shape[1], own.shape[2], xlo.shape[1]
+    count, rows, hx, hy = own.shape[1], own.shape[2], xlo.shape[1], ylo.shape[2]
     for c in range(3):
         f[c, 0:hx] = xlo[c]
-        f[c, hx : hx + count, 0:4] = ylo[c]
-        f[c, hx : hx + count, 4 : 4 + rows] = own[c]
-        f[c, hx : hx + count, 4 + rows :] = yhi[c]
+        f[c, hx : hx + count, 0:hy] = ylo[c]
+        f[c, hx : hx + count, hy : hy + rows] = own[c]
+        f[c, hx : hx + count, hy + rows :] = yhi[c]
         f[c, hx + count :] = xhi[c]
-
-
-def views(kept):
-    return kept.at[0:3], kept.at[3:5], kept.at[5:7]
 
 
 def gather0_kernel(own, ylo, yhi, xlo, xhi, f, low_lanes, high_lanes):
     assemble(own, ylo, yhi, xlo, xhi, f)
     parts = split(f[...].reshape(-1, 128))
-    for out, start in ((low_lanes, 0), (high_lanes, 118)):
+    for out, start in ((low_lanes, 0), (high_lanes, 128 - HZ)):
         edge = matrix(16, 128, lambda r, l: (r < HZ) & (l == start + r))
         dims = (((1,), (1,)), ((), ()))
         terms = [lax.dot_general(edge, p, dims, preferred_element_type=F32) for p in parts]
@@ -180,7 +190,7 @@
 
 def smooth0(f, lower, upper, g, hd, v2, v1):
     both = jnp.concatenate([upper[...], lower[...]], axis=0)
-    place = matrix(32, 128, lambda r, l: ((r < HZ) & (l == r)) | ((r >= 16) & (l == r + 102)))
+    place = matrix(32, 128, lambda r, l: ((r < HZ) & (l == r)) | ((r >= 16) & (l == r + 112 - HZ)))
     tail = select(both, place, (((0,), (0,)), ((), ())))
     g[:, :, :, 0:128] = f[...]
     g[:, :, :, 128:256] = tail.reshape(3, X0, Y0, 128)
@@ -188,8 +198,16 @@
     relax_loop(1, X0 - 2, g, hd, v1, writer(v2), 0)
 
 
-def keep0_kernel(f, lower, upper, kept, v1):
-    smooth0(f, lower, upper, *views(kept), v1)
+def keep0_kernel(f, lower, upper, base, coef, g, hd, v2, v1):
+    smooth0(f, lower, upper, g, hd, v2, v1)
+    coef[0] = g[2, 2:20]
+    coef[1:3] = hd[:, 2:20]
+    relax_loop(2, X0 - 4, g, hd, v2, writer(v1), 0)
+
+    def write(j, i, re, im):
+        base[0, j], base[1, j] = re[4:20, 0:128], im[4:20, 0:128]
+
+    relax_loop(3, X0 - 6, g, hd, v1, write, 0)
 
 
 def down0_kernel(f, lower, upper, coarse, g, hd, v2, v1, sums):
@@ -206,82 +224,131 @@
     rest = matrix(
         128,
         128,
-        lambda r, l: ((r < 8) & (r // 2 + 64 == l)) | ((r >= 120) & (r // 2 + 64 == l)),
+        lambda r, l: ((r < 12) | (r >= 116)) & (r // 2 + 64 == l),
         0.125,
     )
     total = select(pair_rows(sums.at[0], 384), own) + select(pair_rows(sums.at[1], 384), rest)
     coarse[...] = total.reshape(3, 8, 8, 128)
 
 
-def down1_kernel(own, ylo, yhi, xlo, xhi, kept, chunk, v1, sums, g2, hd2, va, vb):
-    g, hd, v2 = views(kept)
-    assemble(own, ylo, yhi, xlo, xhi, g)
-    first_loop(0, X1, g, hd, v1, 1)
-    relax_loop(1, X1 - 2, g, hd, v1, writer(v2), 1)
+def smooth1(halos, g, hd, v2, v1):
+    assemble(*halos, g)
+    first_loop(0, X1D, g, hd, v1, 1)
+    relax_loop(1, X1D - 2, g, hd, v1, writer(v2), 1)
+
+
+def keep1_kernel(own, ylo, yhi, xlo, xhi, base, coef, g, hd, v2, v1):
+    smooth1((own, ylo, yhi, xlo, xhi), g, hd, v2, v1)
+    coef[0] = g[2, 4:16, 4:20]
+    coef[1:3] = hd[:, 4:16, 4:20]
+    relax_loop(4, X1D - 8, g, hd, v2, writer(v1), 1)
+
+    def write(j, i, re, im):
+        base[0, j], base[1, j] = re[4:20, :], im[4:20, :]
+
+    relax_loop(5, X1D - 10, g, hd, v1, write, 1)
+
+
+def down1_kernel(own, ylo, yhi, xlo, xhi, chunk, g, hd, v2, v1, sums, g2, hd2, va, vb):
+    smooth1((own, ylo, yhi, xlo, xhi), g, hd, v2, v1)
+    sums[...] = jnp.zeros_like(sums)
 
     def store(k, parts):
         for c in range(3):
-            row = pl.multiple_of((c * 6 + k) * 16, 16)
-            sums[pl.ds(row, 16), :] = parts[c]
-
-    blocks(6, 3, lambda k: residual_pair(g, v2, 2 + 2 * k, 1), store)
+            row = pl.multiple_of((c * X2D + k) * 2 * Y2, 2 * Y2)
+            sums[pl.ds(row, Y1D), :] = parts[c]
+
+    blocks(X2D, 2, lambda k: residual_pair(g, v2, 2 + 2 * k, 1), store)
     halve = matrix(
         128,
         128,
-        lambda r, l: ((r < 66) & (r // 2 == l)) | ((r >= 124) & (r // 2 + 64 == l)),
+        lambda r, l: ((r < 68) & (r // 2 == l)) | ((r >= 124) & (r // 2 + 64 == l)),
         0.125,
     )
-    g2[...] = select(pair_rows(sums, 288), halve).reshape(3, 6, 8, 128)
-    first_loop(0, 6, g2, hd2, va, 2)
-    relax_loop(1, 4, g2, hd2, va, writer(vb), 2)
-    lane = iota((8, 128), 1) // 32
+    g2[...] = select(pair_rows(sums, 6 * X2D * Y2), halve).reshape(3, X2D, Y2, 128)
+    first_loop(0, X2D, g2, hd2, va, 2)
+    relax_loop(1, X2D - 2, g2, hd2, va, writer(vb), 2)
+    lane = iota((Y2, 128), 1) // 32
     for c in range(5):
         source = (lambda x: g2[c, x]) if c < 3 else (lambda x: vb[c - 3, x])
-        total = source(1)
+        total = source(2)
         for x in range(1, 4):
-            total = jnp.where(lane == x, pltpu.roll(source(1 + x), 32 * x, 1), total)
-        chunk[c] = total[2:6, :]
-
-
-def down2_kernel(own, left, right, a, chunk, planes, sums):
+            total = jnp.where(lane == x, pltpu.roll(source(2 + x), 32 * x, 1), total)
+        for half in range(2):
+            rows = total[4 + 2 * half : 6 + 2 * half, :]
+            chunk[:, 1 + 2 * c + half] = jnp.broadcast_to(rows, (32, 2, 128))
+    pairs = [residual_pair(g2, vb, 2 + 2 * x, 2) for x in range(2)]
+    for c in range(3):
+        for x in range(2):
+            row = (c * 2 + x) * Y2
+            sums[row : row + Y2, :] = pairs[x][c]
+    halve = matrix(128, 128, lambda r, l: (r < 32) & (r // 2 == l), 0.125)
+    small = select(pair_rows(sums, 6 * Y2), halve)
+    total = None
+    for k in range(6):
+        value = small[8 * k : 8 * k + 8, :]
+        value = pltpu.roll(value, 16 * k, 1) if k else value
+        total = value if total is None else total + value
+    chunk[:, 0] = jnp.broadcast_to(total[2:4, :], (32, 2, 128))
+
+
+def spread3_kernel(parts, chunk, planes):
+    for gz in range(4):
+        for gy in range(8):
+            planes[gz, 2 * gy : 2 * gy + 2, :] = parts[gy * 4 + gz, 0]
+    lane = iota((Y3, 128), 1) // 16
+    for c in range(3):
+        total = jnp.zeros((Y3, 128), F32)
+        for x in range(2):
+            for gz in range(4):
+                at = 4 * x + gz
+                step = (16 * (at - 2 * c - x)) % 128
+                value = planes[gz]
+                value = pltpu.roll(value, step, 1) if step else value
+                total = jnp.where(lane == at, value, total)
+        chunk[:, Y3 * c : Y3 * (c + 1), :] = jnp.broadcast_to(total, (16, Y3, 128))
+
+
+def pick2_kernel(index, parts, sheet):
+    for bz in range(3):
+        for by in range(3):
+            y, z = index[1] + (by - 1), index[2] + (bz - 1)
+            inside = (y >= 0) & (y < 8) & (z >= 0) & (z < 4)
+            at = jnp.clip(y, 0, 7) * 4 + jnp.clip(z, 0, 3)
+            factor = jnp.where(inside, 1.0, 0.0)
+            for c in range(5):
+                for half in range(2):
+                    rows = parts[at, 1 + 2 * c + half] * factor
+                    sheet[(bz * 3 + by) * 5 + c, 2 * half : 2 * half + 2, :] = rows
+
+
+def window2_kernel(west, own, east, a, planes):
     lane = iota((Y2, 128), 1) // 32
-    for p, piece in enumerate((left, own, right)):
+    planes[...] = jnp.zeros_like(planes)
+    for bx, piece in enumerate((west, own, east)):
 
         def body(c, _):
-            for gz in range(4):
-                for gy in range(8):
-                    planes[gz, 4 * gy : 4 * gy + 4, :] = piece[gy * 4 + gz, c]
+            for bz in range(3):
+                for by in range(3):
+                    planes[bz, 4 * by : 4 * by + 4, :] = piece[(bz * 3 + by) * 5 + c]
             for x in range(4):
-                total = None
-                for gz in range(4):
-                    value = planes[gz]
-                    if gz != x:
-                        value = pltpu.roll(value, (32 * (gz - x)) % 128, 1)
-                    total = value if total is None else jnp.where(lane == gz, value, total)
-                a[c, 4 * p + x] = total
+                total = jnp.zeros((Y2, 128), F32)
+                for bz, group in enumerate((3, 0, 1)):
+                    step = (32 * (group - x)) % 128
+                    value = planes[bz]
+                    value = pltpu.roll(value, step, 1) if step else value
+                    total = jnp.where(lane == group, value, total)
+                a[c, 4 * bx + x] = total
             return 0
 
         lax.fori_loop(0, 5, body, 0)
-    v = a.at[3:5]
-    for k in range(2):
-        parts = residual_pair(a, v, 4 + 2 * k, 2, True, True)
-        for c in range(3):
-            sums[k, Y2 * c : Y2 * (c + 1), :] = parts[c]
-    total = None
-    for k in range(2):
-        halve = matrix(128, 128, lambda r, l: r // 2 + 64 * k == l, 0.125)
-        term = select(pair_rows(sums.at[k], 3 * Y2), halve)
-        total = term if total is None else total + term
-    chunk[...] = total
 
 
 def up_kernel(
-    index, parts3, a, kept1, kept0, out,
+    index, parts3, a, base1, coef1, base0, coef0, out,
     g3, hd3, va3, vb3, s3, g4, hd4, va4, vb4, t4, w3, t3, hd2, va2, vb2, w2, t2, va1, vb1, t1, va0, vb0,
 ):
     gx, gy, gz = index[0], index[1], index[2]
-    g1, hd1, v21 = views(kept1)
-    g0, hd0, v20 = views(kept0)
     zero3 = jnp.zeros((Y3, 128), F32)
     for ref in (g3, hd3, va3, vb3):
         for c in range(ref.shape[0]):
@@ -331,11 +398,19 @@
     base = PAD3 + 2 * gx
     relax_loop(base - 3, 8, g3, hd3, vb3, writer(va3), 3, True)
 
+    w3[...] = jnp.zeros_like(w3)
+
     def write3(j, i, re, im):
-        w3[0, j], w3[1, j] = re, im
+        w3[0, j, 8 : 8 + Y3], w3[1, j, 8 : 8 + Y3] = re, im
 
     relax_loop(base - 2, 6, g3, hd3, va3, write3, 3, True)
-    twin_rows(t3, select(w3[...].reshape(2 * 6 * Y3, 128), double))
+    rows = w3[:, :, pl.ds(2 * gy + 6, 8), :].reshape(2 * 6 * 8, 128)
+
+    def place2(r, l):
+        at = jnp.where(l < 64, l, l - 128)
+        return r == 16 * gz + (at + 128) // 2 - 64
+
+    twin_rows(t3, select(rows, matrix(128, 128, place2)))
 
     def start2(i, _):
         hd2[0, i], hd2[1, i] = half_inverse(a[2, i], 2)
@@ -345,30 +420,28 @@
         return 0
 
     lax.fori_loop(0, X2, start2, 0)
-    relax_loop(1, X2 - 2, a, hd2, va2, writer(vb2), 2, True, True)
-    w2[...] = jnp.zeros_like(w2)
+    relax_loop(1, X2 - 2, a, hd2, va2, writer(vb2), 2)
 
     def write2(j, i, re, im):
-        w2[0, j, 8 : 8 + Y2], w2[1, j, 8 : 8 + Y2] = re, im
-
-    relax_loop(2, X2 - 4, a, hd2, vb2, write2, 2, True, True)
-    rows = w2[:, :, pl.ds(4 * gy + 6, 8), :].reshape(2 * 8 * 8, 128)
-
-    def place1(r, l):
-        at = jnp.where(l < 96, l, l - 128)
-        return r == 32 * gz + (at + 128) // 2 - 64
-
-    twin_rows(t2, select(rows, matrix(128, 128, place1)))
+        w2[0, j], w2[1, j] = re, im
+
+    relax_loop(2, X2 - 4, a, hd2, vb2, write2, 2)
+    double = matrix(128, 128, lambda r, l: jnp.where(l < 96, l // 2, l // 2 + 64) == r)
+    twin_rows(t2, select(w2[:, :, 2:10, :].reshape(2 * 8 * 8, 128), double))
 
     def start1(i, _):
         for c in range(2):
             row = pl.multiple_of((c * 8 + i // 2) * Y1, Y1)
-            va1[c, i] = v21[c, i] + t2[pl.ds(row, Y1), :]
+            va1[c, i] = t2[pl.ds(row, Y1), :]
         return 0
 
     lax.fori_loop(1, X1 - 1, start1, 0)
-    relax_loop(2, X1 - 4, g1, hd1, va1, writer(vb1), 1)
-    relax_loop(3, X1 - 6, g1, hd1, vb1, writer(va1), 1)
+    free_loop(2, X1 - 4, coef1, va1, writer(vb1), 1)
+
+    def write1(j, i, re, im):
+        va1[0, i], va1[1, i] = base1[0, j] + re, base1[1, j] + im
+
+    free_loop(3, X1 - 6, coef1, vb1, write1, 1)
     own = va1[:, 3:13].reshape(2 * 10 * Y1, 128)
     for half in range(2):
         place = matrix(128, 128, lambda r, l: r == (l + 128 * half) // 2)
@@ -381,16 +454,17 @@
                 lanes = slice(128 * half, 128 * half + 128)
                 value = t1[half, pl.ds(row, Y0), :]
                 for i in range(2):
-                    va0[c, 2 * k + 1 + i, :, lanes] = v20[c, 2 * k + 1 + i, :, lanes] + value
+                    va0[c, 2 * k + 1 + i, :, lanes] = value
         return 0
 
     lax.fori_loop(0, 10, start0, 0)
-    relax_loop(2, X0 - 4, g0, hd0, va0, writer(vb0), 0)
+    free_loop(2, X0 - 4, coef0, va0, writer(vb0), 0)
 
     def write0(j, i, re, im):
-        out[0, j], out[1, j] = re[4:20, 0:128], im[4:20, 0:128]
-
-    relax_loop(3, X0 - 6, g0, hd0, vb0, write0, 0)
+        out[0, j] = base0[0, j] + re[4:20, 0:128]
+        out[1, j] = base0[1, j] + im[4:20, 0:128]
+
+    free_loop(3, X0 - 6, coef0, vb0, write0, 0)
 
 
 def call(kernel, outs, scratch, *args, limit=12, memory="", cost=None):
@@ -413,10 +487,10 @@
     return lax.ppermute(block, axis, pairs)
 
 
-def halos(own, hx):
+def halos(own, hx, hy):
     count, rows = own.shape[1], own.shape[2]
-    ylo = shift(own[:, :, rows - 4 :], "gy", 1)
-    yhi = shift(own[:, :, :4], "gy", -1)
+    ylo = shift(own[:, :, rows - hy :], "gy", 1)
+    yhi = shift(own[:, :, :hy], "gy", -1)
 
     def edge(at):
         return jnp.concatenate([x[:, at : at + hx] for x in (ylo, own, yhi)], axis=2)
@@ -424,51 +498,67 @@
     return own, ylo, yhi, shift(edge(count - hx), "gx", 1), shift(edge(0), "gx", -1)
 
 
-def everyone(block, axes):
-    count = lax.axis_size(axes)
-    return lax.all_to_all(jnp.broadcast_to(block, (count,) + block.shape), axes, 0, 0)
+def around(block, axis):
+    return shift(block, axis, 1), shift(block, axis, -1)
 
 
 def shards(source_field, mach_number):
     own0 = jnp.concatenate([source_field, mach_number.astype(F32)[None]], axis=0)
     flat = (16, 3 * X0 * Y0)
-    f0, low, high = call(gather0_kernel, [(3, X0, Y0, 128), flat, flat], [], *halos(own0, 3))
+    f0, low, high = call(gather0_kernel, [(3, X0, Y0, 128), flat, flat], [], *halos(own0, 3, 4))
     full0, full1 = (X0, Y0, L0), (X1, Y1, L1)
     block0 = (f0, shift(high, "gz", 1), shift(low, "gz", -1))
     smoothed0 = [(3,) + full0] + [(2,) + full0] * 3
     (own1,) = call(
         down0_kernel, [(3, 8, 8, 128)], smoothed0 + [(2, 384, 128)], *block0
     )
-    kept1, chunk2 = call(
+    wide1, wide2 = (X1D, Y1D, L1), (X2D, Y2, 128)
+    block1 = halos(own1, 6, 8)
+    smoothed1 = [(3,) + wide1] + [(2,) + wide1] * 3
+    (chunk2,) = call(
         down1_kernel,
-        [(7,) + full1, (5, 4, 128)],
-        [(2,) + full1, (288, 128), (3, 6, 8, 128)] + [(2, 6, 8, 128)] * 3,
-        *halos(own1, 4),
-    )
-    own2 = everyone(chunk2, ("gy", "gz"))
-    a, chunk3 = call(
-        down2_kernel,
-        [(5, X2, Y2, 128), (48, 128)],
-        [(4, Y2, 128), (2, 96, 128)],
-        own2, shift(own2, "gx", 1), shift(own2, "gx", -1),
-    )
-    parts3 = everyone(chunk3, "gx")
-    (kept0,) = call(keep0_kernel, [(7,) + full0], [(2,) + full0], *block0, cost=(60 << 20, 8 << 20))
+        [(32, 11, 2, 128)],
+        smoothed1 + [(6 * X2D * Y2, 128), (3,) + wide2] + [(2,) + wide2] * 3,
+        *block1,
+    )
+    parts2 = lax.all_to_all(chunk2, ("gy", "gz"), 0, 0)
+    base0, coef0 = call(
+        keep0_kernel,
+        [(2, 16, 16, 128), (3, 18, Y0, L0)],
+        smoothed0,
+        *block0,
+        cost=(60 << 20, 8 << 20),
+    )
+    base1, coef1 = call(
+        keep1_kernel,
+        [(2, 10, Y1, 128), (3, 12, Y1, 128)],
+        smoothed1,
+        *block1,
+        cost=(8 << 20, 1 << 20),
+    )
+    parts2, *kept = lax.optimization_barrier((parts2, base1, coef1, base0, coef0))
+    (chunk3,) = call(spread3_kernel, [(16, 48, 128)], [(4, Y3, 128)], parts2)
+    parts3 = lax.all_to_all(chunk3, "gx", 0, 0)
     index = jnp.stack([lax.axis_index(n) for n in ("gx", "gy", "gz")]).astype(jnp.int32)
+    (sheet,) = call(pick2_kernel, [(45, 4, 128)], [], index, parts2, memory="svv")
+    west, east = around(sheet, "gx")
+    (a,) = call(
+        window2_kernel, [(5, X2, Y2, 128)], [(3, Y2, 128)], west, sheet, east, cost=(4 << 20, 1 << 20)
+    )
     wide3 = (X3 + 2 * PAD3, Y3, 128)
     wide4 = (X4 + 2, Y4, 128)
     scratch = [(3,) + wide3, (2,) + wide3, (2,) + wide3, (2,) + wide3, (3 * X4 * Y3, 128)]
     scratch += [(3,) + wide4, (2,) + wide4, (2,) + wide4, (2,) + wide4, (2 * X4 * Y3, 128)]
-    scratch += [(2, 6, Y3, 128), (2 * 6 * Y2, 128)] + [(2, X2, Y2, 128)] * 3
-    scratch += [(2, 8, Y2 + 16, 128), (2 * 8 * Y1, 128), (2,) + full1, (2,) + full1]
+    scratch += [(2, 6, Y3 + 16, 128), (2 * 6 * Y2, 128)] + [(2, X2, Y2, 128)] * 3
+    scratch += [(2, 8, Y2, 128), (2 * 8 * Y1, 128), (2,) + full1, (2,) + full1]
     scratch += [(2, 2 * 10 * 32, 128), (2,) + full0, (2,) + full0]
     return call(
         up_kernel,
         [(2, 16, 16, 128)],
         scratch,
-        index, parts3, a, kept1, kept0,
+        index, parts3, a, *kept,
         limit=16,
-        memory="svvvvv",
+        memory="svvvvvvv",
     )[0]
 
 

time: 131 us -> 119 us (0.908)
  blocking collectives: 20.9 us -> 0 us
  starting transfers between devices: 47.5 us -> 56.7 us
  Pallas kernels: 20.6 us -> 26.5 us
  local copies, waits for them, and re-layouts: 4.75 us -> 1.45 us
  waiting for transfers between devices: 32.6 us -> 30.6 us
    all_to_all x1 -> x0, blocking collectives: 20.9 us -> none  [everyone(): lax.all_to_all(jnp.broadcast_to(block, (count,) + block.shape), axes, 0, 0)]
    all_to_all x1 -> x2, starting transfers between devices: 8.63 us -> 21.1 us  [the longest x1 12 us: shards(): parts3 = lax.all_to_all(chunk3, 'gx', 0, 0)]
    pallas_call x6 -> x9, Pallas kernels: 20.6 us -> 26.5 us  [call(): pl.pallas_call(kernel, out_shape=[jax.ShapeDtypeStruct(s, F32) for s in o...]
    all_to_all x1 -> x2, waiting for transfers between devices: 9.99 us -> 4.66 us  [the longest x1 3.78 us: shards(): parts2 = lax.all_to_all(chunk2, ('gy', 'gz'), 0, 0)]
    ppermute x12, starting transfers between devices: 38.9 us -> 35.6 us  [shift(): return lax.ppermute(block, axis, pairs)]
    ppermute x12, waiting for transfers between devices: 22.6 us -> 25.9 us  [shift(): return lax.ppermute(block, axis, pairs)]
    unnamed x4 -> x10, local copies, waits for them, and re-layouts: 3.88 us -> 1.41 us
  transfers between devices with their start and end apart: 13 -> 14, of which waited for: 10 -> 12; matrix products, arithmetic and copies ran while one was open for 2% -> 1% of each run, Pallas kernels for 2% -> 7%
where the time goes in v3:
time: 119 us; the launch traced here: 118 us
  starting transfers between devices  56.7 us (48%)
  waiting for transfers between devices  30.6 us (26%)
  Pallas kernels  26.5 us (22%)
  other arithmetic  2.93 us (2%)
  local copies, waits for them, and re-layouts  1.45 us (1%)
    ppermute x12, starting transfers between devices, shift(): return lax.ppermute(block, axis, pairs)  35.6 us
    pallas_call x9, Pallas kernels, call(): pl.pallas_call(kernel, out_shape=[jax.ShapeDtypeStruct(s, F32) for s in o...  26.5 us
    ppermute x12, waiting for transfers between devices, shift(): return lax.ppermute(block, axis, pairs)  25.9 us
    all_to_all x1, starting transfers between devices, shards(): parts3 = lax.all_to_all(chunk3, 'gx', 0, 0)  12 us
    all_to_all x1, starting transfers between devices, shards(): parts2 = lax.all_to_all(chunk2, ('gy', 'gz'), 0, 0)  9.14 us
    all_to_all x1, waiting for transfers between devices, shards(): parts2 = lax.all_to_all(chunk2, ('gy', 'gz'), 0, 0)  3.78 us
  transfers between devices with their start and end apart: 14, of which 12 were waited for; matrix products, arithmetic and copies ran while one was open for 1% of the time, Pallas kernels for 7%

profile of v3, /device:TPU:1, one launch (start us, length us, event | category | flops | bytes accessed | tf_op | source)
XLA Modules:
  0.0 118.4 jit_solution(14410046702125594370)
XLA Ops:
  0.0 0.9 bitcast_convert_fusion
  0.9 1.0 fusion.1
  1.9 4.8 %collective-permute-start = (f32[3,16,4,128]{3,2,1,0:T(4,128)S(1)}, f32[3,16,4,128]{3,2,1,0:T(4,128)S(1)}, u32[]{:S(2)}, u32[]{:S(2)}) collective-permute-start(f32[3,16,4,128]{3,2,1,0:T(4,128)S(1)} %get-tuple-element.32), channel_id=1, source_target_pairs={{0,4},{4,8},{8,12},{12,16},{16,20},{20,24},{24,28},{1,5},{5,9},{9,... | collective-permute-start | bytes 294920 | tf_op jit(solution)/shard_map/ppermute | solution.py:487
  6.7 1.3 %collective-permute-start.1 = (f32[3,16,4,128]{3,2,1,0:T(4,128)S(1)}, f32[3,16,4,128]{3,2,1,0:T(4,128)S(1)}, u32[]{:S(2)}, u32[]{:S(2)}) collective-permute-start(f32[3,16,4,128]{3,2,1,0:T(4,128)S(1)} %get-tuple-element.31), channel_id=1, source_target_pairs={{4,0},{8,4},{12,8},{16,12},{20,16},{24,20},{28,24},{5,1},{9,5},{13... | collective-permute-start | bytes 294920 | tf_op jit(solution)/shard_map/ppermute | solution.py:487
  8.0 0.8 fusion.3
  8.9 0.0 collective-permute-done.ylo
  8.9 3.8 %collective-permute-done.1.yhi = f32[3,16,4,128]{3,2,1,0:T(4,128)S(1)} collective-permute-done((f32[3,16,4,128]{3,2,1,0:T(4,128)S(1)}, f32[3,16,4,128]{3,2,1,0:T(4,128)S(1)}, u32[]{:S(2)}, u32[]{:S(2)}) %collective-permute-start.1) | collective-permute-done | bytes 98336 | tf_op jit(solution)/shard_map/ppermute | solution.py:487
  12.8 5.8 %collective-permute-start.3 = (f32[3,3,24,128]{3,2,1,0:T(8,128)S(1)}, f32[3,3,24,128]{3,2,1,0:T(8,128)S(1)}, u32[]{:S(2)}, u32[]{:S(2)}) collective-permute-start(f32[3,3,24,128]{3,2,1,0:T(8,128)S(1)} %pad_maximum_fusion.4), channel_id=1, source_target_pairs={{32,0},{64,32},{96,64},{128,96},{160,128},{192,160},{224,192},{256... | collective-permute-start | bytes 331784 | tf_op jit(solution)/shard_map/ppermute | solution.py:487
  18.6 1.9 %collective-permute-start.2 = (f32[3,3,24,128]{3,2,1,0:T(8,128)S(1)}, f32[3,3,24,128]{3,2,1,0:T(8,128)S(1)}, u32[]{:S(2)}, u32[]{:S(2)}) collective-permute-start(f32[3,3,24,128]{3,2,1,0:T(8,128)S(1)} %pad_maximum_fusion.3), channel_id=1, source_target_pairs={{0,32},{32,64},{64,96},{96,128},{128,160},{160,192},{192,224},{224... | collective-permute-start | bytes 331784 | tf_op jit(solution)/shard_map/ppermute | solution.py:487
  20.5 0.0 copy-done.4
  20.5 0.0 collective-permute-done.3.xhi
  20.6 1.7 %collective-permute-done.2.xlo = f32[3,3,24,128]{3,2,1,0:T(8,128)S(1)} collective-permute-done((f32[3,3,24,128]{3,2,1,0:T(8,128)S(1)}, f32[3,3,24,128]{3,2,1,0:T(8,128)S(1)}, u32[]{:S(2)}, u32[]{:S(2)}) %collective-permute-start.2) | collective-permute-done | bytes 110624 | tf_op jit(solution)/shard_map/ppermute | solution.py:487
  22.2 0.8 shard_map.28
  23.1 2.3 %collective-permute-start.4 = (f32[16,1584]{1,0:T(8,128)S(1)}, f32[16,1584]{1,0:T(8,128)S(1)}, u32[]{:S(2)}, u32[]{:S(2)}) collective-permute-start(f32[16,1584]{1,0:T(8,128)S(1)} %get-tuple-element.18), channel_id=1, source_target_pairs={{0,1},{1,2},{2,3},{4,5},{5,6},{6,7},{8,9},{9,10},{10,11},{12,13},{... | collective-permute-start | bytes 304136 | tf_op jit(solution)/shard_map/ppermute | solution.py:487
  25.3 1.3 %collective-permute-start.5 = (f32[16,1584]{1,0:T(8,128)S(1)}, f32[16,1584]{1,0:T(8,128)S(1)}, u32[]{:S(2)}, u32[]{:S(2)}) collective-permute-start(f32[16,1584]{1,0:T(8,128)S(1)} %get-tuple-element.19), channel_id=1, source_target_pairs={{1,0},{2,1},{3,2},{5,4},{6,5},{7,6},{9,8},{10,9},{11,10},{13,12},{... | collective-permute-start | bytes 304136 | tf_op jit(solution)/shard_map/ppermute | solution.py:487
  26.6 0.4 collective-permute-done.4.lower
  27.1 4.1 %collective-permute-done.5.upper = f32[16,1584]{1,0:T(8,128)S(1)} collective-permute-done((f32[16,1584]{1,0:T(8,128)S(1)}, f32[16,1584]{1,0:T(8,128)S(1)}, u32[]{:S(2)}, u32[]{:S(2)}) %collective-permute-start.5) | collective-permute-done | bytes 101408 | tf_op jit(solution)/shard_map/ppermute | solution.py:487
  31.2 4.0 %shard_map.29.own = f32[3,8,8,128]{3,2,1,0:T(8,128)S(1)} custom-call(f32[3,22,24,128]{3,2,1,0:T(8,128)S(1)} %get-tuple-element.17.f, f32[16,1584]{1,0:T(8,128)S(1)} %collective-permute-done.4.lower, f32[16,1584]{1,0:T(8,128)S(1)} %collective-permute-done.5.upper), custom_call_target="tpu_custom_call" | custom-call | tf_op jit(solution)/shard_map/pallas_call | solution.py:473
  35.2 4.0 %collective-permute-start.6 = (f32[3,8,8,128]{3,2,1,0:T(8,128)S(1)}, f32[3,8,8,128]{3,2,1,0:T(8,128)S(1)}, u32[]{:S(2)}, u32[]{:S(2)}) collective-permute-start(f32[3,8,8,128]{3,2,1,0:T(8,128)S(1)} %shard_map.29.own), channel_id=1, source_target_pairs={{0,4},{4,8},{8,12},{12,16},{16,20},{20,24},{24,28},{1,5},{5,9},{9,... | collective-permute-start | bytes 294920 | tf_op jit(solution)/shard_map/ppermute | solution.py:487
  39.2 1.3 %collective-permute-start.7 = (f32[3,8,8,128]{3,2,1,0:T(8,128)S(1)}, f32[3,8,8,128]{3,2,1,0:T(8,128)S(1)}, u32[]{:S(2)}, u32[]{:S(2)}) collective-permute-start(f32[3,8,8,128]{3,2,1,0:T(8,128)S(1)} %shard_map.29.own), channel_id=1, source_target_pairs={{4,0},{8,4},{12,8},{16,12},{20,16},{24,20},{28,24},{5,1},{9,5},{13... | collective-permute-start | bytes 294920 | tf_op jit(solution)/shard_map/ppermute | solution.py:487
  40.5 0.9 collective-permute-done.6.ylo
  41.4 6.0 %collective-permute-done.7.yhi = f32[3,8,8,128]{3,2,1,0:T(8,128)S(1)} collective-permute-done((f32[3,8,8,128]{3,2,1,0:T(8,128)S(1)}, f32[3,8,8,128]{3,2,1,0:T(8,128)S(1)}, u32[]{:S(2)}, u32[]{:S(2)}) %collective-permute-start.7) | collective-permute-done | bytes 98336 | tf_op jit(solution)/shard_map/ppermute | solution.py:487
  47.4 2.7 %collective-permute-start.9 = (f32[3,6,24,128]{3,2,1,0:T(8,128)S(1)}, f32[3,6,24,128]{3,2,1,0:T(8,128)S(1)}, u32[]{:S(2)}, u32[]{:S(2)}) collective-permute-start(f32[3,6,24,128]{3,2,1,0:T(8,128)S(1)} %pad_maximum_fusion.2), channel_id=1, source_target_pairs={{32,0},{64,32},{96,64},{128,96},{160,128},{192,160},{224,192},{256... | collective-permute-start | bytes 663560 | tf_op jit(solution)/shard_map/ppermute | solution.py:487
  50.1 4.8 %collective-permute-start.8 = (f32[3,6,24,128]{3,2,1,0:T(8,128)S(1)}, f32[3,6,24,128]{3,2,1,0:T(8,128)S(1)}, u32[]{:S(2)}, u32[]{:S(2)}) collective-permute-start(f32[3,6,24,128]{3,2,1,0:T(8,128)S(1)} %pad_maximum_fusion.1), channel_id=1, source_target_pairs={{0,32},{32,64},{64,96},{96,128},{128,160},{160,192},{192,224},{224... | collective-permute-start | bytes 663560 | tf_op jit(solution)/shard_map/ppermute | solution.py:487
  54.9 1.6 %collective-permute-done.9.xhi = f32[3,6,24,128]{3,2,1,0:T(8,128)S(1)} collective-permute-done((f32[3,6,24,128]{3,2,1,0:T(8,128)S(1)}, f32[3,6,24,128]{3,2,1,0:T(8,128)S(1)}, u32[]{:S(2)}, u32[]{:S(2)}) %collective-permute-start.9) | collective-permute-done | bytes 221216 | tf_op jit(solution)/shard_map/ppermute | solution.py:487
  56.5 1.2 %collective-permute-done.8.xlo = f32[3,6,24,128]{3,2,1,0:T(8,128)S(1)} collective-permute-done((f32[3,6,24,128]{3,2,1,0:T(8,128)S(1)}, f32[3,6,24,128]{3,2,1,0:T(8,128)S(1)}, u32[]{:S(2)}, u32[]{:S(2)}) %collective-permute-start.8) | collective-permute-done | bytes 221216 | tf_op jit(solution)/shard_map/ppermute | solution.py:487
  57.7 2.9 %shard_map.30 = f32[32,11,2,128]{3,2,1,0:T(2,128)} custom-call(f32[3,8,8,128]{3,2,1,0:T(8,128)S(1)} %shard_map.29.own, f32[3,8,8,128]{3,2,1,0:T(8,128)S(1)} %collective-permute-done.6.ylo, f32[3,8,8,128]{3,2,1,0:T(8,128)S(1)} %collective-permute-done.7.yhi, f32[3,6,24,128]{3,2,1,0:T(8,128)S(1)} %collective-permute-done.8.xlo, ...), custom_call_target="tpu_custom_call" | custom-call | tf_op jit(solution)/shard_map/pallas_call | solution.py:473
  60.7 9.1 %all-to-all-start = ((f32[32,11,2,128]{3,2,1,0:T(2,128)}), f32[32,11,2,128]{3,2,1,0:T(2,128)S(1)}, u32[]{:S(2)}, u32[]{:S(2)}) async-start(f32[32,11,2,128]{3,2,1,0:T(2,128)} %shard_map.30), calls=%async_computation | async-start | bytes 720896 | tf_op jit(solution)/shard_map/all_to_all | solution.py:524
  69.8 4.9 %shard_map.32 = (f32[2,16,16,128]{3,2,1,0:T(8,128)S(1)}, f32[3,18,24,256]{3,2,1,0:T(8,128)S(1)}) custom-call(f32[3,22,24,128]{3,2,1,0:T(8,128)S(1)} %get-tuple-element.17.f, f32[16,1584]{1,0:T(8,128)S(1)} %collective-permute-done.4.lower, f32[16,1584]{1,0:T(8,128)S(1)} %collective-permute-done.5.upper), custom_call_target="tpu_custom_call" | custom-call | flops 62914560 | bytes 8388608 | tf_op jit(solution)/shard_map/pallas_call | solution.py:473
  74.7 0.0 copy-start.2
  74.7 0.7 copy-done.2
  75.4 1.6 %shard_map.31 = (f32[2,10,16,128]{3,2,1,0:T(8,128)S(1)}, f32[3,12,16,128]{3,2,1,0:T(8,128)S(1)}) custom-call(f32[3,8,8,128]{3,2,1,0:T(8,128)S(1)} %shard_map.29.own, f32[3,8,8,128]{3,2,1,0:T(8,128)S(1)} %collective-permute-done.6.ylo, f32[3,8,8,128]{3,2,1,0:T(8,128)S(1)} %collective-permute-done.7.yhi, f32[3,6,24,128]{3,2,1,0:T(8,128)S(1)} %collective-permute-done.8.xlo, ...), custom_call_target="tpu_custom_call" | custom-call | flops 8388608 | bytes 1048576 | tf_op jit(solution)/shard_map/pallas_call | solution.py:473
  77.0 0.0 copy-start
  77.0 0.7 copy-done
  77.7 3.8 %all-to-all-done.parts = f32[32,11,2,128]{3,2,1,0:T(2,128)S(1)} async-done(((f32[32,11,2,128]{3,2,1,0:T(2,128)}), f32[32,11,2,128]{3,2,1,0:T(2,128)S(1)}, u32[]{:S(2)}, u32[]{:S(2)}) %all-to-all-start) | async-done | bytes 360480 | tf_op jit(solution)/shard_map/all_to_all | solution.py:524
  81.5 0.9 shard_map.33
  82.4 12.0 %all-to-all-start.1 = ((f32[16,48,128]{2,1,0:T(8,128)}), f32[16,48,128]{2,1,0:T(8,128)S(1)}, u32[]{:S(2)}, u32[]{:S(2)}) async-start(f32[16,48,128]{2,1,0:T(8,128)} %shard_map.33), calls=%async_computation.1 | async-start | bytes 786432 | tf_op jit(solution)/shard_map/all_to_all | solution.py:541
  94.4 0.1 pad_add_fusion.index
  94.5 0.6 shard_map.34.own
  95.1 3.5 %collective-permute-start.10 = (f32[45,4,128]{2,1,0:T(4,128)S(1)}, f32[45,4,128]{2,1,0:T(4,128)S(1)}, u32[]{:S(2)}, u32[]{:S(2)}) collective-permute-start(f32[45,4,128]{2,1,0:T(4,128)S(1)} %shard_map.34.own), channel_id=1, source_target_pairs={{0,32},{32,64},{64,96},{96,128},{128,160},{160,192},{192,224},{224... | collective-permute-start | bytes 276488 | tf_op jit(solution)/shard_map/ppermute | solution.py:487
  98.7 1.9 %collective-permute-start.11 = (f32[45,4,128]{2,1,0:T(4,128)S(1)}, f32[45,4,128]{2,1,0:T(4,128)S(1)}, u32[]{:S(2)}, u32[]{:S(2)}) collective-permute-start(f32[45,4,128]{2,1,0:T(4,128)S(1)} %shard_map.34.own), channel_id=1, source_target_pairs={{32,0},{64,32},{96,64},{128,96},{160,128},{192,160},{224,192},{256... | collective-permute-start | bytes 276488 | tf_op jit(solution)/shard_map/ppermute | solution.py:487
  100.6 2.9 %collective-permute-done.10.west = f32[45,4,128]{2,1,0:T(4,128)S(1)} collective-permute-done((f32[45,4,128]{2,1,0:T(4,128)S(1)}, f32[45,4,128]{2,1,0:T(4,128)S(1)}, u32[]{:S(2)}, u32[]{:S(2)}) %collective-permute-start.10) | collective-permute-done | bytes 92192 | tf_op jit(solution)/shard_map/ppermute | solution.py:487
  103.5 3.3 %collective-permute-done.11.east = f32[45,4,128]{2,1,0:T(4,128)S(1)} collective-permute-done((f32[45,4,128]{2,1,0:T(4,128)S(1)}, f32[45,4,128]{2,1,0:T(4,128)S(1)}, u32[]{:S(2)}, u32[]{:S(2)}) %collective-permute-start.11) | collective-permute-done | bytes 92192 | tf_op jit(solution)/shard_map/ppermute | solution.py:487
  106.7 1.4 %shard_map.35.a = f32[5,12,16,128]{3,2,1,0:T(8,128)S(1)} custom-call(f32[45,4,128]{2,1,0:T(4,128)S(1)} %collective-permute-done.10.west, f32[45,4,128]{2,1,0:T(4,128)S(1)} %shard_map.34.own, f32[45,4,128]{2,1,0:T(4,128)S(1)} %collective-permute-done.11.east), custom_call_target="tpu_custom_call" | custom-call | flops 4194304 | bytes 1048576 | tf_op jit(solution)/shard_map/pallas_call | solution.py:473
  108.1 0.9 all-to-all-done.1.parts3
  109.0 0.0 copy-done.1
  109.0 0.0 copy-done.3
  109.0 9.5 %shard_map.36 = f32[2,16,16,128]{3,2,1,0:T(8,128)} custom-call(s32[3]{0:T(128)S(1)} %pad_add_fusion.index, f32[16,48,128]{2,1,0:T(8,128)S(1)} %all-to-all-done.1.parts3, f32[5,12,16,128]{3,2,1,0:T(8,128)S(1)} %shard_map.35.a, f32[2,10,16,128]{3,2,1,0:T(8,128)S(1)} %get-tuple-element.25.base1, f32[3,12,16,128]{3,2,1,0:T(8,128)S(1)} %copy-done.1, ...), custom_call_target="tpu_custom_call" | custom-call | tf_op jit(solution)/shard_map/pallas_call | solution.py:473
  (13 shorter events, 0.2 us)
Async XLA Ops:
  0.0 20.5 %copy-start.4 = (f32[2,16,16,128]{3,2,1,0:T(8,128)S(1)}, f32[2,16,16,128]{3,2,1,0:T(8,128)}, u32[]{:S(2)}) copy-start(f32[2,16,16,128]{3,2,1,0:T(8,128)} %param.2) | copy-start | bytes 786436
  1.9 7.0 %collective-permute-start = (f32[3,16,4,128]{3,2,1,0:T(4,128)S(1)}, f32[3,16,4,128]{3,2,1,0:T(4,128)S(1)}, u32[]{:S(2)}, u32[]{:S(2)}) collective-permute-start(f32[3,16,4,128]{3,2,1,0:T(4,128)S(1)} %get-tuple-element.32), channel_id=1, source_target_pairs={{0,4},{4,8},{8,12},{12,16},{16,20},{20,24},{24,28},{1,5},{5,9},{9,... | collective-permute-start | bytes 294920 | tf_op jit(solution)/shard_map/ppermute | solution.py:487
  6.7 6.0 %collective-permute-start.1 = (f32[3,16,4,128]{3,2,1,0:T(4,128)S(1)}, f32[3,16,4,128]{3,2,1,0:T(4,128)S(1)}, u32[]{:S(2)}, u32[]{:S(2)}) collective-permute-start(f32[3,16,4,128]{3,2,1,0:T(4,128)S(1)} %get-tuple-element.31), channel_id=1, source_target_pairs={{4,0},{8,4},{12,8},{16,12},{20,16},{24,20},{28,24},{5,1},{9,5},{13... | collective-permute-start | bytes 294920 | tf_op jit(solution)/shard_map/ppermute | solution.py:487
  12.8 7.8 %collective-permute-start.3 = (f32[3,3,24,128]{3,2,1,0:T(8,128)S(1)}, f32[3,3,24,128]{3,2,1,0:T(8,128)S(1)}, u32[]{:S(2)}, u32[]{:S(2)}) collective-permute-start(f32[3,3,24,128]{3,2,1,0:T(8,128)S(1)} %pad_maximum_fusion.4), channel_id=1, source_target_pairs={{32,0},{64,32},{96,64},{128,96},{160,128},{192,160},{224,192},{256... | collective-permute-start | bytes 331784 | tf_op jit(solution)/shard_map/ppermute | solution.py:487
  18.6 3.7 %collective-permute-start.2 = (f32[3,3,24,128]{3,2,1,0:T(8,128)S(1)}, f32[3,3,24,128]{3,2,1,0:T(8,128)S(1)}, u32[]{:S(2)}, u32[]{:S(2)}) collective-permute-start(f32[3,3,24,128]{3,2,1,0:T(8,128)S(1)} %pad_maximum_fusion.3), channel_id=1, source_target_pairs={{0,32},{32,64},{64,96},{96,128},{128,160},{160,192},{192,224},{224... | collective-permute-start | bytes 331784 | tf_op jit(solution)/shard_map/ppermute | solution.py:487
  23.1 4.0 %collective-permute-start.4 = (f32[16,1584]{1,0:T(8,128)S(1)}, f32[16,1584]{1,0:T(8,128)S(1)}, u32[]{:S(2)}, u32[]{:S(2)}) collective-permute-start(f32[16,1584]{1,0:T(8,128)S(1)} %get-tuple-element.18), channel_id=1, source_target_pairs={{0,1},{1,2},{2,3},{4,5},{5,6},{6,7},{8,9},{9,10},{10,11},{12,13},{... | collective-permute-start | bytes 304136 | tf_op jit(solution)/shard_map/ppermute | solution.py:487
  25.3 5.9 %collective-permute-start.5 = (f32[16,1584]{1,0:T(8,128)S(1)}, f32[16,1584]{1,0:T(8,128)S(1)}, u32[]{:S(2)}, u32[]{:S(2)}) collective-permute-start(f32[16,1584]{1,0:T(8,128)S(1)} %get-tuple-element.19), channel_id=1, source_target_pairs={{1,0},{2,1},{3,2},{5,4},{6,5},{7,6},{9,8},{10,9},{11,10},{13,12},{... | collective-permute-start | bytes 304136 | tf_op jit(solution)/shard_map/ppermute | solution.py:487
  35.2 6.2 %collective-permute-start.6 = (f32[3,8,8,128]{3,2,1,0:T(8,128)S(1)}, f32[3,8,8,128]{3,2,1,0:T(8,128)S(1)}, u32[]{:S(2)}, u32[]{:S(2)}) collective-permute-start(f32[3,8,8,128]{3,2,1,0:T(8,128)S(1)} %shard_map.29.own), channel_id=1, source_target_pairs={{0,4},{4,8},{8,12},{12,16},{16,20},{20,24},{24,28},{1,5},{5,9},{9,... | collective-permute-start | bytes 294920 | tf_op jit(solution)/shard_map/ppermute | solution.py:487
  39.2 8.2 %collective-permute-start.7 = (f32[3,8,8,128]{3,2,1,0:T(8,128)S(1)}, f32[3,8,8,128]{3,2,1,0:T(8,128)S(1)}, u32[]{:S(2)}, u32[]{:S(2)}) collective-permute-start(f32[3,8,8,128]{3,2,1,0:T(8,128)S(1)} %shard_map.29.own), channel_id=1, source_target_pairs={{4,0},{8,4},{12,8},{16,12},{20,16},{24,20},{28,24},{5,1},{9,5},{13... | collective-permute-start | bytes 294920 | tf_op jit(solution)/shard_map/ppermute | solution.py:487
  47.4 9.1 %collective-permute-start.9 = (f32[3,6,24,128]{3,2,1,0:T(8,128)S(1)}, f32[3,6,24,128]{3,2,1,0:T(8,128)S(1)}, u32[]{:S(2)}, u32[]{:S(2)}) collective-permute-start(f32[3,6,24,128]{3,2,1,0:T(8,128)S(1)} %pad_maximum_fusion.2), channel_id=1, source_target_pairs={{32,0},{64,32},{96,64},{128,96},{160,128},{192,160},{224,192},{256... | collective-permute-start | bytes 663560 | tf_op jit(solution)/shard_map/ppermute | solution.py:487
  50.1 7.6 %collective-permute-start.8 = (f32[3,6,24,128]{3,2,1,0:T(8,128)S(1)}, f32[3,6,24,128]{3,2,1,0:T(8,128)S(1)}, u32[]{:S(2)}, u32[]{:S(2)}) collective-permute-start(f32[3,6,24,128]{3,2,1,0:T(8,128)S(1)} %pad_maximum_fusion.1), channel_id=1, source_target_pairs={{0,32},{32,64},{64,96},{96,128},{128,160},{160,192},{192,224},{224... | collective-permute-start | bytes 663560 | tf_op jit(solution)/shard_map/ppermute | solution.py:487
  60.7 20.8 %all-to-all-start = ((f32[32,11,2,128]{3,2,1,0:T(2,128)}), f32[32,11,2,128]{3,2,1,0:T(2,128)S(1)}, u32[]{:S(2)}, u32[]{:S(2)}) async-start(f32[32,11,2,128]{3,2,1,0:T(2,128)} %shard_map.30), calls=%async_computation | async-start | bytes 720896 | tf_op jit(solution)/shard_map/all_to_all | solution.py:524
  74.7 0.7 copy-start.2
  77.0 0.7 copy-start
  81.5 27.5 %copy-start.1 = (f32[3,12,16,128]{3,2,1,0:T(8,128)S(1)}, f32[3,12,16,128]{3,2,1,0:T(8,128)}, u32[]{:S(2)}) copy-start(f32[3,12,16,128]{3,2,1,0:T(8,128)} %copy-done) | copy-start | bytes 884740
  81.5 27.5 %copy-start.3 = (f32[2,16,16,128]{3,2,1,0:T(8,128)S(1)}, f32[2,16,16,128]{3,2,1,0:T(8,128)}, u32[]{:S(2)}) copy-start(f32[2,16,16,128]{3,2,1,0:T(8,128)} %copy-done.2) | copy-start | bytes 786436
  82.4 26.6 %all-to-all-start.1 = ((f32[16,48,128]{2,1,0:T(8,128)}), f32[16,48,128]{2,1,0:T(8,128)S(1)}, u32[]{:S(2)}, u32[]{:S(2)}) async-start(f32[16,48,128]{2,1,0:T(8,128)} %shard_map.33), calls=%async_computation.1 | async-start | bytes 786432 | tf_op jit(solution)/shard_map/all_to_all | solution.py:541
  95.1 8.4 %collective-permute-start.10 = (f32[45,4,128]{2,1,0:T(4,128)S(1)}, f32[45,4,128]{2,1,0:T(4,128)S(1)}, u32[]{:S(2)}, u32[]{:S(2)}) collective-permute-start(f32[45,4,128]{2,1,0:T(4,128)S(1)} %shard_map.34.own), channel_id=1, source_target_pairs={{0,32},{32,64},{64,96},{96,128},{128,160},{160,192},{192,224},{224... | collective-permute-start | bytes 276488 | tf_op jit(solution)/shard_map/ppermute | solution.py:487
  98.7 8.1 %collective-permute-start.11 = (f32[45,4,128]{2,1,0:T(4,128)S(1)}, f32[45,4,128]{2,1,0:T(4,128)S(1)}, u32[]{:S(2)}, u32[]{:S(2)}) collective-permute-start(f32[45,4,128]{2,1,0:T(4,128)S(1)} %shard_map.34.own), channel_id=1, source_target_pairs={{32,0},{64,32},{96,64},{128,96},{160,128},{192,160},{224,192},{256... | collective-permute-start | bytes 276488 | tf_op jit(solution)/shard_map/ppermute | solution.py:487

commit v4 on v3

--- a/solution.py
+++ b/solution.py
@@ -10,7 +10,7 @@
 F32, BF16 = jnp.float32, jnp.bfloat16
 WAVE = 0.0625
 DIAG_I = 0.5 * WAVE
-MOST = (2, 5, 6, 8, 16)
+MOST = (11, 7, 6, 16, 16)
 
 X0, Y0, L0 = 22, 24, 256
 HZ = 14
@@ -115,10 +115,12 @@
     blocks(hi - lo, MOST[level], compute, store)
 
 
-def relax_loop(lo, count, g, hd, v, write, level, ymask=False, zmask=False):
+def relax_loop(lo, count, g, hd, v, write, level, ymask=False, zmask=False, mach=None):
+    mach = g.at[2] if mach is None else mach
+
     def compute(j):
         i = lo + j
-        t_r, t_i, c_r, c_i, _ = balance((g[0, i], g[1, i]), g[2, i], v, i, level, ymask, zmask)
+        t_r, t_i, c_r, c_i, _ = balance((g[0, i], g[1, i]), mach[i], v, i, level, ymask, zmask)
         h_r, h_i = hd[0, i], hd[1, i]
         return 0.5 * c_r + (h_r * t_r - h_i * t_i), 0.5 * c_i + (h_r * t_i + h_i * t_r)
 
@@ -178,6 +180,12 @@
         f[c, hx + count :] = xhi[c]
 
 
+def start_kernel(source, mach, own, high, low):
+    for c in range(3):
+        own[c] = source[c] if c < 2 else mach[...].astype(F32)
+        high[c], low[c] = own[c, :, 12:16], own[c, :, 0:4]
+
+
 def gather0_kernel(own, ylo, yhi, xlo, xhi, f, low_lanes, high_lanes):
     assemble(own, ylo, yhi, xlo, xhi, f)
     parts = split(f[...].reshape(-1, 128))
@@ -219,7 +227,7 @@
             for half in range(2):
                 sums[half, pl.ds(row, 16), :] = parts[c][4:20, 128 * half : 128 * half + 128]
 
-    blocks(8, 1, lambda k: residual_pair(g, v2, 3 + 2 * k, 0), store)
+    blocks(8, 4, lambda k: residual_pair(g, v2, 3 + 2 * k, 0), store)
     own = matrix(128, 128, lambda r, l: r // 2 == l, 0.125)
     rest = matrix(
         128,
@@ -237,7 +245,7 @@
     relax_loop(1, X1D - 2, g, hd, v1, writer(v2), 1)
 
 
-def keep1_kernel(own, ylo, yhi, xlo, xhi, base, coef, g, hd, v2, v1):
+def keep1_kernel(own, ylo, yhi, xlo, xhi, base, coef, mach2, g, hd, v2, v1, sums):
     smooth1((own, ylo, yhi, xlo, xhi), g, hd, v2, v1)
     coef[0] = g[2, 4:16, 4:20]
     coef[1:3] = hd[:, 4:16, 4:20]
@@ -247,6 +255,18 @@
         base[0, j], base[1, j] = re[4:20, :], im[4:20, :]
 
     relax_loop(5, X1D - 10, g, hd, v1, write, 1)
+    sums[...] = jnp.zeros_like(sums)
+    for k in range(10):
+        sums[2 * Y2 * k : 2 * Y2 * k + Y1D, :] = g[2, 2 * k] + g[2, 2 * k + 1]
+    halve = matrix(
+        128,
+        128,
+        lambda r, l: ((r < 70) & (r // 2 == l)) | ((r >= 122) & (r // 2 + 64 == l)),
+        0.125,
+    )
+    mach2[0] = jnp.zeros((Y2, 128), F32)
+    mach2[X2 - 1] = jnp.zeros((Y2, 128), F32)
+    mach2[1 : X2 - 1] = select(pair_rows(sums, 20 * Y2), halve).reshape(10, Y2, 128)
 
 
 def down1_kernel(own, ylo, yhi, xlo, xhi, chunk, g, hd, v2, v1, sums, g2, hd2, va, vb):
@@ -258,7 +278,7 @@
             row = pl.multiple_of((c * X2D + k) * 2 * Y2, 2 * Y2)
             sums[pl.ds(row, Y1D), :] = parts[c]
 
-    blocks(X2D, 2, lambda k: residual_pair(g, v2, 2 + 2 * k, 1), store)
+    blocks(X2D, 4, lambda k: residual_pair(g, v2, 2 + 2 * k, 1), store)
     halve = matrix(
         128,
         128,
@@ -269,8 +289,8 @@
     first_loop(0, X2D, g2, hd2, va, 2)
     relax_loop(1, X2D - 2, g2, hd2, va, writer(vb), 2)
     lane = iota((Y2, 128), 1) // 32
-    for c in range(5):
-        source = (lambda x: g2[c, x]) if c < 3 else (lambda x: vb[c - 3, x])
+    for c in range(4):
+        source = (lambda x: g2[c, x]) if c < 2 else (lambda x: vb[c - 2, x])
         total = source(2)
         for x in range(1, 4):
             total = jnp.where(lane == x, pltpu.roll(source(2 + x), 32 * x, 1), total)
@@ -316,10 +336,10 @@
             inside = (y >= 0) & (y < 8) & (z >= 0) & (z < 4)
             at = jnp.clip(y, 0, 7) * 4 + jnp.clip(z, 0, 3)
             factor = jnp.where(inside, 1.0, 0.0)
-            for c in range(5):
+            for c in range(4):
                 for half in range(2):
                     rows = parts[at, 1 + 2 * c + half] * factor
-                    sheet[(bz * 3 + by) * 5 + c, 2 * half : 2 * half + 2, :] = rows
+                    sheet[(bz * 3 + by) * 4 + c, 2 * half : 2 * half + 2, :] = rows
 
 
 def window2_kernel(west, own, east, a, planes):
@@ -330,7 +350,7 @@
         def body(c, _):
             for bz in range(3):
                 for by in range(3):
-                    planes[bz, 4 * by : 4 * by + 4, :] = piece[(bz * 3 + by) * 5 + c]
+                    planes[bz, 4 * by : 4 * by + 4, :] = piece[(bz * 3 + by) * 4 + c]
             for x in range(4):
                 total = jnp.zeros((Y2, 128), F32)
                 for bz, group in enumerate((3, 0, 1)):
@@ -341,11 +361,11 @@
                 a[c, 4 * bx + x] = total
             return 0
 
-        lax.fori_loop(0, 5, body, 0)
+        lax.fori_loop(0, 4, body, 0)
 
 
 def up_kernel(
-    index, parts3, a, base1, coef1, base0, coef0, out,
+    index, parts3, a, mach2, base1, coef1, base0, coef0, out,
     g3, hd3, va3, vb3, s3, g4, hd4, va4, vb4, t4, w3, t3, hd2, va2, vb2, w2, t2, va1, vb1, t1, va0, vb0,
 ):
     gx, gy, gz = index[0], index[1], index[2]
@@ -357,14 +377,15 @@
                 ref[c, PAD3 + X3 + i] = zero3
     low = iota((Y3, 128), 1) < 64
 
-    def spread(s, _):
+    def spread(s):
+        values = [parts3[s, Y3 * c : Y3 * (c + 1), :] for c in range(3)]
+        return [(jnp.where(low, v, 0.0), jnp.where(low, pltpu.roll(v, 64, 1), 0.0)) for v in values]
+
+    def keep(s, values):
         for c in range(3):
-            value = parts3[s, Y3 * c : Y3 * (c + 1), :]
-            g3[c, PAD3 + 2 * s] = jnp.where(low, value, 0.0)
-            g3[c, PAD3 + 2 * s + 1] = jnp.where(low, pltpu.roll(value, 64, 1), 0.0)
-        return 0
-
-    lax.fori_loop(0, 16, spread, 0)
+            g3[c, PAD3 + 2 * s], g3[c, PAD3 + 2 * s + 1] = values[c]
+
+    blocks(16, 4, spread, keep)
     first_loop(PAD3, PAD3 + X3, g3, hd3, va3, 3)
     relax_loop(PAD3, X3, g3, hd3, va3, writer(vb3), 3, True)
 
@@ -372,7 +393,7 @@
         for c in range(3):
             s3[pl.ds(pl.multiple_of((c * X4 + k) * Y3, Y3), Y3), :] = parts[c]
 
-    blocks(X4, 4, lambda k: residual_pair(g3, vb3, PAD3 + 2 * k, 3, True), keep3)
+    blocks(X4, 8, lambda k: residual_pair(g3, vb3, PAD3 + 2 * k, 3, True), keep3)
     halve = matrix(128, 128, lambda r, l: (r // 2 == l) & (r < 64), 0.125)
     g4[:, 1 : 1 + X4] = select(pair_rows(s3, 3 * X4 * Y3), halve).reshape(3, X4, Y4, 128)
     for ref in (va4, vb4):
@@ -387,14 +408,17 @@
     double = matrix(128, 128, lambda r, l: l // 2 == r)
     twin_rows(t4, select(src[:, 1 : 1 + X4].reshape(2 * X4 * Y4, 128), double))
 
-    def add3(k, _):
+    def add3(k):
+        values = [t4[pl.ds(pl.multiple_of((c * X4 + k) * Y3, Y3), Y3), :] for c in range(2)]
+        at = PAD3 + 2 * k
+        return [(vb3[c, at] + values[c], vb3[c, at + 1] + values[c]) for c in range(2)]
+
+    def put3(k, values):
+        at = PAD3 + 2 * k
         for c in range(2):
-            value = t4[pl.ds(pl.multiple_of((c * X4 + k) * Y3, Y3), Y3), :]
-            vb3[c, PAD3 + 2 * k] = vb3[c, PAD3 + 2 * k] + value
-            vb3[c, PAD3 + 2 * k + 1] = vb3[c, PAD3 + 2 * k + 1] + value
-        return 0
-
-    lax.fori_loop(0, X4, add3, 0)
+            vb3[c, at], vb3[c, at + 1] = values[c]
+
+    blocks(X4, 4, add3, put3)
     base = PAD3 + 2 * gx
     relax_loop(base - 3, 8, g3, hd3, vb3, writer(va3), 3, True)
 
@@ -412,30 +436,26 @@
 
     twin_rows(t3, select(rows, matrix(128, 128, place2)))
 
-    def start2(i, _):
-        hd2[0, i], hd2[1, i] = half_inverse(a[2, i], 2)
+    for i in range(X2):
+        hd2[0, i], hd2[1, i] = half_inverse(mach2[i], 2)
         for c in range(2):
-            row = pl.multiple_of((c * 6 + i // 2) * Y2, Y2)
-            va2[c, i] = a[3 + c, i] + jnp.where(a[2, i] > 0.0, t3[pl.ds(row, Y2), :], 0.0)
-        return 0
-
-    lax.fori_loop(0, X2, start2, 0)
-    relax_loop(1, X2 - 2, a, hd2, va2, writer(vb2), 2)
+            row = (c * 6 + i // 2) * Y2
+            va2[c, i] = a[2 + c, i] + t3[row : row + Y2, :]
+
+    relax_loop(1, X2 - 2, a, hd2, va2, writer(vb2), 2, mach=mach2)
 
     def write2(j, i, re, im):
         w2[0, j], w2[1, j] = re, im
 
-    relax_loop(2, X2 - 4, a, hd2, vb2, write2, 2)
+    relax_loop(2, X2 - 4, a, hd2, vb2, write2, 2, mach=mach2)
     double = matrix(128, 128, lambda r, l: jnp.where(l < 96, l // 2, l // 2 + 64) == r)
     twin_rows(t2, select(w2[:, :, 2:10, :].reshape(2 * 8 * 8, 128), double))
 
-    def start1(i, _):
+    for i in range(1, X1 - 1):
         for c in range(2):
-            row = pl.multiple_of((c * 8 + i // 2) * Y1, Y1)
-            va1[c, i] = t2[pl.ds(row, Y1), :]
-        return 0
-
-    lax.fori_loop(1, X1 - 1, start1, 0)
+            row = (c * 8 + i // 2) * Y1
+            va1[c, i] = t2[row : row + Y1, :]
+
     free_loop(2, X1 - 4, coef1, va1, writer(vb1), 1)
 
     def write1(j, i, re, im):
@@ -487,10 +507,9 @@
     return lax.ppermute(block, axis, pairs)
 
 
-def halos(own, hx, hy):
-    count, rows = own.shape[1], own.shape[2]
-    ylo = shift(own[:, :, rows - hy :], "gy", 1)
-    yhi = shift(own[:, :, :hy], "gy", -1)
+def halos(own, high, low, hx):
+    count = own.shape[1]
+    ylo, yhi = shift(high, "gy", 1), shift(low, "gy", -1)
 
     def edge(at):
         return jnp.concatenate([x[:, at : at + hx] for x in (ylo, own, yhi)], axis=2)
@@ -503,9 +522,10 @@
 
 
 def shards(source_field, mach_number):
-    own0 = jnp.concatenate([source_field, mach_number.astype(F32)[None]], axis=0)
+    edge = (3, 16, 4, 128)
+    start = call(start_kernel, [(3, 16, 16, 128), edge, edge], [], source_field, mach_number)
     flat = (16, 3 * X0 * Y0)
-    f0, low, high = call(gather0_kernel, [(3, X0, Y0, 128), flat, flat], [], *halos(own0, 3, 4))
+    f0, low, high = call(gather0_kernel, [(3, X0, Y0, 128), flat, flat], [], *halos(*start, 3))
     full0, full1 = (X0, Y0, L0), (X1, Y1, L1)
     block0 = (f0, shift(high, "gz", 1), shift(low, "gz", -1))
     smoothed0 = [(3,) + full0] + [(2,) + full0] * 3
@@ -513,11 +533,11 @@
         down0_kernel, [(3, 8, 8, 128)], smoothed0 + [(2, 384, 128)], *block0
     )
     wide1, wide2 = (X1D, Y1D, L1), (X2D, Y2, 128)
-    block1 = halos(own1, 6, 8)
+    block1 = halos(own1, own1, own1, 6)
     smoothed1 = [(3,) + wide1] + [(2,) + wide1] * 3
     (chunk2,) = call(
         down1_kernel,
-        [(32, 11, 2, 128)],
+        [(32, 9, 2, 128)],
         smoothed1 + [(6 * X2D * Y2, 128), (3,) + wide2] + [(2,) + wide2] * 3,
         *block1,
     )
@@ -529,21 +549,21 @@
         *block0,
         cost=(60 << 20, 8 << 20),
     )
-    base1, coef1 = call(
+    base1, coef1, mach2 = call(
         keep1_kernel,
-        [(2, 10, Y1, 128), (3, 12, Y1, 128)],
-        smoothed1,
+        [(2, 10, Y1, 128), (3, 12, Y1, 128), (X2, Y2, 128)],
+        smoothed1 + [(20 * Y2, 128)],
         *block1,
         cost=(8 << 20, 1 << 20),
     )
-    parts2, *kept = lax.optimization_barrier((parts2, base1, coef1, base0, coef0))
+    parts2, *kept = lax.optimization_barrier((parts2, mach2, base1, coef1, base0, coef0))
     (chunk3,) = call(spread3_kernel, [(16, 48, 128)], [(4, Y3, 128)], parts2)
     parts3 = lax.all_to_all(chunk3, "gx", 0, 0)
     index = jnp.stack([lax.axis_index(n) for n in ("gx", "gy", "gz")]).astype(jnp.int32)
-    (sheet,) = call(pick2_kernel, [(45, 4, 128)], [], index, parts2, memory="svv")
+    (sheet,) = call(pick2_kernel, [(36, 4, 128)], [], index, parts2, memory="svv")
     west, east = around(sheet, "gx")
     (a,) = call(
-        window2_kernel, [(5, X2, Y2, 128)], [(3, Y2, 128)], west, sheet, east, cost=(4 << 20, 1 << 20)
+        window2_kernel, [(4, X2, Y2, 128)], [(3, Y2, 128)], west, sheet, east, cost=(4 << 20, 1 << 20)
     )
     wide3 = (X3 + 2 * PAD3, Y3, 128)
     wide4 = (X4 + 2, Y4, 128)
@@ -558,7 +578,7 @@
         scratch,
         index, parts3, a, *kept,
         limit=16,
-        memory="svvvvvvv",
+        memory="svvvvvvvv",
     )[0]
 
 

time: 119 us -> 115 us (0.966)
  Pallas kernels: 26.5 us -> 21 us
  other arithmetic: 2.93 us -> 0.16 us
  local copies, waits for them, and re-layouts: 1.45 us -> 3.84 us
  waiting for transfers between devices: 30.6 us -> 31.8 us
    pallas_call x9 -> x10, Pallas kernels: 26.5 us -> 21 us  [call(): pl.pallas_call(kernel, out_shape=[jax.ShapeDtypeStruct(s, F32) for s in o...]
    unnamed x10 -> x16, local copies, waits for them, and re-layouts: 1.41 us -> 3.78 us
    concatenate x3 -> x0, other arithmetic: 1.87 us -> none  [shards(): jnp.concatenate([source_field, mach_number.astype(F32)[None]], axis=0)]
  transfers between devices with their start and end apart: 14 -> 14, of which waited for: 12 -> 13; matrix products, arithmetic and copies ran while one was open for 1% -> 0% of each run, Pallas kernels for 7% -> 6%
where the time goes in v4:
time: 115 us; the launch traced here: 114 us
  starting transfers between devices  57.1 us (50%)
  waiting for transfers between devices  31.8 us (28%)
  Pallas kernels  21 us (18%)
  local copies, waits for them, and re-layouts  3.84 us (3%)
    ppermute x12, starting transfers between devices, shift(): return lax.ppermute(block, axis, pairs)  35.6 us
    ppermute x12, waiting for transfers between devices, shift(): return lax.ppermute(block, axis, pairs)  26.6 us
    pallas_call x10, Pallas kernels, call(): pl.pallas_call(kernel, out_shape=[jax.ShapeDtypeStruct(s, F32) for s in o...  21 us
    all_to_all x1, starting transfers between devices, shards(): parts3 = lax.all_to_all(chunk3, 'gx', 0, 0)  12.4 us
    all_to_all x1, starting transfers between devices, shards(): parts2 = lax.all_to_all(chunk2, ('gy', 'gz'), 0, 0)  9.13 us
    all_to_all x1, waiting for transfers between devices, shards(): parts2 = lax.all_to_all(chunk2, ('gy', 'gz'), 0, 0)  3.84 us
    unnamed x16, local copies, waits for them, and re-layouts  3.78 us
  transfers between devices with their start and end apart: 14, of which 13 were waited for; matrix products, arithmetic and copies ran while one was open for 0% of the time, Pallas kernels for 6%

profile of v4, /device:TPU:1, one launch (start us, length us, event | category | flops | bytes accessed | tf_op | source)
XLA Modules:
  0.0 114.1 jit_solution(6224071395538161095)
XLA Ops:
  0.0 0.9 copy-done
  1.0 0.8 copy-done.7
  1.8 0.1 shard_map.28
  1.9 4.8 %collective-permute-start = (f32[3,16,4,128]{3,2,1,0:T(4,128)S(1)}, f32[3,16,4,128]{3,2,1,0:T(4,128)S(1)}, u32[]{:S(2)}, u32[]{:S(2)}) collective-permute-start(f32[3,16,4,128]{3,2,1,0:T(4,128)S(1)} %get-tuple-element.23), channel_id=1, source_target_pairs={{0,4},{4,8},{8,12},{12,16},{16,20},{20,24},{24,28},{1,5},{5,9},{9,... | collective-permute-start | bytes 294920 | tf_op jit(solution)/shard_map/ppermute | solution.py:507
  6.7 1.3 %collective-permute-start.1 = (f32[3,16,4,128]{3,2,1,0:T(4,128)S(1)}, f32[3,16,4,128]{3,2,1,0:T(4,128)S(1)}, u32[]{:S(2)}, u32[]{:S(2)}) collective-permute-start(f32[3,16,4,128]{3,2,1,0:T(4,128)S(1)} %get-tuple-element.24), channel_id=1, source_target_pairs={{4,0},{8,4},{12,8},{16,12},{20,16},{24,20},{28,24},{5,1},{9,5},{13... | collective-permute-start | bytes 294920 | tf_op jit(solution)/shard_map/ppermute | solution.py:507
  8.0 0.3 collective-permute-done.ylo
  8.3 4.4 %collective-permute-done.1.yhi = f32[3,16,4,128]{3,2,1,0:T(4,128)S(1)} collective-permute-done((f32[3,16,4,128]{3,2,1,0:T(4,128)S(1)}, f32[3,16,4,128]{3,2,1,0:T(4,128)S(1)}, u32[]{:S(2)}, u32[]{:S(2)}) %collective-permute-start.1) | collective-permute-done | bytes 98336 | tf_op jit(solution)/shard_map/ppermute | solution.py:507
  12.7 5.8 %collective-permute-start.3 = (f32[3,3,24,128]{3,2,1,0:T(8,128)S(1)}, f32[3,3,24,128]{3,2,1,0:T(8,128)S(1)}, u32[]{:S(2)}, u32[]{:S(2)}) collective-permute-start(f32[3,3,24,128]{3,2,1,0:T(8,128)S(1)} %pad_maximum_fusion.3), channel_id=1, source_target_pairs={{32,0},{64,32},{96,64},{128,96},{160,128},{192,160},{224,192},{256... | collective-permute-start | bytes 331784 | tf_op jit(solution)/shard_map/ppermute | solution.py:507
  18.5 1.9 %collective-permute-start.2 = (f32[3,3,24,128]{3,2,1,0:T(8,128)S(1)}, f32[3,3,24,128]{3,2,1,0:T(8,128)S(1)}, u32[]{:S(2)}, u32[]{:S(2)}) collective-permute-start(f32[3,3,24,128]{3,2,1,0:T(8,128)S(1)} %pad_maximum_fusion.2), channel_id=1, source_target_pairs={{0,32},{32,64},{64,96},{96,128},{128,160},{160,192},{192,224},{224... | collective-permute-start | bytes 331784 | tf_op jit(solution)/shard_map/ppermute | solution.py:507
  20.5 0.0 collective-permute-done.3.xhi
  20.5 1.7 %collective-permute-done.2.xlo = f32[3,3,24,128]{3,2,1,0:T(8,128)S(1)} collective-permute-done((f32[3,3,24,128]{3,2,1,0:T(8,128)S(1)}, f32[3,3,24,128]{3,2,1,0:T(8,128)S(1)}, u32[]{:S(2)}, u32[]{:S(2)}) %collective-permute-start.2) | collective-permute-done | bytes 110624 | tf_op jit(solution)/shard_map/ppermute | solution.py:507
  22.2 0.8 shard_map.29
  23.0 2.3 %collective-permute-start.4 = (f32[16,1584]{1,0:T(8,128)S(1)}, f32[16,1584]{1,0:T(8,128)S(1)}, u32[]{:S(2)}, u32[]{:S(2)}) collective-permute-start(f32[16,1584]{1,0:T(8,128)S(1)} %get-tuple-element.26), channel_id=1, source_target_pairs={{0,1},{1,2},{2,3},{4,5},{5,6},{6,7},{8,9},{9,10},{10,11},{12,13},{... | collective-permute-start | bytes 304136 | tf_op jit(solution)/shard_map/ppermute | solution.py:507
  25.3 1.3 %collective-permute-start.5 = (f32[16,1584]{1,0:T(8,128)S(1)}, f32[16,1584]{1,0:T(8,128)S(1)}, u32[]{:S(2)}, u32[]{:S(2)}) collective-permute-start(f32[16,1584]{1,0:T(8,128)S(1)} %get-tuple-element.27), channel_id=1, source_target_pairs={{1,0},{2,1},{3,2},{5,4},{6,5},{7,6},{9,8},{10,9},{11,10},{13,12},{... | collective-permute-start | bytes 304136 | tf_op jit(solution)/shard_map/ppermute | solution.py:507
  26.6 0.4 collective-permute-done.4.lower
  27.0 4.1 %collective-permute-done.5.upper = f32[16,1584]{1,0:T(8,128)S(1)} collective-permute-done((f32[16,1584]{1,0:T(8,128)S(1)}, f32[16,1584]{1,0:T(8,128)S(1)}, u32[]{:S(2)}, u32[]{:S(2)}) %collective-permute-start.5) | collective-permute-done | bytes 101408 | tf_op jit(solution)/shard_map/ppermute | solution.py:507
  31.1 3.0 %shard_map.30.own = f32[3,8,8,128]{3,2,1,0:T(8,128)S(1)} custom-call(f32[3,22,24,128]{3,2,1,0:T(8,128)S(1)} %get-tuple-element.25.f, f32[16,1584]{1,0:T(8,128)S(1)} %collective-permute-done.4.lower, f32[16,1584]{1,0:T(8,128)S(1)} %collective-permute-done.5.upper), custom_call_target="tpu_custom_call" | custom-call | tf_op jit(solution)/shard_map/pallas_call | solution.py:493
  34.2 4.0 %collective-permute-start.6 = (f32[3,8,8,128]{3,2,1,0:T(8,128)S(1)}, f32[3,8,8,128]{3,2,1,0:T(8,128)S(1)}, u32[]{:S(2)}, u32[]{:S(2)}) collective-permute-start(f32[3,8,8,128]{3,2,1,0:T(8,128)S(1)} %shard_map.30.own), channel_id=1, source_target_pairs={{0,4},{4,8},{8,12},{12,16},{16,20},{20,24},{24,28},{1,5},{5,9},{9,... | collective-permute-start | bytes 294920 | tf_op jit(solution)/shard_map/ppermute | solution.py:507
  38.2 1.3 %collective-permute-start.7 = (f32[3,8,8,128]{3,2,1,0:T(8,128)S(1)}, f32[3,8,8,128]{3,2,1,0:T(8,128)S(1)}, u32[]{:S(2)}, u32[]{:S(2)}) collective-permute-start(f32[3,8,8,128]{3,2,1,0:T(8,128)S(1)} %shard_map.30.own), channel_id=1, source_target_pairs={{4,0},{8,4},{12,8},{16,12},{20,16},{24,20},{28,24},{5,1},{9,5},{13... | collective-permute-start | bytes 294920 | tf_op jit(solution)/shard_map/ppermute | solution.py:507
  39.5 0.9 collective-permute-done.6.ylo
  40.4 6.0 %collective-permute-done.7.yhi = f32[3,8,8,128]{3,2,1,0:T(8,128)S(1)} collective-permute-done((f32[3,8,8,128]{3,2,1,0:T(8,128)S(1)}, f32[3,8,8,128]{3,2,1,0:T(8,128)S(1)}, u32[]{:S(2)}, u32[]{:S(2)}) %collective-permute-start.7) | collective-permute-done | bytes 98336 | tf_op jit(solution)/shard_map/ppermute | solution.py:507
  46.4 2.7 %collective-permute-start.9 = (f32[3,6,24,128]{3,2,1,0:T(8,128)S(1)}, f32[3,6,24,128]{3,2,1,0:T(8,128)S(1)}, u32[]{:S(2)}, u32[]{:S(2)}) collective-permute-start(f32[3,6,24,128]{3,2,1,0:T(8,128)S(1)} %pad_maximum_fusion.1), channel_id=1, source_target_pairs={{32,0},{64,32},{96,64},{128,96},{160,128},{192,160},{224,192},{256... | collective-permute-start | bytes 663560 | tf_op jit(solution)/shard_map/ppermute | solution.py:507
  49.1 4.8 %collective-permute-start.8 = (f32[3,6,24,128]{3,2,1,0:T(8,128)S(1)}, f32[3,6,24,128]{3,2,1,0:T(8,128)S(1)}, u32[]{:S(2)}, u32[]{:S(2)}) collective-permute-start(f32[3,6,24,128]{3,2,1,0:T(8,128)S(1)} %pad_maximum_fusion), channel_id=1, source_target_pairs={{0,32},{32,64},{64,96},{96,128},{128,160},{160,192},{192,224},{224... | collective-permute-start | bytes 663560 | tf_op jit(solution)/shard_map/ppermute | solution.py:507
  53.9 1.6 %collective-permute-done.9.xhi = f32[3,6,24,128]{3,2,1,0:T(8,128)S(1)} collective-permute-done((f32[3,6,24,128]{3,2,1,0:T(8,128)S(1)}, f32[3,6,24,128]{3,2,1,0:T(8,128)S(1)}, u32[]{:S(2)}, u32[]{:S(2)}) %collective-permute-start.9) | collective-permute-done | bytes 221216 | tf_op jit(solution)/shard_map/ppermute | solution.py:507
  55.5 1.2 %collective-permute-done.8.xlo = f32[3,6,24,128]{3,2,1,0:T(8,128)S(1)} collective-permute-done((f32[3,6,24,128]{3,2,1,0:T(8,128)S(1)}, f32[3,6,24,128]{3,2,1,0:T(8,128)S(1)}, u32[]{:S(2)}, u32[]{:S(2)}) %collective-permute-start.8) | collective-permute-done | bytes 221216 | tf_op jit(solution)/shard_map/ppermute | solution.py:507
  56.7 2.5 %shard_map.31 = f32[32,9,2,128]{3,2,1,0:T(2,128)} custom-call(f32[3,8,8,128]{3,2,1,0:T(8,128)S(1)} %shard_map.30.own, f32[3,8,8,128]{3,2,1,0:T(8,128)S(1)} %collective-permute-done.6.ylo, f32[3,8,8,128]{3,2,1,0:T(8,128)S(1)} %collective-permute-done.7.yhi, f32[3,6,24,128]{3,2,1,0:T(8,128)S(1)} %collective-permute-done.8.xlo, ...), custom_call_target="tpu_custom_call" | custom-call | tf_op jit(solution)/shard_map/pallas_call | solution.py:493
  59.3 9.1 %all-to-all-start = ((f32[32,9,2,128]{3,2,1,0:T(2,128)}), f32[32,9,2,128]{3,2,1,0:T(2,128)S(1)}, u32[]{:S(2)}, u32[]{:S(2)}) async-start(f32[32,9,2,128]{3,2,1,0:T(2,128)} %shard_map.31), calls=%async_computation | async-start | bytes 589824 | tf_op jit(solution)/shard_map/all_to_all | solution.py:544
  68.4 3.5 %shard_map.33 = (f32[2,16,16,128]{3,2,1,0:T(8,128)S(1)}, f32[3,18,24,256]{3,2,1,0:T(8,128)S(1)}) custom-call(f32[3,22,24,128]{3,2,1,0:T(8,128)S(1)} %get-tuple-element.25.f, f32[16,1584]{1,0:T(8,128)S(1)} %collective-permute-done.4.lower, f32[16,1584]{1,0:T(8,128)S(1)} %collective-permute-done.5.upper), custom_call_target="tpu_custom_call" | custom-call | flops 62914560 | bytes 8388608 | tf_op jit(solution)/shard_map/pallas_call | solution.py:493
  71.9 0.0 copy-start.1
  71.9 0.7 copy-done.1
  72.6 1.5 %shard_map.32 = (f32[2,10,16,128]{3,2,1,0:T(8,128)S(1)}, f32[3,12,16,128]{3,2,1,0:T(8,128)S(1)}, f32[12,16,128]{2,1,0:T(8,128)S(1)}) custom-call(f32[3,8,8,128]{3,2,1,0:T(8,128)S(1)} %shard_map.30.own, f32[3,8,8,128]{3,2,1,0:T(8,128)S(1)} %collective-permute-done.6.ylo, f32[3,8,8,128]{3,2,1,0:T(8,128)S(1)} %collective-permute-done.7.yhi, ...), custom_call_target="tpu_custom_call" | custom-call | flops 8388608 | bytes 1048576 | tf_op jit(solution)/shard_map/pallas_call | solution.py:493
  74.1 0.0 copy-start.3
  74.1 0.7 copy-done.3
  74.8 0.6 copy-done.5
  75.4 3.8 %all-to-all-done.parts = f32[32,9,2,128]{3,2,1,0:T(2,128)S(1)} async-done(((f32[32,9,2,128]{3,2,1,0:T(2,128)}), f32[32,9,2,128]{3,2,1,0:T(2,128)S(1)}, u32[]{:S(2)}, u32[]{:S(2)}) %all-to-all-start) | async-done | bytes 294944 | tf_op jit(solution)/shard_map/all_to_all | solution.py:544
  79.2 0.9 shard_map.34
  80.1 12.4 %all-to-all-start.1 = ((f32[16,48,128]{2,1,0:T(8,128)}), f32[16,48,128]{2,1,0:T(8,128)S(1)}, u32[]{:S(2)}, u32[]{:S(2)}) async-start(f32[16,48,128]{2,1,0:T(8,128)} %shard_map.34), calls=%async_computation.1 | async-start | bytes 786432 | tf_op jit(solution)/shard_map/all_to_all | solution.py:561
  92.5 0.1 pad_add_fusion.index
  92.6 0.6 shard_map.35.own
  93.2 3.5 %collective-permute-start.10 = (f32[36,4,128]{2,1,0:T(4,128)S(1)}, f32[36,4,128]{2,1,0:T(4,128)S(1)}, u32[]{:S(2)}, u32[]{:S(2)}) collective-permute-start(f32[36,4,128]{2,1,0:T(4,128)S(1)} %shard_map.35.own), channel_id=1, source_target_pairs={{0,32},{32,64},{64,96},{96,128},{128,160},{160,192},{192,224},{224... | collective-permute-start | bytes 221192 | tf_op jit(solution)/shard_map/ppermute | solution.py:507
  96.8 1.9 %collective-permute-start.11 = (f32[36,4,128]{2,1,0:T(4,128)S(1)}, f32[36,4,128]{2,1,0:T(4,128)S(1)}, u32[]{:S(2)}, u32[]{:S(2)}) collective-permute-start(f32[36,4,128]{2,1,0:T(4,128)S(1)} %shard_map.35.own), channel_id=1, source_target_pairs={{32,0},{64,32},{96,64},{128,96},{160,128},{192,160},{224,192},{256... | collective-permute-start | bytes 221192 | tf_op jit(solution)/shard_map/ppermute | solution.py:507
  98.7 2.6 %collective-permute-done.10.west = f32[36,4,128]{2,1,0:T(4,128)S(1)} collective-permute-done((f32[36,4,128]{2,1,0:T(4,128)S(1)}, f32[36,4,128]{2,1,0:T(4,128)S(1)}, u32[]{:S(2)}, u32[]{:S(2)}) %collective-permute-start.10) | collective-permute-done | bytes 73760 | tf_op jit(solution)/shard_map/ppermute | solution.py:507
  101.3 3.4 %collective-permute-done.11.east = f32[36,4,128]{2,1,0:T(4,128)S(1)} collective-permute-done((f32[36,4,128]{2,1,0:T(4,128)S(1)}, f32[36,4,128]{2,1,0:T(4,128)S(1)}, u32[]{:S(2)}, u32[]{:S(2)}) %collective-permute-start.11) | collective-permute-done | bytes 73760 | tf_op jit(solution)/shard_map/ppermute | solution.py:507
  104.6 1.1 shard_map.36.a
  105.7 1.4 %all-to-all-done.1.parts3 = f32[16,48,128]{2,1,0:T(8,128)S(1)} async-done(((f32[16,48,128]{2,1,0:T(8,128)}), f32[16,48,128]{2,1,0:T(8,128)S(1)}, u32[]{:S(2)}, u32[]{:S(2)}) %all-to-all-start.1) | async-done | bytes 393248 | tf_op jit(solution)/shard_map/all_to_all | solution.py:561
  107.1 0.0 copy-done.2
  107.1 0.0 copy-done.6
  107.1 7.0 %shard_map.37 = f32[2,16,16,128]{3,2,1,0:T(8,128)} custom-call(s32[3]{0:T(128)S(1)} %pad_add_fusion.index, f32[16,48,128]{2,1,0:T(8,128)S(1)} %all-to-all-done.1.parts3, f32[4,12,16,128]{3,2,1,0:T(8,128)S(1)} %shard_map.36.a, f32[12,16,128]{2,1,0:T(8,128)S(1)} %copy-done.6, f32[2,10,16,128]{3,2,1,0:T(8,128)S(1)} %copy-done.4, ...), custom_call_target="tpu_custom_call" | custom-call | tf_op jit(solution)/shard_map/pallas_call | solution.py:493
  (17 shorter events, 0.2 us)
Async XLA Ops:
  0.0 0.9 copy-start
  1.0 0.8 copy-start.7
  1.9 6.5 %collective-permute-start = (f32[3,16,4,128]{3,2,1,0:T(4,128)S(1)}, f32[3,16,4,128]{3,2,1,0:T(4,128)S(1)}, u32[]{:S(2)}, u32[]{:S(2)}) collective-permute-start(f32[3,16,4,128]{3,2,1,0:T(4,128)S(1)} %get-tuple-element.23), channel_id=1, source_target_pairs={{0,4},{4,8},{8,12},{12,16},{16,20},{20,24},{24,28},{1,5},{5,9},{9,... | collective-permute-start | bytes 294920 | tf_op jit(solution)/shard_map/ppermute | solution.py:507
  6.7 6.0 %collective-permute-start.1 = (f32[3,16,4,128]{3,2,1,0:T(4,128)S(1)}, f32[3,16,4,128]{3,2,1,0:T(4,128)S(1)}, u32[]{:S(2)}, u32[]{:S(2)}) collective-permute-start(f32[3,16,4,128]{3,2,1,0:T(4,128)S(1)} %get-tuple-element.24), channel_id=1, source_target_pairs={{4,0},{8,4},{12,8},{16,12},{20,16},{24,20},{28,24},{5,1},{9,5},{13... | collective-permute-start | bytes 294920 | tf_op jit(solution)/shard_map/ppermute | solution.py:507
  12.7 7.7 %collective-permute-start.3 = (f32[3,3,24,128]{3,2,1,0:T(8,128)S(1)}, f32[3,3,24,128]{3,2,1,0:T(8,128)S(1)}, u32[]{:S(2)}, u32[]{:S(2)}) collective-permute-start(f32[3,3,24,128]{3,2,1,0:T(8,128)S(1)} %pad_maximum_fusion.3), channel_id=1, source_target_pairs={{32,0},{64,32},{96,64},{128,96},{160,128},{192,160},{224,192},{256... | collective-permute-start | bytes 331784 | tf_op jit(solution)/shard_map/ppermute | solution.py:507
  18.5 3.7 %collective-permute-start.2 = (f32[3,3,24,128]{3,2,1,0:T(8,128)S(1)}, f32[3,3,24,128]{3,2,1,0:T(8,128)S(1)}, u32[]{:S(2)}, u32[]{:S(2)}) collective-permute-start(f32[3,3,24,128]{3,2,1,0:T(8,128)S(1)} %pad_maximum_fusion.2), channel_id=1, source_target_pairs={{0,32},{32,64},{64,96},{96,128},{128,160},{160,192},{192,224},{224... | collective-permute-start | bytes 331784 | tf_op jit(solution)/shard_map/ppermute | solution.py:507
  23.0 4.0 %collective-permute-start.4 = (f32[16,1584]{1,0:T(8,128)S(1)}, f32[16,1584]{1,0:T(8,128)S(1)}, u32[]{:S(2)}, u32[]{:S(2)}) collective-permute-start(f32[16,1584]{1,0:T(8,128)S(1)} %get-tuple-element.26), channel_id=1, source_target_pairs={{0,1},{1,2},{2,3},{4,5},{5,6},{6,7},{8,9},{9,10},{10,11},{12,13},{... | collective-permute-start | bytes 304136 | tf_op jit(solution)/shard_map/ppermute | solution.py:507
  25.3 5.9 %collective-permute-start.5 = (f32[16,1584]{1,0:T(8,128)S(1)}, f32[16,1584]{1,0:T(8,128)S(1)}, u32[]{:S(2)}, u32[]{:S(2)}) collective-permute-start(f32[16,1584]{1,0:T(8,128)S(1)} %get-tuple-element.27), channel_id=1, source_target_pairs={{1,0},{2,1},{3,2},{5,4},{6,5},{7,6},{9,8},{10,9},{11,10},{13,12},{... | collective-permute-start | bytes 304136 | tf_op jit(solution)/shard_map/ppermute | solution.py:507
  34.2 6.2 %collective-permute-start.6 = (f32[3,8,8,128]{3,2,1,0:T(8,128)S(1)}, f32[3,8,8,128]{3,2,1,0:T(8,128)S(1)}, u32[]{:S(2)}, u32[]{:S(2)}) collective-permute-start(f32[3,8,8,128]{3,2,1,0:T(8,128)S(1)} %shard_map.30.own), channel_id=1, source_target_pairs={{0,4},{4,8},{8,12},{12,16},{16,20},{20,24},{24,28},{1,5},{5,9},{9,... | collective-permute-start | bytes 294920 | tf_op jit(solution)/shard_map/ppermute | solution.py:507
  38.2 8.2 %collective-permute-start.7 = (f32[3,8,8,128]{3,2,1,0:T(8,128)S(1)}, f32[3,8,8,128]{3,2,1,0:T(8,128)S(1)}, u32[]{:S(2)}, u32[]{:S(2)}) collective-permute-start(f32[3,8,8,128]{3,2,1,0:T(8,128)S(1)} %shard_map.30.own), channel_id=1, source_target_pairs={{4,0},{8,4},{12,8},{16,12},{20,16},{24,20},{28,24},{5,1},{9,5},{13... | collective-permute-start | bytes 294920 | tf_op jit(solution)/shard_map/ppermute | solution.py:507
  46.4 9.1 %collective-permute-start.9 = (f32[3,6,24,128]{3,2,1,0:T(8,128)S(1)}, f32[3,6,24,128]{3,2,1,0:T(8,128)S(1)}, u32[]{:S(2)}, u32[]{:S(2)}) collective-permute-start(f32[3,6,24,128]{3,2,1,0:T(8,128)S(1)} %pad_maximum_fusion.1), channel_id=1, source_target_pairs={{32,0},{64,32},{96,64},{128,96},{160,128},{192,160},{224,192},{256... | collective-permute-start | bytes 663560 | tf_op jit(solution)/shard_map/ppermute | solution.py:507
  49.1 7.6 %collective-permute-start.8 = (f32[3,6,24,128]{3,2,1,0:T(8,128)S(1)}, f32[3,6,24,128]{3,2,1,0:T(8,128)S(1)}, u32[]{:S(2)}, u32[]{:S(2)}) collective-permute-start(f32[3,6,24,128]{3,2,1,0:T(8,128)S(1)} %pad_maximum_fusion), channel_id=1, source_target_pairs={{0,32},{32,64},{64,96},{96,128},{128,160},{160,192},{192,224},{224... | collective-permute-start | bytes 663560 | tf_op jit(solution)/shard_map/ppermute | solution.py:507
  59.3 19.9 %all-to-all-start = ((f32[32,9,2,128]{3,2,1,0:T(2,128)}), f32[32,9,2,128]{3,2,1,0:T(2,128)S(1)}, u32[]{:S(2)}, u32[]{:S(2)}) async-start(f32[32,9,2,128]{3,2,1,0:T(2,128)} %shard_map.31), calls=%async_computation | async-start | bytes 589824 | tf_op jit(solution)/shard_map/all_to_all | solution.py:544
  71.9 0.7 copy-start.1
  74.1 0.7 copy-start.3
  74.8 0.6 copy-start.5
  75.4 31.7 %copy-start.2 = (f32[2,16,16,128]{3,2,1,0:T(8,128)S(1)}, f32[2,16,16,128]{3,2,1,0:T(8,128)}, u32[]{:S(2)}) copy-start(f32[2,16,16,128]{3,2,1,0:T(8,128)} %copy-done.1) | copy-start | bytes 786436
  79.2 27.9 %copy-start.4 = (f32[2,10,16,128]{3,2,1,0:T(8,128)S(1)}, f32[2,10,16,128]{3,2,1,0:T(8,128)}, u32[]{:S(2)}) copy-start(f32[2,10,16,128]{3,2,1,0:T(8,128)} %copy-done.3) | copy-start | bytes 491524
  79.2 27.9 %copy-start.6 = (f32[12,16,128]{2,1,0:T(8,128)S(1)}, f32[12,16,128]{2,1,0:T(8,128)}, u32[]{:S(2)}) copy-start(f32[12,16,128]{2,1,0:T(8,128)} %copy-done.5) | copy-start | bytes 294916
  80.1 27.0 %all-to-all-start.1 = ((f32[16,48,128]{2,1,0:T(8,128)}), f32[16,48,128]{2,1,0:T(8,128)S(1)}, u32[]{:S(2)}, u32[]{:S(2)}) async-start(f32[16,48,128]{2,1,0:T(8,128)} %shard_map.34), calls=%async_computation.1 | async-start | bytes 786432 | tf_op jit(solution)/shard_map/all_to_all | solution.py:561
  93.2 8.1 %collective-permute-start.10 = (f32[36,4,128]{2,1,0:T(4,128)S(1)}, f32[36,4,128]{2,1,0:T(4,128)S(1)}, u32[]{:S(2)}, u32[]{:S(2)}) collective-permute-start(f32[36,4,128]{2,1,0:T(4,128)S(1)} %shard_map.35.own), channel_id=1, source_target_pairs={{0,32},{32,64},{64,96},{96,128},{128,160},{160,192},{192,224},{224... | collective-permute-start | bytes 221192 | tf_op jit(solution)/shard_map/ppermute | solution.py:507
  96.8 7.9 %collective-permute-start.11 = (f32[36,4,128]{2,1,0:T(4,128)S(1)}, f32[36,4,128]{2,1,0:T(4,128)S(1)}, u32[]{:S(2)}, u32[]{:S(2)}) collective-permute-start(f32[36,4,128]{2,1,0:T(4,128)S(1)} %shard_map.35.own), channel_id=1, source_target_pairs={{32,0},{64,32},{96,64},{128,96},{160,128},{192,160},{224,192},{256... | collective-permute-start | bytes 221192 | tf_op jit(solution)/shard_map/ppermute | solution.py:507

commit v5 on v4

--- a/solution.py
+++ b/solution.py
@@ -170,14 +170,20 @@
     return jnp.where(rule(iota(shape, 0), iota(shape, 1)), value, 0.0).astype(BF16)
 
 
+def ends():
+    at = lax.axis_index("gx")
+    return jnp.where(at > 0, 1.0, 0.0), jnp.where(at < 15, 1.0, 0.0)
+
+
 def assemble(own, ylo, yhi, xlo, xhi, f):
     count, rows, hx, hy = own.shape[1], own.shape[2], xlo.shape[1], ylo.shape[2]
+    low, high = ends()
     for c in range(3):
-        f[c, 0:hx] = xlo[c]
+        f[c, 0:hx] = xlo[c] if c < 2 else xlo[c] * low
         f[c, hx : hx + count, 0:hy] = ylo[c]
         f[c, hx : hx + count, hy : hy + rows] = own[c]
         f[c, hx : hx + count, hy + rows :] = yhi[c]
-        f[c, hx + count :] = xhi[c]
+        f[c, hx + count :] = xhi[c] if c < 2 else xhi[c] * high
 
 
 def start_kernel(source, mach, own, high, low):
@@ -329,10 +335,10 @@
         chunk[:, Y3 * c : Y3 * (c + 1), :] = jnp.broadcast_to(total, (16, Y3, 128))
 
 
-def pick2_kernel(index, parts, sheet):
+def pick2_kernel(parts, sheet):
     for bz in range(3):
         for by in range(3):
-            y, z = index[1] + (by - 1), index[2] + (bz - 1)
+            y, z = lax.axis_index("gy") + (by - 1), lax.axis_index("gz") + (bz - 1)
             inside = (y >= 0) & (y < 8) & (z >= 0) & (z < 4)
             at = jnp.clip(y, 0, 7) * 4 + jnp.clip(z, 0, 3)
             factor = jnp.where(inside, 1.0, 0.0)
@@ -345,7 +351,9 @@
 def window2_kernel(west, own, east, a, planes):
     lane = iota((Y2, 128), 1) // 32
     planes[...] = jnp.zeros_like(planes)
+    low, high = ends()
     for bx, piece in enumerate((west, own, east)):
+        factor = (low, None, high)[bx]
 
         def body(c, _):
             for bz in range(3):
@@ -358,17 +366,17 @@
                     value = planes[bz]
                     value = pltpu.roll(value, step, 1) if step else value
                     total = jnp.where(lane == group, value, total)
-                a[c, 4 * bx + x] = total
+                a[c, 4 * bx + x] = total if factor is None else total * factor
             return 0
 
         lax.fori_loop(0, 4, body, 0)
 
 
 def up_kernel(
-    index, parts3, a, mach2, base1, coef1, base0, coef0, out,
+    parts3, a, mach2, base1, coef1, base0, coef0, out,
     g3, hd3, va3, vb3, s3, g4, hd4, va4, vb4, t4, w3, t3, hd2, va2, vb2, w2, t2, va1, vb1, t1, va0, vb0,
 ):
-    gx, gy, gz = index[0], index[1], index[2]
+    gx, gy, gz = (lax.axis_index(n) for n in ("gx", "gy", "gz"))
     zero3 = jnp.zeros((Y3, 128), F32)
     for ref in (g3, hd3, va3, vb3):
         for c in range(ref.shape[0]):
@@ -487,14 +495,13 @@
     free_loop(3, X0 - 6, coef0, vb0, write0, 0)
 
 
-def call(kernel, outs, scratch, *args, limit=12, memory="", cost=None):
-    memory = memory or "v" * (len(args) + len(outs))
-    specs = [pl.BlockSpec(memory_space=pltpu.SMEM if m == "s" else pltpu.VMEM) for m in memory]
+def call(kernel, outs, scratch, *args, limit=12, cost=None):
+    spec = pl.BlockSpec(memory_space=pltpu.VMEM)
     return pl.pallas_call(
         kernel,
         out_shape=[jax.ShapeDtypeStruct(s, F32) for s in outs],
-        in_specs=specs[: len(args)],
-        out_specs=specs[len(args) :],
+        in_specs=[spec] * len(args),
+        out_specs=[spec] * len(outs),
         scratch_shapes=[pltpu.VMEM(s, F32) for s in scratch],
         compiler_params=pltpu.CompilerParams(vmem_limit_bytes=limit << 20),
         cost_estimate=cost and pl.CostEstimate(cost[0], 0, cost[1]),
@@ -503,7 +510,9 @@
 
 def shift(block, axis, step):
     count = lax.axis_size(axis)
-    pairs = [(i, i + step) for i in range(count) if 0 <= i + step < count]
+    pairs = [(i, (i + step) % count) for i in range(count)]
+    if axis != "gx":
+        pairs = [(i, j) for i, j in pairs if j == i + step]
     return lax.ppermute(block, axis, pairs)
 
 
@@ -525,7 +534,12 @@
     edge = (3, 16, 4, 128)
     start = call(start_kernel, [(3, 16, 16, 128), edge, edge], [], source_field, mach_number)
     flat = (16, 3 * X0 * Y0)
-    f0, low, high = call(gather0_kernel, [(3, X0, Y0, 128), flat, flat], [], *halos(*start, 3))
+    f0, low, high = call(
+        gather0_kernel,
+        [(3, X0, Y0, 128), flat, flat],
+        [],
+        *halos(*start, 3),
+    )
     full0, full1 = (X0, Y0, L0), (X1, Y1, L1)
     block0 = (f0, shift(high, "gz", 1), shift(low, "gz", -1))
     smoothed0 = [(3,) + full0] + [(2,) + full0] * 3
@@ -559,11 +573,14 @@
     parts2, *kept = lax.optimization_barrier((parts2, mach2, base1, coef1, base0, coef0))
     (chunk3,) = call(spread3_kernel, [(16, 48, 128)], [(4, Y3, 128)], parts2)
     parts3 = lax.all_to_all(chunk3, "gx", 0, 0)
-    index = jnp.stack([lax.axis_index(n) for n in ("gx", "gy", "gz")]).astype(jnp.int32)
-    (sheet,) = call(pick2_kernel, [(36, 4, 128)], [], index, parts2, memory="svv")
+    (sheet,) = call(pick2_kernel, [(36, 4, 128)], [], parts2)
     west, east = around(sheet, "gx")
     (a,) = call(
-        window2_kernel, [(4, X2, Y2, 128)], [(3, Y2, 128)], west, sheet, east, cost=(4 << 20, 1 << 20)
+        window2_kernel,
+        [(4, X2, Y2, 128)],
+        [(3, Y2, 128)],
+        west, sheet, east,
+        cost=(4 << 20, 1 << 20),
     )
     wide3 = (X3 + 2 * PAD3, Y3, 128)
     wide4 = (X4 + 2, Y4, 128)
@@ -576,9 +593,8 @@
         up_kernel,
         [(2, 16, 16, 128)],
         scratch,
-        index, parts3, a, *kept,
+        parts3, a, *kept,
         limit=16,
-        memory="svvvvvvvv",
     )[0]
 
 

time: 115 us -> 106 us (0.922)
  starting transfers between devices: 57.1 us -> 46.9 us
  waiting for transfers between devices: 31.8 us -> 34.8 us
    ppermute x12, starting transfers between devices: 35.6 us -> 27.3 us  [shift(): return lax.ppermute(block, axis, pairs)]
    ppermute x12, waiting for transfers between devices: 26.6 us -> 29.7 us  [shift(): return lax.ppermute(block, axis, pairs)]
    all_to_all x1, starting transfers between devices: 12.4 us -> 10.7 us  [shards(): parts3 = lax.all_to_all(chunk3, 'gx', 0, 0)]
  transfers between devices with their start and end apart: 14 -> 14, of which waited for: 13 -> 14; matrix products, arithmetic and copies ran while one was open for 0% -> 0% of each run, Pallas kernels for 6% -> 6%
where the time goes in v5:
time: 106 us
  starting transfers between devices  46.9 us (44%)
  waiting for transfers between devices  34.8 us (33%)
  Pallas kernels  19.9 us (19%)
  local copies, waits for them, and re-layouts  3.84 us (4%)
    ppermute x12, waiting for transfers between devices, shift(): return lax.ppermute(block, axis, pairs)  29.7 us
    ppermute x12, starting transfers between devices, shift(): return lax.ppermute(block, axis, pairs)  27.3 us
    pallas_call x10, Pallas kernels, call(): pl.pallas_call(kernel, out_shape=[jax.ShapeDtypeStruct(s, F32) for s in o...  19.9 us
    all_to_all x1, starting transfers between devices, shards(): parts3 = lax.all_to_all(chunk3, 'gx', 0, 0)  10.7 us
    all_to_all x1, starting transfers between devices, shards(): parts2 = lax.all_to_all(chunk2, ('gy', 'gz'), 0, 0)  8.85 us
    all_to_all x1, waiting for transfers between devices, shards(): parts2 = lax.all_to_all(chunk2, ('gy', 'gz'), 0, 0)  3.79 us
    unnamed x16, local copies, waits for them, and re-layouts  3.78 us
  transfers between devices with their start and end apart: 14, of which 14 were waited for; matrix products, arithmetic and copies ran while one was open for 0% of the time, Pallas kernels for 6%

profile of v5, /device:TPU:1, one launch (start us, length us, event | category | flops | bytes accessed | tf_op | source)
XLA Modules:
  0.0 105.7 jit_solution(11901470448378169334)
XLA Ops:
  0.0 0.0 copy-start.2
  0.0 0.9 copy-done.2
  1.0 0.8 copy-done.7
  1.8 0.1 shard_map.28
  1.9 4.8 %collective-permute-start = (f32[3,16,4,128]{3,2,1,0:T(4,128)S(1)}, f32[3,16,4,128]{3,2,1,0:T(4,128)S(1)}, u32[]{:S(2)}, u32[]{:S(2)}) collective-permute-start(f32[3,16,4,128]{3,2,1,0:T(4,128)S(1)} %get-tuple-element.23), channel_id=1, source_target_pairs={{0,4},{4,8},{8,12},{12,16},{16,20},{20,24},{24,28},{1,5},{5,9},{9,... | collective-permute-start | bytes 294920 | tf_op jit(solution)/shard_map/ppermute | solution.py:516
  6.7 1.3 %collective-permute-start.1 = (f32[3,16,4,128]{3,2,1,0:T(4,128)S(1)}, f32[3,16,4,128]{3,2,1,0:T(4,128)S(1)}, u32[]{:S(2)}, u32[]{:S(2)}) collective-permute-start(f32[3,16,4,128]{3,2,1,0:T(4,128)S(1)} %get-tuple-element.24), channel_id=1, source_target_pairs={{4,0},{8,4},{12,8},{16,12},{20,16},{24,20},{28,24},{5,1},{9,5},{13... | collective-permute-start | bytes 294920 | tf_op jit(solution)/shard_map/ppermute | solution.py:516
  8.0 0.3 collective-permute-done.ylo
  8.3 4.4 %collective-permute-done.1.yhi = f32[3,16,4,128]{3,2,1,0:T(4,128)S(1)} collective-permute-done((f32[3,16,4,128]{3,2,1,0:T(4,128)S(1)}, f32[3,16,4,128]{3,2,1,0:T(4,128)S(1)}, u32[]{:S(2)}, u32[]{:S(2)}) %collective-permute-start.1) | collective-permute-done | bytes 98336 | tf_op jit(solution)/shard_map/ppermute | solution.py:516
  12.7 3.9 %collective-permute-start.3 = (f32[3,3,24,128]{3,2,1,0:T(8,128)S(1)}, f32[3,3,24,128]{3,2,1,0:T(8,128)S(1)}, u32[]{:S(2)}, u32[]{:S(2)}) collective-permute-start(f32[3,3,24,128]{3,2,1,0:T(8,128)S(1)} %pad_maximum_fusion.3), channel_id=1, source_target_pairs={{0,480},{32,0},{64,32},{96,64},{128,96},{160,128},{192,160},{224,1... | collective-permute-start | bytes 331784 | tf_op jit(solution)/shard_map/ppermute | solution.py:516
  16.6 0.0 collective-permute-start.2
  16.6 1.5 %collective-permute-done.3.xhi = f32[3,3,24,128]{3,2,1,0:T(8,128)S(1)} collective-permute-done((f32[3,3,24,128]{3,2,1,0:T(8,128)S(1)}, f32[3,3,24,128]{3,2,1,0:T(8,128)S(1)}, u32[]{:S(2)}, u32[]{:S(2)}) %collective-permute-start.3) | collective-permute-done | bytes 110624 | tf_op jit(solution)/shard_map/ppermute | solution.py:516
  18.2 0.2 collective-permute-done.2.xlo
  18.4 0.8 shard_map.29
  19.2 2.9 %collective-permute-start.4 = (f32[16,1584]{1,0:T(8,128)S(1)}, f32[16,1584]{1,0:T(8,128)S(1)}, u32[]{:S(2)}, u32[]{:S(2)}) collective-permute-start(f32[16,1584]{1,0:T(8,128)S(1)} %get-tuple-element.26), channel_id=1, source_target_pairs={{0,1},{1,2},{2,3},{4,5},{5,6},{6,7},{8,9},{9,10},{10,11},{12,13},{... | collective-permute-start | bytes 304136 | tf_op jit(solution)/shard_map/ppermute | solution.py:516
  22.1 1.3 %collective-permute-start.5 = (f32[16,1584]{1,0:T(8,128)S(1)}, f32[16,1584]{1,0:T(8,128)S(1)}, u32[]{:S(2)}, u32[]{:S(2)}) collective-permute-start(f32[16,1584]{1,0:T(8,128)S(1)} %get-tuple-element.27), channel_id=1, source_target_pairs={{1,0},{2,1},{3,2},{5,4},{6,5},{7,6},{9,8},{10,9},{11,10},{13,12},{... | collective-permute-start | bytes 304136 | tf_op jit(solution)/shard_map/ppermute | solution.py:516
  23.4 0.4 collective-permute-done.4.lower
  23.8 3.8 %collective-permute-done.5.upper = f32[16,1584]{1,0:T(8,128)S(1)} collective-permute-done((f32[16,1584]{1,0:T(8,128)S(1)}, f32[16,1584]{1,0:T(8,128)S(1)}, u32[]{:S(2)}, u32[]{:S(2)}) %collective-permute-start.5) | collective-permute-done | bytes 101408 | tf_op jit(solution)/shard_map/ppermute | solution.py:516
  27.6 3.0 %shard_map.30.own = f32[3,8,8,128]{3,2,1,0:T(8,128)S(1)} custom-call(f32[3,22,24,128]{3,2,1,0:T(8,128)S(1)} %get-tuple-element.25.f, f32[16,1584]{1,0:T(8,128)S(1)} %collective-permute-done.4.lower, f32[16,1584]{1,0:T(8,128)S(1)} %collective-permute-done.5.upper), custom_call_target="tpu_custom_call" | custom-call | tf_op jit(solution)/shard_map/pallas_call | solution.py:500
  30.6 4.0 %collective-permute-start.6 = (f32[3,8,8,128]{3,2,1,0:T(8,128)S(1)}, f32[3,8,8,128]{3,2,1,0:T(8,128)S(1)}, u32[]{:S(2)}, u32[]{:S(2)}) collective-permute-start(f32[3,8,8,128]{3,2,1,0:T(8,128)S(1)} %shard_map.30.own), channel_id=1, source_target_pairs={{0,4},{4,8},{8,12},{12,16},{16,20},{20,24},{24,28},{1,5},{5,9},{9,... | collective-permute-start | bytes 294920 | tf_op jit(solution)/shard_map/ppermute | solution.py:516
  34.6 1.3 %collective-permute-start.7 = (f32[3,8,8,128]{3,2,1,0:T(8,128)S(1)}, f32[3,8,8,128]{3,2,1,0:T(8,128)S(1)}, u32[]{:S(2)}, u32[]{:S(2)}) collective-permute-start(f32[3,8,8,128]{3,2,1,0:T(8,128)S(1)} %shard_map.30.own), channel_id=1, source_target_pairs={{4,0},{8,4},{12,8},{16,12},{20,16},{24,20},{28,24},{5,1},{9,5},{13... | collective-permute-start | bytes 294920 | tf_op jit(solution)/shard_map/ppermute | solution.py:516
  35.9 0.3 collective-permute-done.6.ylo
  36.2 5.6 %collective-permute-done.7.yhi = f32[3,8,8,128]{3,2,1,0:T(8,128)S(1)} collective-permute-done((f32[3,8,8,128]{3,2,1,0:T(8,128)S(1)}, f32[3,8,8,128]{3,2,1,0:T(8,128)S(1)}, u32[]{:S(2)}, u32[]{:S(2)}) %collective-permute-start.7) | collective-permute-done | bytes 98336 | tf_op jit(solution)/shard_map/ppermute | solution.py:516
  41.9 6.2 %collective-permute-start.9 = (f32[3,6,24,128]{3,2,1,0:T(8,128)S(1)}, f32[3,6,24,128]{3,2,1,0:T(8,128)S(1)}, u32[]{:S(2)}, u32[]{:S(2)}) collective-permute-start(f32[3,6,24,128]{3,2,1,0:T(8,128)S(1)} %pad_maximum_fusion.1), channel_id=1, source_target_pairs={{0,480},{32,0},{64,32},{96,64},{128,96},{160,128},{192,160},{224,1... | collective-permute-start | bytes 663560 | tf_op jit(solution)/shard_map/ppermute | solution.py:516
  48.0 0.0 collective-permute-start.8
  48.1 1.8 %collective-permute-done.9.xhi = f32[3,6,24,128]{3,2,1,0:T(8,128)S(1)} collective-permute-done((f32[3,6,24,128]{3,2,1,0:T(8,128)S(1)}, f32[3,6,24,128]{3,2,1,0:T(8,128)S(1)}, u32[]{:S(2)}, u32[]{:S(2)}) %collective-permute-start.9) | collective-permute-done | bytes 221216 | tf_op jit(solution)/shard_map/ppermute | solution.py:516
  49.9 1.1 %collective-permute-done.8.xlo = f32[3,6,24,128]{3,2,1,0:T(8,128)S(1)} collective-permute-done((f32[3,6,24,128]{3,2,1,0:T(8,128)S(1)}, f32[3,6,24,128]{3,2,1,0:T(8,128)S(1)}, u32[]{:S(2)}, u32[]{:S(2)}) %collective-permute-start.8) | collective-permute-done | bytes 221216 | tf_op jit(solution)/shard_map/ppermute | solution.py:516
  50.9 2.5 %shard_map.31 = f32[32,9,2,128]{3,2,1,0:T(2,128)} custom-call(f32[3,8,8,128]{3,2,1,0:T(8,128)S(1)} %shard_map.30.own, f32[3,8,8,128]{3,2,1,0:T(8,128)S(1)} %collective-permute-done.6.ylo, f32[3,8,8,128]{3,2,1,0:T(8,128)S(1)} %collective-permute-done.7.yhi, f32[3,6,24,128]{3,2,1,0:T(8,128)S(1)} %collective-permute-done.8.xlo, ...), custom_call_target="tpu_custom_call" | custom-call | tf_op jit(solution)/shard_map/pallas_call | solution.py:500
  53.5 8.9 %all-to-all-start = ((f32[32,9,2,128]{3,2,1,0:T(2,128)}), f32[32,9,2,128]{3,2,1,0:T(2,128)S(1)}, u32[]{:S(2)}, u32[]{:S(2)}) async-start(f32[32,9,2,128]{3,2,1,0:T(2,128)} %shard_map.31), calls=%async_computation | async-start | bytes 589824 | tf_op jit(solution)/shard_map/all_to_all | solution.py:558
  62.3 3.5 %shard_map.33 = (f32[2,16,16,128]{3,2,1,0:T(8,128)S(1)}, f32[3,18,24,256]{3,2,1,0:T(8,128)S(1)}) custom-call(f32[3,22,24,128]{3,2,1,0:T(8,128)S(1)} %get-tuple-element.25.f, f32[16,1584]{1,0:T(8,128)S(1)} %collective-permute-done.4.lower, f32[16,1584]{1,0:T(8,128)S(1)} %collective-permute-done.5.upper), custom_call_target="tpu_custom_call" | custom-call | flops 62914560 | bytes 8388608 | tf_op jit(solution)/shard_map/pallas_call | solution.py:500
  65.8 0.0 copy-start
  65.8 0.7 copy-done
  66.5 1.5 %shard_map.32 = (f32[2,10,16,128]{3,2,1,0:T(8,128)S(1)}, f32[3,12,16,128]{3,2,1,0:T(8,128)S(1)}, f32[12,16,128]{2,1,0:T(8,128)S(1)}) custom-call(f32[3,8,8,128]{3,2,1,0:T(8,128)S(1)} %shard_map.30.own, f32[3,8,8,128]{3,2,1,0:T(8,128)S(1)} %collective-permute-done.6.ylo, f32[3,8,8,128]{3,2,1,0:T(8,128)S(1)} %collective-permute-done.7.yhi, ...), custom_call_target="tpu_custom_call" | custom-call | flops 8388608 | bytes 1048576 | tf_op jit(solution)/shard_map/pallas_call | solution.py:500
  68.0 0.0 copy-start.3
  68.0 0.7 copy-done.3
  68.7 0.6 copy-done.5
  69.3 3.8 %all-to-all-done.parts = f32[32,9,2,128]{3,2,1,0:T(2,128)S(1)} async-done(((f32[32,9,2,128]{3,2,1,0:T(2,128)}), f32[32,9,2,128]{3,2,1,0:T(2,128)S(1)}, u32[]{:S(2)}, u32[]{:S(2)}) %all-to-all-start) | async-done | bytes 294944 | tf_op jit(solution)/shard_map/all_to_all | solution.py:558
  73.1 0.9 shard_map.34
  74.0 10.7 %all-to-all-start.1 = ((f32[16,48,128]{2,1,0:T(8,128)}), f32[16,48,128]{2,1,0:T(8,128)S(1)}, u32[]{:S(2)}, u32[]{:S(2)}) async-start(f32[16,48,128]{2,1,0:T(8,128)} %shard_map.34), calls=%async_computation.1 | async-start | bytes 786432 | tf_op jit(solution)/shard_map/all_to_all | solution.py:575
  84.7 1.6 %collective-permute-start.10 = (f32[36,4,128]{2,1,0:T(4,128)S(1)}, f32[36,4,128]{2,1,0:T(4,128)S(1)}, u32[]{:S(2)}, u32[]{:S(2)}) collective-permute-start(f32[36,4,128]{2,1,0:T(4,128)S(1)} %shard_map.35.own), channel_id=1, source_target_pairs={{0,32},{32,64},{64,96},{96,128},{128,160},{160,192},{192,224},{224... | collective-permute-start | bytes 221192 | tf_op jit(solution)/shard_map/ppermute | solution.py:516
  86.4 0.0 collective-permute-start.11
  86.4 7.1 %collective-permute-done.10.west = f32[36,4,128]{2,1,0:T(4,128)S(1)} collective-permute-done((f32[36,4,128]{2,1,0:T(4,128)S(1)}, f32[36,4,128]{2,1,0:T(4,128)S(1)}, u32[]{:S(2)}, u32[]{:S(2)}) %collective-permute-start.10) | collective-permute-done | bytes 73760 | tf_op jit(solution)/shard_map/ppermute | solution.py:516
  93.4 3.4 %collective-permute-done.11.east = f32[36,4,128]{2,1,0:T(4,128)S(1)} collective-permute-done((f32[36,4,128]{2,1,0:T(4,128)S(1)}, f32[36,4,128]{2,1,0:T(4,128)S(1)}, u32[]{:S(2)}, u32[]{:S(2)}) %collective-permute-start.11) | collective-permute-done | bytes 73760 | tf_op jit(solution)/shard_map/ppermute | solution.py:516
  96.8 1.1 %shard_map.36.a = f32[4,12,16,128]{3,2,1,0:T(8,128)S(1)} custom-call(f32[36,4,128]{2,1,0:T(4,128)S(1)} %collective-permute-done.10.west, f32[36,4,128]{2,1,0:T(4,128)S(1)} %shard_map.35.own, f32[36,4,128]{2,1,0:T(4,128)S(1)} %collective-permute-done.11.east), custom_call_target="tpu_custom_call" | custom-call | flops 4194304 | bytes 1048576 | tf_op jit(solution)/shard_map/pallas_call | solution.py:500
  97.9 1.3 %all-to-all-done.1.parts3 = f32[16,48,128]{2,1,0:T(8,128)S(1)} async-done(((f32[16,48,128]{2,1,0:T(8,128)}), f32[16,48,128]{2,1,0:T(8,128)S(1)}, u32[]{:S(2)}, u32[]{:S(2)}) %all-to-all-start.1) | async-done | bytes 393248 | tf_op jit(solution)/shard_map/all_to_all | solution.py:575
  99.2 0.0 copy-done.1
  99.2 0.0 copy-done.4
  99.2 0.0 copy-done.6
  99.2 6.5 %shard_map.37 = f32[2,16,16,128]{3,2,1,0:T(8,128)} custom-call(f32[16,48,128]{2,1,0:T(8,128)S(1)} %all-to-all-done.1.parts3, f32[4,12,16,128]{3,2,1,0:T(8,128)S(1)} %shard_map.36.a, f32[12,16,128]{2,1,0:T(8,128)S(1)} %copy-done.6, f32[2,10,16,128]{3,2,1,0:T(8,128)S(1)} %copy-done.4, f32[3,12,16,128]{3,2,1,0:T(8,128)S(1)} %get-tuple-element.36.coef1, ...), custom_call_target="tpu_custom_call" | custom-call | tf_op jit(solution)/shard_map/pallas_call | solution.py:500
  (16 shorter events, 0.2 us)
Async XLA Ops:
  0.0 0.9 copy-start.2
  1.0 0.8 copy-start.7
  1.9 6.5 %collective-permute-start = (f32[3,16,4,128]{3,2,1,0:T(4,128)S(1)}, f32[3,16,4,128]{3,2,1,0:T(4,128)S(1)}, u32[]{:S(2)}, u32[]{:S(2)}) collective-permute-start(f32[3,16,4,128]{3,2,1,0:T(4,128)S(1)} %get-tuple-element.23), channel_id=1, source_target_pairs={{0,4},{4,8},{8,12},{12,16},{16,20},{20,24},{24,28},{1,5},{5,9},{9,... | collective-permute-start | bytes 294920 | tf_op jit(solution)/shard_map/ppermute | solution.py:516
  6.7 6.0 %collective-permute-start.1 = (f32[3,16,4,128]{3,2,1,0:T(4,128)S(1)}, f32[3,16,4,128]{3,2,1,0:T(4,128)S(1)}, u32[]{:S(2)}, u32[]{:S(2)}) collective-permute-start(f32[3,16,4,128]{3,2,1,0:T(4,128)S(1)} %get-tuple-element.24), channel_id=1, source_target_pairs={{4,0},{8,4},{12,8},{16,12},{20,16},{24,20},{28,24},{5,1},{9,5},{13... | collective-permute-start | bytes 294920 | tf_op jit(solution)/shard_map/ppermute | solution.py:516
  12.7 5.5 %collective-permute-start.3 = (f32[3,3,24,128]{3,2,1,0:T(8,128)S(1)}, f32[3,3,24,128]{3,2,1,0:T(8,128)S(1)}, u32[]{:S(2)}, u32[]{:S(2)}) collective-permute-start(f32[3,3,24,128]{3,2,1,0:T(8,128)S(1)} %pad_maximum_fusion.3), channel_id=1, source_target_pairs={{0,480},{32,0},{64,32},{96,64},{128,96},{160,128},{192,160},{224,1... | collective-permute-start | bytes 331784 | tf_op jit(solution)/shard_map/ppermute | solution.py:516
  16.6 1.8 %collective-permute-start.2 = (f32[3,3,24,128]{3,2,1,0:T(8,128)S(1)}, f32[3,3,24,128]{3,2,1,0:T(8,128)S(1)}, u32[]{:S(2)}, u32[]{:S(2)}) collective-permute-start(f32[3,3,24,128]{3,2,1,0:T(8,128)S(1)} %pad_maximum_fusion.2), channel_id=1, source_target_pairs={{0,32},{32,64},{64,96},{96,128},{128,160},{160,192},{192,224},{224... | collective-permute-start | bytes 331784 | tf_op jit(solution)/shard_map/ppermute | solution.py:516
  19.2 4.6 %collective-permute-start.4 = (f32[16,1584]{1,0:T(8,128)S(1)}, f32[16,1584]{1,0:T(8,128)S(1)}, u32[]{:S(2)}, u32[]{:S(2)}) collective-permute-start(f32[16,1584]{1,0:T(8,128)S(1)} %get-tuple-element.26), channel_id=1, source_target_pairs={{0,1},{1,2},{2,3},{4,5},{5,6},{6,7},{8,9},{9,10},{10,11},{12,13},{... | collective-permute-start | bytes 304136 | tf_op jit(solution)/shard_map/ppermute | solution.py:516
  22.1 5.4 %collective-permute-start.5 = (f32[16,1584]{1,0:T(8,128)S(1)}, f32[16,1584]{1,0:T(8,128)S(1)}, u32[]{:S(2)}, u32[]{:S(2)}) collective-permute-start(f32[16,1584]{1,0:T(8,128)S(1)} %get-tuple-element.27), channel_id=1, source_target_pairs={{1,0},{2,1},{3,2},{5,4},{6,5},{7,6},{9,8},{10,9},{11,10},{13,12},{... | collective-permute-start | bytes 304136 | tf_op jit(solution)/shard_map/ppermute | solution.py:516
  30.6 5.6 %collective-permute-start.6 = (f32[3,8,8,128]{3,2,1,0:T(8,128)S(1)}, f32[3,8,8,128]{3,2,1,0:T(8,128)S(1)}, u32[]{:S(2)}, u32[]{:S(2)}) collective-permute-start(f32[3,8,8,128]{3,2,1,0:T(8,128)S(1)} %shard_map.30.own), channel_id=1, source_target_pairs={{0,4},{4,8},{8,12},{12,16},{16,20},{20,24},{24,28},{1,5},{5,9},{9,... | collective-permute-start | bytes 294920 | tf_op jit(solution)/shard_map/ppermute | solution.py:516
  34.6 7.2 %collective-permute-start.7 = (f32[3,8,8,128]{3,2,1,0:T(8,128)S(1)}, f32[3,8,8,128]{3,2,1,0:T(8,128)S(1)}, u32[]{:S(2)}, u32[]{:S(2)}) collective-permute-start(f32[3,8,8,128]{3,2,1,0:T(8,128)S(1)} %shard_map.30.own), channel_id=1, source_target_pairs={{4,0},{8,4},{12,8},{16,12},{20,16},{24,20},{28,24},{5,1},{9,5},{13... | collective-permute-start | bytes 294920 | tf_op jit(solution)/shard_map/ppermute | solution.py:516
  41.9 8.0 %collective-permute-start.9 = (f32[3,6,24,128]{3,2,1,0:T(8,128)S(1)}, f32[3,6,24,128]{3,2,1,0:T(8,128)S(1)}, u32[]{:S(2)}, u32[]{:S(2)}) collective-permute-start(f32[3,6,24,128]{3,2,1,0:T(8,128)S(1)} %pad_maximum_fusion.1), channel_id=1, source_target_pairs={{0,480},{32,0},{64,32},{96,64},{128,96},{160,128},{192,160},{224,1... | collective-permute-start | bytes 663560 | tf_op jit(solution)/shard_map/ppermute | solution.py:516
  48.0 2.9 %collective-permute-start.8 = (f32[3,6,24,128]{3,2,1,0:T(8,128)S(1)}, f32[3,6,24,128]{3,2,1,0:T(8,128)S(1)}, u32[]{:S(2)}, u32[]{:S(2)}) collective-permute-start(f32[3,6,24,128]{3,2,1,0:T(8,128)S(1)} %pad_maximum_fusion), channel_id=1, source_target_pairs={{0,32},{32,64},{64,96},{96,128},{128,160},{160,192},{192,224},{224... | collective-permute-start | bytes 663560 | tf_op jit(solution)/shard_map/ppermute | solution.py:516
  53.5 19.6 %all-to-all-start = ((f32[32,9,2,128]{3,2,1,0:T(2,128)}), f32[32,9,2,128]{3,2,1,0:T(2,128)S(1)}, u32[]{:S(2)}, u32[]{:S(2)}) async-start(f32[32,9,2,128]{3,2,1,0:T(2,128)} %shard_map.31), calls=%async_computation | async-start | bytes 589824 | tf_op jit(solution)/shard_map/all_to_all | solution.py:558
  65.8 0.7 copy-start
  68.0 0.7 copy-start.3
  68.7 0.6 copy-start.5
  69.3 29.9 %copy-start.1 = (f32[2,16,16,128]{3,2,1,0:T(8,128)S(1)}, f32[2,16,16,128]{3,2,1,0:T(8,128)}, u32[]{:S(2)}) copy-start(f32[2,16,16,128]{3,2,1,0:T(8,128)} %copy-done) | copy-start | bytes 786436
  73.1 26.2 %copy-start.4 = (f32[2,10,16,128]{3,2,1,0:T(8,128)S(1)}, f32[2,10,16,128]{3,2,1,0:T(8,128)}, u32[]{:S(2)}) copy-start(f32[2,10,16,128]{3,2,1,0:T(8,128)} %copy-done.3) | copy-start | bytes 491524
  73.1 26.2 %copy-start.6 = (f32[12,16,128]{2,1,0:T(8,128)S(1)}, f32[12,16,128]{2,1,0:T(8,128)}, u32[]{:S(2)}) copy-start(f32[12,16,128]{2,1,0:T(8,128)} %copy-done.5) | copy-start | bytes 294916
  74.0 25.3 %all-to-all-start.1 = ((f32[16,48,128]{2,1,0:T(8,128)}), f32[16,48,128]{2,1,0:T(8,128)S(1)}, u32[]{:S(2)}, u32[]{:S(2)}) async-start(f32[16,48,128]{2,1,0:T(8,128)} %shard_map.34), calls=%async_computation.1 | async-start | bytes 786432 | tf_op jit(solution)/shard_map/all_to_all | solution.py:575
  84.7 8.7 %collective-permute-start.10 = (f32[36,4,128]{2,1,0:T(4,128)S(1)}, f32[36,4,128]{2,1,0:T(4,128)S(1)}, u32[]{:S(2)}, u32[]{:S(2)}) collective-permute-start(f32[36,4,128]{2,1,0:T(4,128)S(1)} %shard_map.35.own), channel_id=1, source_target_pairs={{0,32},{32,64},{64,96},{96,128},{128,160},{160,192},{192,224},{224... | collective-permute-start | bytes 221192 | tf_op jit(solution)/shard_map/ppermute | solution.py:516
  86.4 10.4 %collective-permute-start.11 = (f32[36,4,128]{2,1,0:T(4,128)S(1)}, f32[36,4,128]{2,1,0:T(4,128)S(1)}, u32[]{:S(2)}, u32[]{:S(2)}) collective-permute-start(f32[36,4,128]{2,1,0:T(4,128)S(1)} %shard_map.35.own), channel_id=1, source_target_pairs={{0,480},{32,0},{64,32},{96,64},{128,96},{160,128},{192,160},{224,1... | collective-permute-start | bytes 221192 | tf_op jit(solution)/shard_map/ppermute | solution.py:516

commit v6 on v5

--- a/solution.py
+++ b/solution.py
@@ -556,6 +556,8 @@
         *block1,
     )
     parts2 = lax.all_to_all(chunk2, ("gy", "gz"), 0, 0)
+    (chunk3,) = call(spread3_kernel, [(16, 48, 128)], [(4, Y3, 128)], parts2)
+    chunk3, block0, block1 = lax.optimization_barrier((chunk3, block0, tuple(block1)))
     base0, coef0 = call(
         keep0_kernel,
         [(2, 16, 16, 128), (3, 18, Y0, L0)],
@@ -570,8 +572,7 @@
         *block1,
         cost=(8 << 20, 1 << 20),
     )
-    parts2, *kept = lax.optimization_barrier((parts2, mach2, base1, coef1, base0, coef0))
-    (chunk3,) = call(spread3_kernel, [(16, 48, 128)], [(4, Y3, 128)], parts2)
+    kept = (mach2, base1, coef1, base0, coef0)
     parts3 = lax.all_to_all(chunk3, "gx", 0, 0)
     (sheet,) = call(pick2_kernel, [(36, 4, 128)], [], parts2)
     west, east = around(sheet, "gx")

time: 106 us -> 110 us (1.038)
  blocking collectives: 0 us -> 27.2 us
  starting transfers between devices: 46.9 us -> 33.1 us
  waiting for transfers between devices: 34.8 us -> 26.7 us
    all_to_all x0 -> x1, blocking collectives: none -> 27.2 us  [shards(): parts2 = lax.all_to_all(chunk2, ('gy', 'gz'), 0, 0)]
    all_to_all x1 -> x0, starting transfers between devices: 8.85 us -> none  [shards(): parts2 = lax.all_to_all(chunk2, ('gy', 'gz'), 0, 0)]
    ppermute x12, waiting for transfers between devices: 29.7 us -> 25.4 us  [shift(): return lax.ppermute(block, axis, pairs)]
    all_to_all x1 -> x0, waiting for transfers between devices: 3.79 us -> none  [shards(): parts2 = lax.all_to_all(chunk2, ('gy', 'gz'), 0, 0)]
    ppermute x12, starting transfers between devices: 27.3 us -> 24.6 us  [shift(): return lax.ppermute(block, axis, pairs)]
    all_to_all x1, starting transfers between devices: 10.7 us -> 8.45 us  [shards(): parts3 = lax.all_to_all(chunk3, 'gx', 0, 0)]
    unnamed x16 -> x8, local copies, waits for them, and re-layouts: 3.78 us -> 2.71 us
  transfers between devices with their start and end apart: 14 -> 13, of which waited for: 14 -> 11; matrix products, arithmetic and copies ran while one was open for 0% -> 0% of each run, Pallas kernels for 6% -> 6%
where the time goes in v6:
time: 110 us; the launch traced here: 109 us
  starting transfers between devices  33.1 us (30%)
  blocking collectives  27.2 us (25%)
  waiting for transfers between devices  26.7 us (24%)
  Pallas kernels  19.2 us (17%)
  local copies, waits for them, and re-layouts  2.77 us (3%)
    all_to_all x1, blocking collectives, shards(): parts2 = lax.all_to_all(chunk2, ('gy', 'gz'), 0, 0)  27.2 us
    ppermute x12, waiting for transfers between devices, shift(): return lax.ppermute(block, axis, pairs)  25.4 us
    ppermute x12, starting transfers between devices, shift(): return lax.ppermute(block, axis, pairs)  24.6 us
    pallas_call x10, Pallas kernels, call(): pl.pallas_call(kernel, out_shape=[jax.ShapeDtypeStruct(s, F32) for s in o...  19.2 us
    all_to_all x1, starting transfers between devices, shards(): parts3 = lax.all_to_all(chunk3, 'gx', 0, 0)  8.45 us
    unnamed x8, local copies, waits for them, and re-layouts  2.71 us
  transfers between devices with their start and end apart: 13, of which 11 were waited for; matrix products, arithmetic and copies ran while one was open for 0% of the time, Pallas kernels for 6%

profile of v6, /device:TPU:1, one launch (start us, length us, event | category | flops | bytes accessed | tf_op | source)
XLA Modules:
  0.0 109.2 jit_solution(1007706254099489229)
XLA Ops:
  0.0 0.0 copy-start
  0.0 0.9 copy-done
  1.0 0.0 copy-start.3
  1.0 0.8 copy-done.3
  1.8 0.1 shard_map.28
  1.9 4.8 %collective-permute-start = (f32[3,16,4,128]{3,2,1,0:T(4,128)S(1)}, f32[3,16,4,128]{3,2,1,0:T(4,128)S(1)}, u32[]{:S(2)}, u32[]{:S(2)}) collective-permute-start(f32[3,16,4,128]{3,2,1,0:T(4,128)S(1)} %get-tuple-element.26), channel_id=1, source_target_pairs={{0,4},{4,8},{8,12},{12,16},{16,20},{20,24},{24,28},{1,5},{5,9},{9,... | collective-permute-start | bytes 294920 | tf_op jit(solution)/shard_map/ppermute | solution.py:516
  6.7 1.3 %collective-permute-start.1 = (f32[3,16,4,128]{3,2,1,0:T(4,128)S(1)}, f32[3,16,4,128]{3,2,1,0:T(4,128)S(1)}, u32[]{:S(2)}, u32[]{:S(2)}) collective-permute-start(f32[3,16,4,128]{3,2,1,0:T(4,128)S(1)} %get-tuple-element.27), channel_id=1, source_target_pairs={{4,0},{8,4},{12,8},{16,12},{20,16},{24,20},{28,24},{5,1},{9,5},{13... | collective-permute-start | bytes 294920 | tf_op jit(solution)/shard_map/ppermute | solution.py:516
  8.0 0.3 collective-permute-done.ylo
  8.3 4.4 %collective-permute-done.1.yhi = f32[3,16,4,128]{3,2,1,0:T(4,128)S(1)} collective-permute-done((f32[3,16,4,128]{3,2,1,0:T(4,128)S(1)}, f32[3,16,4,128]{3,2,1,0:T(4,128)S(1)}, u32[]{:S(2)}, u32[]{:S(2)}) %collective-permute-start.1) | collective-permute-done | bytes 98336 | tf_op jit(solution)/shard_map/ppermute | solution.py:516
  12.7 3.0 %collective-permute-start.2 = (f32[3,3,24,128]{3,2,1,0:T(8,128)S(1)}, f32[3,3,24,128]{3,2,1,0:T(8,128)S(1)}, u32[]{:S(2)}, u32[]{:S(2)}) collective-permute-start(f32[3,3,24,128]{3,2,1,0:T(8,128)S(1)} %pad_maximum_fusion.2), channel_id=1, source_target_pairs={{0,32},{32,64},{64,96},{96,128},{128,160},{160,192},{192,224},{224... | collective-permute-start | bytes 331784 | tf_op jit(solution)/shard_map/ppermute | solution.py:516
  15.8 0.9 collective-permute-start.3
  16.6 0.9 collective-permute-done.2.xlo
  17.5 2.5 %collective-permute-done.3.xhi = f32[3,3,24,128]{3,2,1,0:T(8,128)S(1)} collective-permute-done((f32[3,3,24,128]{3,2,1,0:T(8,128)S(1)}, f32[3,3,24,128]{3,2,1,0:T(8,128)S(1)}, u32[]{:S(2)}, u32[]{:S(2)}) %collective-permute-start.3) | collective-permute-done | bytes 110624 | tf_op jit(solution)/shard_map/ppermute | solution.py:516
  20.0 0.8 shard_map.29
  20.8 3.1 %collective-permute-start.4 = (f32[16,1584]{1,0:T(8,128)S(1)}, f32[16,1584]{1,0:T(8,128)S(1)}, u32[]{:S(2)}, u32[]{:S(2)}) collective-permute-start(f32[16,1584]{1,0:T(8,128)S(1)} %get-tuple-element.29), channel_id=1, source_target_pairs={{0,1},{1,2},{2,3},{4,5},{5,6},{6,7},{8,9},{9,10},{10,11},{12,13},{... | collective-permute-start | bytes 304136 | tf_op jit(solution)/shard_map/ppermute | solution.py:516
  23.9 1.3 %collective-permute-start.5 = (f32[16,1584]{1,0:T(8,128)S(1)}, f32[16,1584]{1,0:T(8,128)S(1)}, u32[]{:S(2)}, u32[]{:S(2)}) collective-permute-start(f32[16,1584]{1,0:T(8,128)S(1)} %get-tuple-element.30), channel_id=1, source_target_pairs={{1,0},{2,1},{3,2},{5,4},{6,5},{7,6},{9,8},{10,9},{11,10},{13,12},{... | collective-permute-start | bytes 304136 | tf_op jit(solution)/shard_map/ppermute | solution.py:516
  25.2 1.1 collective-permute-done.4.lower
  26.3 3.8 %collective-permute-done.5.upper = f32[16,1584]{1,0:T(8,128)S(1)} collective-permute-done((f32[16,1584]{1,0:T(8,128)S(1)}, f32[16,1584]{1,0:T(8,128)S(1)}, u32[]{:S(2)}, u32[]{:S(2)}) %collective-permute-start.5) | collective-permute-done | bytes 101408 | tf_op jit(solution)/shard_map/ppermute | solution.py:516
  30.1 3.0 %shard_map.30.own = f32[3,8,8,128]{3,2,1,0:T(8,128)S(1)} custom-call(f32[3,22,24,128]{3,2,1,0:T(8,128)S(1)} %get-tuple-element.40.f, f32[16,1584]{1,0:T(8,128)S(1)} %collective-permute-done.4.lower, f32[16,1584]{1,0:T(8,128)S(1)} %collective-permute-done.5.upper), custom_call_target="tpu_custom_call" | custom-call | tf_op jit(solution)/shard_map/pallas_call | solution.py:500
  33.1 1.3 %collective-permute-start.7 = (f32[3,8,8,128]{3,2,1,0:T(8,128)S(1)}, f32[3,8,8,128]{3,2,1,0:T(8,128)S(1)}, u32[]{:S(2)}, u32[]{:S(2)}) collective-permute-start(f32[3,8,8,128]{3,2,1,0:T(8,128)S(1)} %shard_map.30.own), channel_id=1, source_target_pairs={{4,0},{8,4},{12,8},{16,12},{20,16},{24,20},{28,24},{5,1},{9,5},{13... | collective-permute-start | bytes 294920 | tf_op jit(solution)/shard_map/ppermute | solution.py:516
  34.4 4.6 %collective-permute-start.6 = (f32[3,8,8,128]{3,2,1,0:T(8,128)S(1)}, f32[3,8,8,128]{3,2,1,0:T(8,128)S(1)}, u32[]{:S(2)}, u32[]{:S(2)}) collective-permute-start(f32[3,8,8,128]{3,2,1,0:T(8,128)S(1)} %shard_map.30.own), channel_id=1, source_target_pairs={{0,4},{4,8},{8,12},{12,16},{16,20},{20,24},{24,28},{1,5},{5,9},{9,... | collective-permute-start | bytes 294920 | tf_op jit(solution)/shard_map/ppermute | solution.py:516
  39.1 1.6 %collective-permute-done.6.ylo = f32[3,8,8,128]{3,2,1,0:T(8,128)S(1)} collective-permute-done((f32[3,8,8,128]{3,2,1,0:T(8,128)S(1)}, f32[3,8,8,128]{3,2,1,0:T(8,128)S(1)}, u32[]{:S(2)}, u32[]{:S(2)}) %collective-permute-start.6) | collective-permute-done | bytes 98336 | tf_op jit(solution)/shard_map/ppermute | solution.py:516
  40.7 0.0 collective-permute-done.7.yhi
  40.7 2.5 %collective-permute-start.8 = (f32[3,6,24,128]{3,2,1,0:T(8,128)S(1)}, f32[3,6,24,128]{3,2,1,0:T(8,128)S(1)}, u32[]{:S(2)}, u32[]{:S(2)}) collective-permute-start(f32[3,6,24,128]{3,2,1,0:T(8,128)S(1)} %pad_maximum_fusion), channel_id=1, source_target_pairs={{0,32},{32,64},{64,96},{96,128},{128,160},{160,192},{192,224},{224... | collective-permute-start | bytes 663560 | tf_op jit(solution)/shard_map/ppermute | solution.py:516
  43.2 0.0 collective-permute-start.9
  43.3 2.8 %collective-permute-done.8.xlo = f32[3,6,24,128]{3,2,1,0:T(8,128)S(1)} collective-permute-done((f32[3,6,24,128]{3,2,1,0:T(8,128)S(1)}, f32[3,6,24,128]{3,2,1,0:T(8,128)S(1)}, u32[]{:S(2)}, u32[]{:S(2)}) %collective-permute-start.8) | collective-permute-done | bytes 221216 | tf_op jit(solution)/shard_map/ppermute | solution.py:516
  46.1 2.8 %collective-permute-done.9.xhi = f32[3,6,24,128]{3,2,1,0:T(8,128)S(1)} collective-permute-done((f32[3,6,24,128]{3,2,1,0:T(8,128)S(1)}, f32[3,6,24,128]{3,2,1,0:T(8,128)S(1)}, u32[]{:S(2)}, u32[]{:S(2)}) %collective-permute-start.9) | collective-permute-done | bytes 221216 | tf_op jit(solution)/shard_map/ppermute | solution.py:516
  48.9 1.8 %shard_map.31 = f32[32,9,2,128]{3,2,1,0:T(2,128)S(1)} custom-call(f32[3,8,8,128]{3,2,1,0:T(8,128)S(1)} %shard_map.30.own, f32[3,8,8,128]{3,2,1,0:T(8,128)S(1)} %collective-permute-done.6.ylo, f32[3,8,8,128]{3,2,1,0:T(8,128)S(1)} %collective-permute-done.7.yhi, f32[3,6,24,128]{3,2,1,0:T(8,128)S(1)} %collective-permute-done.8.xlo, ...), custom_call_target="tpu_custom_call" | custom-call | tf_op jit(solution)/shard_map/pallas_call | solution.py:500
  50.7 27.2 %all_to_all.10.parts = f32[32,9,2,128]{3,2,1,0:T(2,128)S(1)} all-to-all(f32[32,9,2,128]{3,2,1,0:T(2,128)S(1)} %shard_map.31), channel_id=1, replica_groups=mesh['gx'=16,'gy'=8,'gz'=4] {'gy','gz'}, dimensions={0} | all-to-all | bytes 589824 | tf_op jit(solution)/shard_map/all_to_all | solution.py:558
  77.9 0.9 shard_map.32
  78.8 8.4 %all-to-all-start.1 = ((f32[16,48,128]{2,1,0:T(8,128)}), f32[16,48,128]{2,1,0:T(8,128)S(1)}, u32[]{:S(2)}, u32[]{:S(2)}) async-start(f32[16,48,128]{2,1,0:T(8,128)} %shard_map.32), calls=%async_computation.1 | async-start | bytes 786432 | tf_op jit(solution)/shard_map/all_to_all | solution.py:576
  87.3 0.1 collective-permute-start.11
  87.4 1.6 %collective-permute-start.10 = (f32[36,4,128]{2,1,0:T(4,128)S(1)}, f32[36,4,128]{2,1,0:T(4,128)S(1)}, u32[]{:S(2)}, u32[]{:S(2)}) collective-permute-start(f32[36,4,128]{2,1,0:T(4,128)S(1)} %shard_map.33.own), channel_id=1, source_target_pairs={{0,32},{32,64},{64,96},{96,128},{128,160},{160,192},{192,224},{224... | collective-permute-start | bytes 221192 | tf_op jit(solution)/shard_map/ppermute | solution.py:516
  89.0 1.5 %shard_map.35 = (f32[2,10,16,128]{3,2,1,0:T(8,128)S(1)}, f32[3,12,16,128]{3,2,1,0:T(8,128)S(1)}, f32[12,16,128]{2,1,0:T(8,128)S(1)}) custom-call(f32[3,8,8,128]{3,2,1,0:T(8,128)S(1)} %shard_map.30.own, f32[3,8,8,128]{3,2,1,0:T(8,128)S(1)} %collective-permute-done.6.ylo, f32[3,8,8,128]{3,2,1,0:T(8,128)S(1)} %collective-permute-done.7.yhi, ...), custom_call_target="tpu_custom_call" | custom-call | flops 8388608 | bytes 1048576 | tf_op jit(solution)/shard_map/pallas_call | solution.py:500
  90.5 0.0 copy-start.1
  90.5 3.5 %shard_map.36 = (f32[2,16,16,128]{3,2,1,0:T(8,128)S(1)}, f32[3,18,24,256]{3,2,1,0:T(8,128)S(1)}) custom-call(f32[3,22,24,128]{3,2,1,0:T(8,128)S(1)} %get-tuple-element.40.f, f32[16,1584]{1,0:T(8,128)S(1)} %collective-permute-done.4.lower, f32[16,1584]{1,0:T(8,128)S(1)} %collective-permute-done.5.upper), custom_call_target="tpu_custom_call" | custom-call | flops 62914560 | bytes 8388608 | tf_op jit(solution)/shard_map/pallas_call | solution.py:500
  94.0 5.3 %collective-permute-done.11.east = f32[36,4,128]{2,1,0:T(4,128)S(1)} collective-permute-done((f32[36,4,128]{2,1,0:T(4,128)S(1)}, f32[36,4,128]{2,1,0:T(4,128)S(1)}, u32[]{:S(2)}, u32[]{:S(2)}) %collective-permute-start.11) | collective-permute-done | bytes 73760 | tf_op jit(solution)/shard_map/ppermute | solution.py:516
  99.3 0.0 collective-permute-done.10.west
  99.3 0.0 copy-done.1
  99.3 1.1 %shard_map.34.a = f32[4,12,16,128]{3,2,1,0:T(8,128)S(1)} custom-call(f32[36,4,128]{2,1,0:T(4,128)S(1)} %collective-permute-done.10.west, f32[36,4,128]{2,1,0:T(4,128)S(1)} %shard_map.33.own, f32[36,4,128]{2,1,0:T(4,128)S(1)} %collective-permute-done.11.east), custom_call_target="tpu_custom_call" | custom-call | flops 4194304 | bytes 1048576 | tf_op jit(solution)/shard_map/pallas_call | solution.py:500
  100.4 1.3 %all-to-all-done.1.parts3 = f32[16,48,128]{2,1,0:T(8,128)S(1)} async-done(((f32[16,48,128]{2,1,0:T(8,128)}), f32[16,48,128]{2,1,0:T(8,128)S(1)}, u32[]{:S(2)}, u32[]{:S(2)}) %all-to-all-start.1) | async-done | bytes 393248 | tf_op jit(solution)/shard_map/all_to_all | solution.py:576
  101.8 0.0 copy-start.2
  101.8 0.9 copy-done.2
  102.7 6.5 %shard_map.37 = f32[2,16,16,128]{3,2,1,0:T(8,128)} custom-call(f32[16,48,128]{2,1,0:T(8,128)S(1)} %all-to-all-done.1.parts3, f32[4,12,16,128]{3,2,1,0:T(8,128)S(1)} %shard_map.34.a, f32[12,16,128]{2,1,0:T(8,128)S(1)} %get-tuple-element.37.mach2, f32[2,10,16,128]{3,2,1,0:T(8,128)S(1)} %copy-done.2, f32[3,12,16,128]{3,2,1,0:T(8,128)S(1)} %get-tuple-element.39.coef1, ...), custom_call_target="tpu_custom_call" | custom-call | tf_op jit(solution)/shard_map/pallas_call | solution.py:500
  (11 shorter events, 0.2 us)
Async XLA Ops:
  0.0 0.9 copy-start
  1.0 0.8 copy-start.3
  1.9 6.5 %collective-permute-start = (f32[3,16,4,128]{3,2,1,0:T(4,128)S(1)}, f32[3,16,4,128]{3,2,1,0:T(4,128)S(1)}, u32[]{:S(2)}, u32[]{:S(2)}) collective-permute-start(f32[3,16,4,128]{3,2,1,0:T(4,128)S(1)} %get-tuple-element.26), channel_id=1, source_target_pairs={{0,4},{4,8},{8,12},{12,16},{16,20},{20,24},{24,28},{1,5},{5,9},{9,... | collective-permute-start | bytes 294920 | tf_op jit(solution)/shard_map/ppermute | solution.py:516
  6.7 6.0 %collective-permute-start.1 = (f32[3,16,4,128]{3,2,1,0:T(4,128)S(1)}, f32[3,16,4,128]{3,2,1,0:T(4,128)S(1)}, u32[]{:S(2)}, u32[]{:S(2)}) collective-permute-start(f32[3,16,4,128]{3,2,1,0:T(4,128)S(1)} %get-tuple-element.27), channel_id=1, source_target_pairs={{4,0},{8,4},{12,8},{16,12},{20,16},{24,20},{28,24},{5,1},{9,5},{13... | collective-permute-start | bytes 294920 | tf_op jit(solution)/shard_map/ppermute | solution.py:516
  12.7 4.8 %collective-permute-start.2 = (f32[3,3,24,128]{3,2,1,0:T(8,128)S(1)}, f32[3,3,24,128]{3,2,1,0:T(8,128)S(1)}, u32[]{:S(2)}, u32[]{:S(2)}) collective-permute-start(f32[3,3,24,128]{3,2,1,0:T(8,128)S(1)} %pad_maximum_fusion.2), channel_id=1, source_target_pairs={{0,32},{32,64},{64,96},{96,128},{128,160},{160,192},{192,224},{224... | collective-permute-start | bytes 331784 | tf_op jit(solution)/shard_map/ppermute | solution.py:516
  15.8 4.2 %collective-permute-start.3 = (f32[3,3,24,128]{3,2,1,0:T(8,128)S(1)}, f32[3,3,24,128]{3,2,1,0:T(8,128)S(1)}, u32[]{:S(2)}, u32[]{:S(2)}) collective-permute-start(f32[3,3,24,128]{3,2,1,0:T(8,128)S(1)} %pad_maximum_fusion.3), channel_id=1, source_target_pairs={{0,480},{32,0},{64,32},{96,64},{128,96},{160,128},{192,160},{224,1... | collective-permute-start | bytes 331784 | tf_op jit(solution)/shard_map/ppermute | solution.py:516
  20.8 5.5 %collective-permute-start.4 = (f32[16,1584]{1,0:T(8,128)S(1)}, f32[16,1584]{1,0:T(8,128)S(1)}, u32[]{:S(2)}, u32[]{:S(2)}) collective-permute-start(f32[16,1584]{1,0:T(8,128)S(1)} %get-tuple-element.29), channel_id=1, source_target_pairs={{0,1},{1,2},{2,3},{4,5},{5,6},{6,7},{8,9},{9,10},{10,11},{12,13},{... | collective-permute-start | bytes 304136 | tf_op jit(solution)/shard_map/ppermute | solution.py:516
  23.9 6.2 %collective-permute-start.5 = (f32[16,1584]{1,0:T(8,128)S(1)}, f32[16,1584]{1,0:T(8,128)S(1)}, u32[]{:S(2)}, u32[]{:S(2)}) collective-permute-start(f32[16,1584]{1,0:T(8,128)S(1)} %get-tuple-element.30), channel_id=1, source_target_pairs={{1,0},{2,1},{3,2},{5,4},{6,5},{7,6},{9,8},{10,9},{11,10},{13,12},{... | collective-permute-start | bytes 304136 | tf_op jit(solution)/shard_map/ppermute | solution.py:516
  33.1 7.6 %collective-permute-start.7 = (f32[3,8,8,128]{3,2,1,0:T(8,128)S(1)}, f32[3,8,8,128]{3,2,1,0:T(8,128)S(1)}, u32[]{:S(2)}, u32[]{:S(2)}) collective-permute-start(f32[3,8,8,128]{3,2,1,0:T(8,128)S(1)} %shard_map.30.own), channel_id=1, source_target_pairs={{4,0},{8,4},{12,8},{16,12},{20,16},{24,20},{28,24},{5,1},{9,5},{13... | collective-permute-start | bytes 294920 | tf_op jit(solution)/shard_map/ppermute | solution.py:516
  34.4 6.3 %collective-permute-start.6 = (f32[3,8,8,128]{3,2,1,0:T(8,128)S(1)}, f32[3,8,8,128]{3,2,1,0:T(8,128)S(1)}, u32[]{:S(2)}, u32[]{:S(2)}) collective-permute-start(f32[3,8,8,128]{3,2,1,0:T(8,128)S(1)} %shard_map.30.own), channel_id=1, source_target_pairs={{0,4},{4,8},{8,12},{12,16},{16,20},{20,24},{24,28},{1,5},{5,9},{9,... | collective-permute-start | bytes 294920 | tf_op jit(solution)/shard_map/ppermute | solution.py:516
  40.7 5.4 %collective-permute-start.8 = (f32[3,6,24,128]{3,2,1,0:T(8,128)S(1)}, f32[3,6,24,128]{3,2,1,0:T(8,128)S(1)}, u32[]{:S(2)}, u32[]{:S(2)}) collective-permute-start(f32[3,6,24,128]{3,2,1,0:T(8,128)S(1)} %pad_maximum_fusion), channel_id=1, source_target_pairs={{0,32},{32,64},{64,96},{96,128},{128,160},{160,192},{192,224},{224... | collective-permute-start | bytes 663560 | tf_op jit(solution)/shard_map/ppermute | solution.py:516
  43.2 5.6 %collective-permute-start.9 = (f32[3,6,24,128]{3,2,1,0:T(8,128)S(1)}, f32[3,6,24,128]{3,2,1,0:T(8,128)S(1)}, u32[]{:S(2)}, u32[]{:S(2)}) collective-permute-start(f32[3,6,24,128]{3,2,1,0:T(8,128)S(1)} %pad_maximum_fusion.1), channel_id=1, source_target_pairs={{0,480},{32,0},{64,32},{96,64},{128,96},{160,128},{192,160},{224,1... | collective-permute-start | bytes 663560 | tf_op jit(solution)/shard_map/ppermute | solution.py:516
  78.8 23.0 %all-to-all-start.1 = ((f32[16,48,128]{2,1,0:T(8,128)}), f32[16,48,128]{2,1,0:T(8,128)S(1)}, u32[]{:S(2)}, u32[]{:S(2)}) async-start(f32[16,48,128]{2,1,0:T(8,128)} %shard_map.32), calls=%async_computation.1 | async-start | bytes 786432 | tf_op jit(solution)/shard_map/all_to_all | solution.py:576
  87.3 12.1 %collective-permute-start.11 = (f32[36,4,128]{2,1,0:T(4,128)S(1)}, f32[36,4,128]{2,1,0:T(4,128)S(1)}, u32[]{:S(2)}, u32[]{:S(2)}) collective-permute-start(f32[36,4,128]{2,1,0:T(4,128)S(1)} %shard_map.33.own), channel_id=1, source_target_pairs={{0,480},{32,0},{64,32},{96,64},{128,96},{160,128},{192,160},{224,1... | collective-permute-start | bytes 221192 | tf_op jit(solution)/shard_map/ppermute | solution.py:516
  87.4 11.9 %collective-permute-start.10 = (f32[36,4,128]{2,1,0:T(4,128)S(1)}, f32[36,4,128]{2,1,0:T(4,128)S(1)}, u32[]{:S(2)}, u32[]{:S(2)}) collective-permute-start(f32[36,4,128]{2,1,0:T(4,128)S(1)} %shard_map.33.own), channel_id=1, source_target_pairs={{0,32},{32,64},{64,96},{96,128},{128,160},{160,192},{192,224},{224... | collective-permute-start | bytes 221192 | tf_op jit(solution)/shard_map/ppermute | solution.py:516
  90.5 8.8 %copy-start.1 = (f32[2,10,16,128]{3,2,1,0:T(8,128)}, f32[2,10,16,128]{3,2,1,0:T(8,128)S(1)}, u32[]{:S(2)}) copy-start(f32[2,10,16,128]{3,2,1,0:T(8,128)S(1)} %get-tuple-element.38.base1) | copy-start | bytes 491524
  101.8 0.9 copy-start.2

commit v7 on v5

--- a/solution.py
+++ b/solution.py
@@ -170,20 +170,23 @@
     return jnp.where(rule(iota(shape, 0), iota(shape, 1)), value, 0.0).astype(BF16)
 
 
-def ends():
-    at = lax.axis_index("gx")
-    return jnp.where(at > 0, 1.0, 0.0), jnp.where(at < 15, 1.0, 0.0)
+def ends(axis):
+    at = lax.axis_index(axis)
+    return jnp.where(at > 0, 1.0, 0.0), jnp.where(at < lax.axis_size(axis) - 1, 1.0, 0.0)
 
 
 def assemble(own, ylo, yhi, xlo, xhi, f):
     count, rows, hx, hy = own.shape[1], own.shape[2], xlo.shape[1], ylo.shape[2]
-    low, high = ends()
+    low, high = ends("gx")
     for c in range(3):
         f[c, 0:hx] = xlo[c] if c < 2 else xlo[c] * low
         f[c, hx : hx + count, 0:hy] = ylo[c]
         f[c, hx : hx + count, hy : hy + rows] = own[c]
         f[c, hx : hx + count, hy + rows :] = yhi[c]
         f[c, hx + count :] = xhi[c] if c < 2 else xhi[c] * high
+    low, high = ends("gy")
+    f[2, :, 0:hy] = f[2, :, 0:hy] * low
+    f[2, :, hy + rows :] = f[2, :, hy + rows :] * high
 
 
 def start_kernel(source, mach, own, high, low):
@@ -351,7 +354,7 @@
 def window2_kernel(west, own, east, a, planes):
     lane = iota((Y2, 128), 1) // 32
     planes[...] = jnp.zeros_like(planes)
-    low, high = ends()
+    low, high = ends("gx")
     for bx, piece in enumerate((west, own, east)):
         factor = (low, None, high)[bx]
 
@@ -511,7 +514,7 @@
 def shift(block, axis, step):
     count = lax.axis_size(axis)
     pairs = [(i, (i + step) % count) for i in range(count)]
-    if axis != "gx":
+    if axis == "gz":
         pairs = [(i, j) for i, j in pairs if j == i + step]
     return lax.ppermute(block, axis, pairs)
 

time: 106 us -> 106 us (level)
  starting transfers between devices: 46.9 us -> 53.6 us
  waiting for transfers between devices: 34.8 us -> 28.1 us
    ppermute x12, starting transfers between devices: 27.3 us -> 35.3 us  [shift(): return lax.ppermute(block, axis, pairs)]
    ppermute x12, waiting for transfers between devices: 29.7 us -> 23 us  [shift(): return lax.ppermute(block, axis, pairs)]
    all_to_all x1, starting transfers between devices: 8.85 us -> 7.65 us  [shards(): parts2 = lax.all_to_all(chunk2, ('gy', 'gz'), 0, 0)]
  transfers between devices with their start and end apart: 14 -> 14, of which waited for: 14 -> 12; matrix products, arithmetic and copies ran while one was open for 0% -> 0% of each run, Pallas kernels for 6% -> 6%
where the time goes in v7:
time: 106 us
  starting transfers between devices  53.6 us (51%)
  waiting for transfers between devices  28.1 us (27%)
  Pallas kernels  19.9 us (19%)
  local copies, waits for them, and re-layouts  3.84 us (4%)
    ppermute x12, starting transfers between devices, shift(): return lax.ppermute(block, axis, pairs)  35.3 us
    ppermute x12, waiting for transfers between devices, shift(): return lax.ppermute(block, axis, pairs)  23 us
    pallas_call x10, Pallas kernels, call(): pl.pallas_call(kernel, out_shape=[jax.ShapeDtypeStruct(s, F32) for s in o...  19.9 us
    all_to_all x1, starting transfers between devices, shards(): parts3 = lax.all_to_all(chunk3, 'gx', 0, 0)  10.7 us
    all_to_all x1, starting transfers between devices, shards(): parts2 = lax.all_to_all(chunk2, ('gy', 'gz'), 0, 0)  7.65 us
    all_to_all x1, waiting for transfers between devices, shards(): parts2 = lax.all_to_all(chunk2, ('gy', 'gz'), 0, 0)  3.79 us
    unnamed x16, local copies, waits for them, and re-layouts  3.78 us
  transfers between devices with their start and end apart: 14, of which 12 were waited for; matrix products, arithmetic and copies ran while one was open for 0% of the time, Pallas kernels for 6%

profile of v7, /device:TPU:1, one launch (start us, length us, event | category | flops | bytes accessed | tf_op | source)
XLA Modules:
  0.0 105.7 jit_solution(17712174829323413160)
XLA Ops:
  0.0 0.0 copy-start.2
  0.0 0.9 copy-done.2
  1.0 0.8 copy-done.7
  1.8 0.1 shard_map.28
  1.9 4.8 %collective-permute-start = (f32[3,16,4,128]{3,2,1,0:T(4,128)S(1)}, f32[3,16,4,128]{3,2,1,0:T(4,128)S(1)}, u32[]{:S(2)}, u32[]{:S(2)}) collective-permute-start(f32[3,16,4,128]{3,2,1,0:T(4,128)S(1)} %get-tuple-element.23), channel_id=1, source_target_pairs={{0,4},{4,8},{8,12},{12,16},{16,20},{20,24},{24,28},{28,0},{1,5},{5... | collective-permute-start | bytes 294920 | tf_op jit(solution)/shard_map/ppermute | solution.py:519
  6.7 8.6 %collective-permute-start.1 = (f32[3,16,4,128]{3,2,1,0:T(4,128)S(1)}, f32[3,16,4,128]{3,2,1,0:T(4,128)S(1)}, u32[]{:S(2)}, u32[]{:S(2)}) collective-permute-start(f32[3,16,4,128]{3,2,1,0:T(4,128)S(1)} %get-tuple-element.24), channel_id=1, source_target_pairs={{0,28},{4,0},{8,4},{12,8},{16,12},{20,16},{24,20},{28,24},{1,29},{... | collective-permute-start | bytes 294920 | tf_op jit(solution)/shard_map/ppermute | solution.py:519
  15.3 0.6 collective-permute-done.ylo
  15.9 1.0 collective-permute-done.1.yhi
  16.9 1.5 %collective-permute-start.3 = (f32[3,3,24,128]{3,2,1,0:T(8,128)S(1)}, f32[3,3,24,128]{3,2,1,0:T(8,128)S(1)}, u32[]{:S(2)}, u32[]{:S(2)}) collective-permute-start(f32[3,3,24,128]{3,2,1,0:T(8,128)S(1)} %pad_maximum_fusion.3), channel_id=1, source_target_pairs={{0,480},{32,0},{64,32},{96,64},{128,96},{160,128},{192,160},{224,1... | collective-permute-start | bytes 331784 | tf_op jit(solution)/shard_map/ppermute | solution.py:519
  18.5 1.2 %collective-permute-start.2 = (f32[3,3,24,128]{3,2,1,0:T(8,128)S(1)}, f32[3,3,24,128]{3,2,1,0:T(8,128)S(1)}, u32[]{:S(2)}, u32[]{:S(2)}) collective-permute-start(f32[3,3,24,128]{3,2,1,0:T(8,128)S(1)} %pad_maximum_fusion.2), channel_id=1, source_target_pairs={{0,32},{32,64},{64,96},{96,128},{128,160},{160,192},{192,224},{224... | collective-permute-start | bytes 331784 | tf_op jit(solution)/shard_map/ppermute | solution.py:519
  19.7 2.4 %collective-permute-done.3.xhi = f32[3,3,24,128]{3,2,1,0:T(8,128)S(1)} collective-permute-done((f32[3,3,24,128]{3,2,1,0:T(8,128)S(1)}, f32[3,3,24,128]{3,2,1,0:T(8,128)S(1)}, u32[]{:S(2)}, u32[]{:S(2)}) %collective-permute-start.3) | collective-permute-done | bytes 110624 | tf_op jit(solution)/shard_map/ppermute | solution.py:519
  22.1 0.0 collective-permute-done.2.xlo
  22.1 0.8 shard_map.29
  22.9 3.1 %collective-permute-start.4 = (f32[16,1584]{1,0:T(8,128)S(1)}, f32[16,1584]{1,0:T(8,128)S(1)}, u32[]{:S(2)}, u32[]{:S(2)}) collective-permute-start(f32[16,1584]{1,0:T(8,128)S(1)} %get-tuple-element.26), channel_id=1, source_target_pairs={{0,1},{1,2},{2,3},{4,5},{5,6},{6,7},{8,9},{9,10},{10,11},{12,13},{... | collective-permute-start | bytes 304136 | tf_op jit(solution)/shard_map/ppermute | solution.py:519
  26.1 1.3 %collective-permute-start.5 = (f32[16,1584]{1,0:T(8,128)S(1)}, f32[16,1584]{1,0:T(8,128)S(1)}, u32[]{:S(2)}, u32[]{:S(2)}) collective-permute-start(f32[16,1584]{1,0:T(8,128)S(1)} %get-tuple-element.27), channel_id=1, source_target_pairs={{1,0},{2,1},{3,2},{5,4},{6,5},{7,6},{9,8},{10,9},{11,10},{13,12},{... | collective-permute-start | bytes 304136 | tf_op jit(solution)/shard_map/ppermute | solution.py:519
  27.4 0.4 collective-permute-done.4.lower
  27.8 3.8 %collective-permute-done.5.upper = f32[16,1584]{1,0:T(8,128)S(1)} collective-permute-done((f32[16,1584]{1,0:T(8,128)S(1)}, f32[16,1584]{1,0:T(8,128)S(1)}, u32[]{:S(2)}, u32[]{:S(2)}) %collective-permute-start.5) | collective-permute-done | bytes 101408 | tf_op jit(solution)/shard_map/ppermute | solution.py:519
  31.5 3.0 %shard_map.30.own = f32[3,8,8,128]{3,2,1,0:T(8,128)S(1)} custom-call(f32[3,22,24,128]{3,2,1,0:T(8,128)S(1)} %get-tuple-element.25.f, f32[16,1584]{1,0:T(8,128)S(1)} %collective-permute-done.4.lower, f32[16,1584]{1,0:T(8,128)S(1)} %collective-permute-done.5.upper), custom_call_target="tpu_custom_call" | custom-call | tf_op jit(solution)/shard_map/pallas_call | solution.py:503
  34.5 1.9 %collective-permute-start.6 = (f32[3,8,8,128]{3,2,1,0:T(8,128)S(1)}, f32[3,8,8,128]{3,2,1,0:T(8,128)S(1)}, u32[]{:S(2)}, u32[]{:S(2)}) collective-permute-start(f32[3,8,8,128]{3,2,1,0:T(8,128)S(1)} %shard_map.30.own), channel_id=1, source_target_pairs={{0,4},{4,8},{8,12},{12,16},{16,20},{20,24},{24,28},{28,0},{1,5},{5... | collective-permute-start | bytes 294920 | tf_op jit(solution)/shard_map/ppermute | solution.py:519
  36.5 5.2 %collective-permute-start.7 = (f32[3,8,8,128]{3,2,1,0:T(8,128)S(1)}, f32[3,8,8,128]{3,2,1,0:T(8,128)S(1)}, u32[]{:S(2)}, u32[]{:S(2)}) collective-permute-start(f32[3,8,8,128]{3,2,1,0:T(8,128)S(1)} %shard_map.30.own), channel_id=1, source_target_pairs={{0,28},{4,0},{8,4},{12,8},{16,12},{20,16},{24,20},{28,24},{1,29},{... | collective-permute-start | bytes 294920 | tf_op jit(solution)/shard_map/ppermute | solution.py:519
  41.7 0.0 collective-permute-done.6.ylo
  41.8 1.5 %collective-permute-done.7.yhi = f32[3,8,8,128]{3,2,1,0:T(8,128)S(1)} collective-permute-done((f32[3,8,8,128]{3,2,1,0:T(8,128)S(1)}, f32[3,8,8,128]{3,2,1,0:T(8,128)S(1)}, u32[]{:S(2)}, u32[]{:S(2)}) %collective-permute-start.7) | collective-permute-done | bytes 98336 | tf_op jit(solution)/shard_map/ppermute | solution.py:519
  43.4 5.9 %collective-permute-start.9 = (f32[3,6,24,128]{3,2,1,0:T(8,128)S(1)}, f32[3,6,24,128]{3,2,1,0:T(8,128)S(1)}, u32[]{:S(2)}, u32[]{:S(2)}) collective-permute-start(f32[3,6,24,128]{3,2,1,0:T(8,128)S(1)} %pad_maximum_fusion.1), channel_id=1, source_target_pairs={{0,480},{32,0},{64,32},{96,64},{128,96},{160,128},{192,160},{224,1... | collective-permute-start | bytes 663560 | tf_op jit(solution)/shard_map/ppermute | solution.py:519
  49.3 0.0 collective-permute-start.8
  49.3 1.8 %collective-permute-done.9.xhi = f32[3,6,24,128]{3,2,1,0:T(8,128)S(1)} collective-permute-done((f32[3,6,24,128]{3,2,1,0:T(8,128)S(1)}, f32[3,6,24,128]{3,2,1,0:T(8,128)S(1)}, u32[]{:S(2)}, u32[]{:S(2)}) %collective-permute-start.9) | collective-permute-done | bytes 221216 | tf_op jit(solution)/shard_map/ppermute | solution.py:519
  51.1 1.1 %collective-permute-done.8.xlo = f32[3,6,24,128]{3,2,1,0:T(8,128)S(1)} collective-permute-done((f32[3,6,24,128]{3,2,1,0:T(8,128)S(1)}, f32[3,6,24,128]{3,2,1,0:T(8,128)S(1)}, u32[]{:S(2)}, u32[]{:S(2)}) %collective-permute-start.8) | collective-permute-done | bytes 221216 | tf_op jit(solution)/shard_map/ppermute | solution.py:519
  52.2 2.5 %shard_map.31 = f32[32,9,2,128]{3,2,1,0:T(2,128)} custom-call(f32[3,8,8,128]{3,2,1,0:T(8,128)S(1)} %shard_map.30.own, f32[3,8,8,128]{3,2,1,0:T(8,128)S(1)} %collective-permute-done.6.ylo, f32[3,8,8,128]{3,2,1,0:T(8,128)S(1)} %collective-permute-done.7.yhi, f32[3,6,24,128]{3,2,1,0:T(8,128)S(1)} %collective-permute-done.8.xlo, ...), custom_call_target="tpu_custom_call" | custom-call | tf_op jit(solution)/shard_map/pallas_call | solution.py:503
  54.7 7.7 %all-to-all-start = ((f32[32,9,2,128]{3,2,1,0:T(2,128)}), f32[32,9,2,128]{3,2,1,0:T(2,128)S(1)}, u32[]{:S(2)}, u32[]{:S(2)}) async-start(f32[32,9,2,128]{3,2,1,0:T(2,128)} %shard_map.31), calls=%async_computation | async-start | bytes 589824 | tf_op jit(solution)/shard_map/all_to_all | solution.py:561
  62.4 3.5 %shard_map.33 = (f32[2,16,16,128]{3,2,1,0:T(8,128)S(1)}, f32[3,18,24,256]{3,2,1,0:T(8,128)S(1)}) custom-call(f32[3,22,24,128]{3,2,1,0:T(8,128)S(1)} %get-tuple-element.25.f, f32[16,1584]{1,0:T(8,128)S(1)} %collective-permute-done.4.lower, f32[16,1584]{1,0:T(8,128)S(1)} %collective-permute-done.5.upper), custom_call_target="tpu_custom_call" | custom-call | flops 62914560 | bytes 8388608 | tf_op jit(solution)/shard_map/pallas_call | solution.py:503
  65.8 0.0 copy-start
  65.8 0.7 copy-done
  66.5 1.5 %shard_map.32 = (f32[2,10,16,128]{3,2,1,0:T(8,128)S(1)}, f32[3,12,16,128]{3,2,1,0:T(8,128)S(1)}, f32[12,16,128]{2,1,0:T(8,128)S(1)}) custom-call(f32[3,8,8,128]{3,2,1,0:T(8,128)S(1)} %shard_map.30.own, f32[3,8,8,128]{3,2,1,0:T(8,128)S(1)} %collective-permute-done.6.ylo, f32[3,8,8,128]{3,2,1,0:T(8,128)S(1)} %collective-permute-done.7.yhi, ...), custom_call_target="tpu_custom_call" | custom-call | flops 8388608 | bytes 1048576 | tf_op jit(solution)/shard_map/pallas_call | solution.py:503
  68.0 0.0 copy-start.3
  68.0 0.7 copy-done.3
  68.7 0.6 copy-done.5
  69.3 3.8 %all-to-all-done.parts = f32[32,9,2,128]{3,2,1,0:T(2,128)S(1)} async-done(((f32[32,9,2,128]{3,2,1,0:T(2,128)}), f32[32,9,2,128]{3,2,1,0:T(2,128)S(1)}, u32[]{:S(2)}, u32[]{:S(2)}) %all-to-all-start) | async-done | bytes 294944 | tf_op jit(solution)/shard_map/all_to_all | solution.py:561
  73.1 0.9 shard_map.34
  74.0 10.7 %all-to-all-start.1 = ((f32[16,48,128]{2,1,0:T(8,128)}), f32[16,48,128]{2,1,0:T(8,128)S(1)}, u32[]{:S(2)}, u32[]{:S(2)}) async-start(f32[16,48,128]{2,1,0:T(8,128)} %shard_map.34), calls=%async_computation.1 | async-start | bytes 786432 | tf_op jit(solution)/shard_map/all_to_all | solution.py:578
  84.7 1.6 %collective-permute-start.10 = (f32[36,4,128]{2,1,0:T(4,128)S(1)}, f32[36,4,128]{2,1,0:T(4,128)S(1)}, u32[]{:S(2)}, u32[]{:S(2)}) collective-permute-start(f32[36,4,128]{2,1,0:T(4,128)S(1)} %shard_map.35.own), channel_id=1, source_target_pairs={{0,32},{32,64},{64,96},{96,128},{128,160},{160,192},{192,224},{224... | collective-permute-start | bytes 221192 | tf_op jit(solution)/shard_map/ppermute | solution.py:519
  86.4 0.0 collective-permute-start.11
  86.4 7.1 %collective-permute-done.10.west = f32[36,4,128]{2,1,0:T(4,128)S(1)} collective-permute-done((f32[36,4,128]{2,1,0:T(4,128)S(1)}, f32[36,4,128]{2,1,0:T(4,128)S(1)}, u32[]{:S(2)}, u32[]{:S(2)}) %collective-permute-start.10) | collective-permute-done | bytes 73760 | tf_op jit(solution)/shard_map/ppermute | solution.py:519
  93.4 3.4 %collective-permute-done.11.east = f32[36,4,128]{2,1,0:T(4,128)S(1)} collective-permute-done((f32[36,4,128]{2,1,0:T(4,128)S(1)}, f32[36,4,128]{2,1,0:T(4,128)S(1)}, u32[]{:S(2)}, u32[]{:S(2)}) %collective-permute-start.11) | collective-permute-done | bytes 73760 | tf_op jit(solution)/shard_map/ppermute | solution.py:519
  96.8 1.1 %shard_map.36.a = f32[4,12,16,128]{3,2,1,0:T(8,128)S(1)} custom-call(f32[36,4,128]{2,1,0:T(4,128)S(1)} %collective-permute-done.10.west, f32[36,4,128]{2,1,0:T(4,128)S(1)} %shard_map.35.own, f32[36,4,128]{2,1,0:T(4,128)S(1)} %collective-permute-done.11.east), custom_call_target="tpu_custom_call" | custom-call | flops 4194304 | bytes 1048576 | tf_op jit(solution)/shard_map/pallas_call | solution.py:503
  97.9 1.3 %all-to-all-done.1.parts3 = f32[16,48,128]{2,1,0:T(8,128)S(1)} async-done(((f32[16,48,128]{2,1,0:T(8,128)}), f32[16,48,128]{2,1,0:T(8,128)S(1)}, u32[]{:S(2)}, u32[]{:S(2)}) %all-to-all-start.1) | async-done | bytes 393248 | tf_op jit(solution)/shard_map/all_to_all | solution.py:578
  99.2 0.0 copy-done.1
  99.2 0.0 copy-done.4
  99.3 0.0 copy-done.6
  99.3 6.5 %shard_map.37 = f32[2,16,16,128]{3,2,1,0:T(8,128)} custom-call(f32[16,48,128]{2,1,0:T(8,128)S(1)} %all-to-all-done.1.parts3, f32[4,12,16,128]{3,2,1,0:T(8,128)S(1)} %shard_map.36.a, f32[12,16,128]{2,1,0:T(8,128)S(1)} %copy-done.6, f32[2,10,16,128]{3,2,1,0:T(8,128)S(1)} %copy-done.4, f32[3,12,16,128]{3,2,1,0:T(8,128)S(1)} %get-tuple-element.36.coef1, ...), custom_call_target="tpu_custom_call" | custom-call | tf_op jit(solution)/shard_map/pallas_call | solution.py:503
  (16 shorter events, 0.2 us)
Async XLA Ops:
  0.0 0.9 copy-start.2
  1.0 0.8 copy-start.7
  1.9 14.0 %collective-permute-start = (f32[3,16,4,128]{3,2,1,0:T(4,128)S(1)}, f32[3,16,4,128]{3,2,1,0:T(4,128)S(1)}, u32[]{:S(2)}, u32[]{:S(2)}) collective-permute-start(f32[3,16,4,128]{3,2,1,0:T(4,128)S(1)} %get-tuple-element.23), channel_id=1, source_target_pairs={{0,4},{4,8},{8,12},{12,16},{16,20},{20,24},{24,28},{28,0},{1,5},{5... | collective-permute-start | bytes 294920 | tf_op jit(solution)/shard_map/ppermute | solution.py:519
  6.7 10.2 %collective-permute-start.1 = (f32[3,16,4,128]{3,2,1,0:T(4,128)S(1)}, f32[3,16,4,128]{3,2,1,0:T(4,128)S(1)}, u32[]{:S(2)}, u32[]{:S(2)}) collective-permute-start(f32[3,16,4,128]{3,2,1,0:T(4,128)S(1)} %get-tuple-element.24), channel_id=1, source_target_pairs={{0,28},{4,0},{8,4},{12,8},{16,12},{20,16},{24,20},{28,24},{1,29},{... | collective-permute-start | bytes 294920 | tf_op jit(solution)/shard_map/ppermute | solution.py:519
  16.9 5.2 %collective-permute-start.3 = (f32[3,3,24,128]{3,2,1,0:T(8,128)S(1)}, f32[3,3,24,128]{3,2,1,0:T(8,128)S(1)}, u32[]{:S(2)}, u32[]{:S(2)}) collective-permute-start(f32[3,3,24,128]{3,2,1,0:T(8,128)S(1)} %pad_maximum_fusion.3), channel_id=1, source_target_pairs={{0,480},{32,0},{64,32},{96,64},{128,96},{160,128},{192,160},{224,1... | collective-permute-start | bytes 331784 | tf_op jit(solution)/shard_map/ppermute | solution.py:519
  18.5 3.6 %collective-permute-start.2 = (f32[3,3,24,128]{3,2,1,0:T(8,128)S(1)}, f32[3,3,24,128]{3,2,1,0:T(8,128)S(1)}, u32[]{:S(2)}, u32[]{:S(2)}) collective-permute-start(f32[3,3,24,128]{3,2,1,0:T(8,128)S(1)} %pad_maximum_fusion.2), channel_id=1, source_target_pairs={{0,32},{32,64},{64,96},{96,128},{128,160},{160,192},{192,224},{224... | collective-permute-start | bytes 331784 | tf_op jit(solution)/shard_map/ppermute | solution.py:519
  22.9 4.8 %collective-permute-start.4 = (f32[16,1584]{1,0:T(8,128)S(1)}, f32[16,1584]{1,0:T(8,128)S(1)}, u32[]{:S(2)}, u32[]{:S(2)}) collective-permute-start(f32[16,1584]{1,0:T(8,128)S(1)} %get-tuple-element.26), channel_id=1, source_target_pairs={{0,1},{1,2},{2,3},{4,5},{5,6},{6,7},{8,9},{9,10},{10,11},{12,13},{... | collective-permute-start | bytes 304136 | tf_op jit(solution)/shard_map/ppermute | solution.py:519
  26.1 5.4 %collective-permute-start.5 = (f32[16,1584]{1,0:T(8,128)S(1)}, f32[16,1584]{1,0:T(8,128)S(1)}, u32[]{:S(2)}, u32[]{:S(2)}) collective-permute-start(f32[16,1584]{1,0:T(8,128)S(1)} %get-tuple-element.27), channel_id=1, source_target_pairs={{1,0},{2,1},{3,2},{5,4},{6,5},{7,6},{9,8},{10,9},{11,10},{13,12},{... | collective-permute-start | bytes 304136 | tf_op jit(solution)/shard_map/ppermute | solution.py:519
  34.5 7.2 %collective-permute-start.6 = (f32[3,8,8,128]{3,2,1,0:T(8,128)S(1)}, f32[3,8,8,128]{3,2,1,0:T(8,128)S(1)}, u32[]{:S(2)}, u32[]{:S(2)}) collective-permute-start(f32[3,8,8,128]{3,2,1,0:T(8,128)S(1)} %shard_map.30.own), channel_id=1, source_target_pairs={{0,4},{4,8},{8,12},{12,16},{16,20},{20,24},{24,28},{28,0},{1,5},{5... | collective-permute-start | bytes 294920 | tf_op jit(solution)/shard_map/ppermute | solution.py:519
  36.5 6.9 %collective-permute-start.7 = (f32[3,8,8,128]{3,2,1,0:T(8,128)S(1)}, f32[3,8,8,128]{3,2,1,0:T(8,128)S(1)}, u32[]{:S(2)}, u32[]{:S(2)}) collective-permute-start(f32[3,8,8,128]{3,2,1,0:T(8,128)S(1)} %shard_map.30.own), channel_id=1, source_target_pairs={{0,28},{4,0},{8,4},{12,8},{16,12},{20,16},{24,20},{28,24},{1,29},{... | collective-permute-start | bytes 294920 | tf_op jit(solution)/shard_map/ppermute | solution.py:519
  43.4 7.7 %collective-permute-start.9 = (f32[3,6,24,128]{3,2,1,0:T(8,128)S(1)}, f32[3,6,24,128]{3,2,1,0:T(8,128)S(1)}, u32[]{:S(2)}, u32[]{:S(2)}) collective-permute-start(f32[3,6,24,128]{3,2,1,0:T(8,128)S(1)} %pad_maximum_fusion.1), channel_id=1, source_target_pairs={{0,480},{32,0},{64,32},{96,64},{128,96},{160,128},{192,160},{224,1... | collective-permute-start | bytes 663560 | tf_op jit(solution)/shard_map/ppermute | solution.py:519
  49.3 2.9 %collective-permute-start.8 = (f32[3,6,24,128]{3,2,1,0:T(8,128)S(1)}, f32[3,6,24,128]{3,2,1,0:T(8,128)S(1)}, u32[]{:S(2)}, u32[]{:S(2)}) collective-permute-start(f32[3,6,24,128]{3,2,1,0:T(8,128)S(1)} %pad_maximum_fusion), channel_id=1, source_target_pairs={{0,32},{32,64},{64,96},{96,128},{128,160},{160,192},{192,224},{224... | collective-permute-start | bytes 663560 | tf_op jit(solution)/shard_map/ppermute | solution.py:519
  54.7 18.4 %all-to-all-start = ((f32[32,9,2,128]{3,2,1,0:T(2,128)}), f32[32,9,2,128]{3,2,1,0:T(2,128)S(1)}, u32[]{:S(2)}, u32[]{:S(2)}) async-start(f32[32,9,2,128]{3,2,1,0:T(2,128)} %shard_map.31), calls=%async_computation | async-start | bytes 589824 | tf_op jit(solution)/shard_map/all_to_all | solution.py:561
  65.8 0.7 copy-start
  68.0 0.7 copy-start.3
  68.7 0.6 copy-start.5
  69.3 29.9 %copy-start.1 = (f32[2,16,16,128]{3,2,1,0:T(8,128)S(1)}, f32[2,16,16,128]{3,2,1,0:T(8,128)}, u32[]{:S(2)}) copy-start(f32[2,16,16,128]{3,2,1,0:T(8,128)} %copy-done) | copy-start | bytes 786436
  73.1 26.1 %copy-start.4 = (f32[2,10,16,128]{3,2,1,0:T(8,128)S(1)}, f32[2,10,16,128]{3,2,1,0:T(8,128)}, u32[]{:S(2)}) copy-start(f32[2,10,16,128]{3,2,1,0:T(8,128)} %copy-done.3) | copy-start | bytes 491524
  73.1 26.1 %copy-start.6 = (f32[12,16,128]{2,1,0:T(8,128)S(1)}, f32[12,16,128]{2,1,0:T(8,128)}, u32[]{:S(2)}) copy-start(f32[12,16,128]{2,1,0:T(8,128)} %copy-done.5) | copy-start | bytes 294916
  74.0 25.3 %all-to-all-start.1 = ((f32[16,48,128]{2,1,0:T(8,128)}), f32[16,48,128]{2,1,0:T(8,128)S(1)}, u32[]{:S(2)}, u32[]{:S(2)}) async-start(f32[16,48,128]{2,1,0:T(8,128)} %shard_map.34), calls=%async_computation.1 | async-start | bytes 786432 | tf_op jit(solution)/shard_map/all_to_all | solution.py:578
  84.7 8.7 %collective-permute-start.10 = (f32[36,4,128]{2,1,0:T(4,128)S(1)}, f32[36,4,128]{2,1,0:T(4,128)S(1)}, u32[]{:S(2)}, u32[]{:S(2)}) collective-permute-start(f32[36,4,128]{2,1,0:T(4,128)S(1)} %shard_map.35.own), channel_id=1, source_target_pairs={{0,32},{32,64},{64,96},{96,128},{128,160},{160,192},{192,224},{224... | collective-permute-start | bytes 221192 | tf_op jit(solution)/shard_map/ppermute | solution.py:519
  86.4 10.4 %collective-permute-start.11 = (f32[36,4,128]{2,1,0:T(4,128)S(1)}, f32[36,4,128]{2,1,0:T(4,128)S(1)}, u32[]{:S(2)}, u32[]{:S(2)}) collective-permute-start(f32[36,4,128]{2,1,0:T(4,128)S(1)} %shard_map.35.own), channel_id=1, source_target_pairs={{0,480},{32,0},{64,32},{96,64},{128,96},{160,128},{192,160},{224,1... | collective-permute-start | bytes 221192 | tf_op jit(solution)/shard_map/ppermute | solution.py:519

commit v8 on v5

--- a/solution.py
+++ b/solution.py
@@ -28,14 +28,12 @@
 
 def split(x):
     high = x.astype(BF16)
-    rest = x - high.astype(F32)
-    middle = rest.astype(BF16)
-    return high, middle, (rest - middle.astype(F32)).astype(BF16)
+    return high, (x - high.astype(F32)).astype(BF16)
 
 
 def select(x, matrix, dims=(((1,), (0,)), ((), ()))):
     parts = [lax.dot_general(p, matrix, dims, preferred_element_type=F32) for p in split(x)]
-    return parts[0] + (parts[1] + parts[2])
+    return parts[0] + parts[1]
 
 
 def coefficients(mach, level):
@@ -199,7 +197,7 @@
         edge = matrix(16, 128, lambda r, l: (r < HZ) & (l == start + r))
         dims = (((1,), (1,)), ((), ()))
         terms = [lax.dot_general(edge, p, dims, preferred_element_type=F32) for p in parts]
-        out[...] = terms[0] + (terms[1] + terms[2])
+        out[...] = terms[0] + terms[1]
 
 
 def smooth0(f, lower, upper, g, hd, v2, v1):

time: 106 us -> 105 us (level)
  no operation moved by 1% of the time
where the time goes in v8:
time: 105 us
  starting transfers between devices  46.9 us (45%)
  waiting for transfers between devices  35.1 us (33%)
  Pallas kernels  18.9 us (18%)
  local copies, waits for them, and re-layouts  3.85 us (4%)
    ppermute x12, waiting for transfers between devices, shift(): return lax.ppermute(block, axis, pairs)  29.7 us
    ppermute x12, starting transfers between devices, shift(): return lax.ppermute(block, axis, pairs)  27.3 us
    pallas_call x10, Pallas kernels, call(): pl.pallas_call(kernel, out_shape=[jax.ShapeDtypeStruct(s, F32) for s in o...  18.9 us
    all_to_all x1, starting transfers between devices, shards(): parts3 = lax.all_to_all(chunk3, 'gx', 0, 0)  10.7 us
    all_to_all x1, starting transfers between devices, shards(): parts2 = lax.all_to_all(chunk2, ('gy', 'gz'), 0, 0)  8.84 us
    all_to_all x1, waiting for transfers between devices, shards(): parts2 = lax.all_to_all(chunk2, ('gy', 'gz'), 0, 0)  4.04 us
    unnamed x16, local copies, waits for them, and re-layouts  3.79 us
  transfers between devices with their start and end apart: 14, of which 14 were waited for; matrix products, arithmetic and copies ran while one was open for 0% of the time, Pallas kernels for 6%

profile of v8, /device:TPU:1, one launch (start us, length us, event | category | flops | bytes accessed | tf_op | source)
XLA Modules:
  0.0 104.9 jit_solution(7809299565373140436)
XLA Ops:
  0.0 0.0 copy-start.2
  0.0 0.9 copy-done.2
  1.0 0.0 copy-start.7
  1.0 0.8 copy-done.7
  1.8 0.1 shard_map.28
  1.9 4.8 %collective-permute-start = (f32[3,16,4,128]{3,2,1,0:T(4,128)S(1)}, f32[3,16,4,128]{3,2,1,0:T(4,128)S(1)}, u32[]{:S(2)}, u32[]{:S(2)}) collective-permute-start(f32[3,16,4,128]{3,2,1,0:T(4,128)S(1)} %get-tuple-element.23), channel_id=1, source_target_pairs={{0,4},{4,8},{8,12},{12,16},{16,20},{20,24},{24,28},{1,5},{5,9},{9,... | collective-permute-start | bytes 294920 | tf_op jit(solution)/shard_map/ppermute | solution.py:514
  6.7 1.3 %collective-permute-start.1 = (f32[3,16,4,128]{3,2,1,0:T(4,128)S(1)}, f32[3,16,4,128]{3,2,1,0:T(4,128)S(1)}, u32[]{:S(2)}, u32[]{:S(2)}) collective-permute-start(f32[3,16,4,128]{3,2,1,0:T(4,128)S(1)} %get-tuple-element.24), channel_id=1, source_target_pairs={{4,0},{8,4},{12,8},{16,12},{20,16},{24,20},{28,24},{5,1},{9,5},{13... | collective-permute-start | bytes 294920 | tf_op jit(solution)/shard_map/ppermute | solution.py:514
  8.0 0.3 collective-permute-done.ylo
  8.3 4.4 %collective-permute-done.1.yhi = f32[3,16,4,128]{3,2,1,0:T(4,128)S(1)} collective-permute-done((f32[3,16,4,128]{3,2,1,0:T(4,128)S(1)}, f32[3,16,4,128]{3,2,1,0:T(4,128)S(1)}, u32[]{:S(2)}, u32[]{:S(2)}) %collective-permute-start.1) | collective-permute-done | bytes 98336 | tf_op jit(solution)/shard_map/ppermute | solution.py:514
  12.7 3.9 %collective-permute-start.3 = (f32[3,3,24,128]{3,2,1,0:T(8,128)S(1)}, f32[3,3,24,128]{3,2,1,0:T(8,128)S(1)}, u32[]{:S(2)}, u32[]{:S(2)}) collective-permute-start(f32[3,3,24,128]{3,2,1,0:T(8,128)S(1)} %pad_maximum_fusion.3), channel_id=1, source_target_pairs={{0,480},{32,0},{64,32},{96,64},{128,96},{160,128},{192,160},{224,1... | collective-permute-start | bytes 331784 | tf_op jit(solution)/shard_map/ppermute | solution.py:514
  16.6 0.0 collective-permute-start.2
  16.6 1.5 %collective-permute-done.3.xhi = f32[3,3,24,128]{3,2,1,0:T(8,128)S(1)} collective-permute-done((f32[3,3,24,128]{3,2,1,0:T(8,128)S(1)}, f32[3,3,24,128]{3,2,1,0:T(8,128)S(1)}, u32[]{:S(2)}, u32[]{:S(2)}) %collective-permute-start.3) | collective-permute-done | bytes 110624 | tf_op jit(solution)/shard_map/ppermute | solution.py:514
  18.2 0.2 collective-permute-done.2.xlo
  18.4 0.6 shard_map.29
  19.0 2.9 %collective-permute-start.4 = (f32[16,1584]{1,0:T(8,128)S(1)}, f32[16,1584]{1,0:T(8,128)S(1)}, u32[]{:S(2)}, u32[]{:S(2)}) collective-permute-start(f32[16,1584]{1,0:T(8,128)S(1)} %get-tuple-element.26), channel_id=1, source_target_pairs={{0,1},{1,2},{2,3},{4,5},{5,6},{6,7},{8,9},{9,10},{10,11},{12,13},{... | collective-permute-start | bytes 304136 | tf_op jit(solution)/shard_map/ppermute | solution.py:514
  21.9 1.3 %collective-permute-start.5 = (f32[16,1584]{1,0:T(8,128)S(1)}, f32[16,1584]{1,0:T(8,128)S(1)}, u32[]{:S(2)}, u32[]{:S(2)}) collective-permute-start(f32[16,1584]{1,0:T(8,128)S(1)} %get-tuple-element.27), channel_id=1, source_target_pairs={{1,0},{2,1},{3,2},{5,4},{6,5},{7,6},{9,8},{10,9},{11,10},{13,12},{... | collective-permute-start | bytes 304136 | tf_op jit(solution)/shard_map/ppermute | solution.py:514
  23.2 0.4 collective-permute-done.4.lower
  23.6 3.8 %collective-permute-done.5.upper = f32[16,1584]{1,0:T(8,128)S(1)} collective-permute-done((f32[16,1584]{1,0:T(8,128)S(1)}, f32[16,1584]{1,0:T(8,128)S(1)}, u32[]{:S(2)}, u32[]{:S(2)}) %collective-permute-start.5) | collective-permute-done | bytes 101408 | tf_op jit(solution)/shard_map/ppermute | solution.py:514
  27.3 2.7 %shard_map.30.own = f32[3,8,8,128]{3,2,1,0:T(8,128)S(1)} custom-call(f32[3,22,24,128]{3,2,1,0:T(8,128)S(1)} %get-tuple-element.25.f, f32[16,1584]{1,0:T(8,128)S(1)} %collective-permute-done.4.lower, f32[16,1584]{1,0:T(8,128)S(1)} %collective-permute-done.5.upper), custom_call_target="tpu_custom_call" | custom-call | tf_op jit(solution)/shard_map/pallas_call | solution.py:498
  30.1 4.0 %collective-permute-start.6 = (f32[3,8,8,128]{3,2,1,0:T(8,128)S(1)}, f32[3,8,8,128]{3,2,1,0:T(8,128)S(1)}, u32[]{:S(2)}, u32[]{:S(2)}) collective-permute-start(f32[3,8,8,128]{3,2,1,0:T(8,128)S(1)} %shard_map.30.own), channel_id=1, source_target_pairs={{0,4},{4,8},{8,12},{12,16},{16,20},{20,24},{24,28},{1,5},{5,9},{9,... | collective-permute-start | bytes 294920 | tf_op jit(solution)/shard_map/ppermute | solution.py:514
  34.1 1.3 %collective-permute-start.7 = (f32[3,8,8,128]{3,2,1,0:T(8,128)S(1)}, f32[3,8,8,128]{3,2,1,0:T(8,128)S(1)}, u32[]{:S(2)}, u32[]{:S(2)}) collective-permute-start(f32[3,8,8,128]{3,2,1,0:T(8,128)S(1)} %shard_map.30.own), channel_id=1, source_target_pairs={{4,0},{8,4},{12,8},{16,12},{20,16},{24,20},{28,24},{5,1},{9,5},{13... | collective-permute-start | bytes 294920 | tf_op jit(solution)/shard_map/ppermute | solution.py:514
  35.4 0.3 collective-permute-done.6.ylo
  35.7 5.6 %collective-permute-done.7.yhi = f32[3,8,8,128]{3,2,1,0:T(8,128)S(1)} collective-permute-done((f32[3,8,8,128]{3,2,1,0:T(8,128)S(1)}, f32[3,8,8,128]{3,2,1,0:T(8,128)S(1)}, u32[]{:S(2)}, u32[]{:S(2)}) %collective-permute-start.7) | collective-permute-done | bytes 98336 | tf_op jit(solution)/shard_map/ppermute | solution.py:514
  41.4 6.1 %collective-permute-start.9 = (f32[3,6,24,128]{3,2,1,0:T(8,128)S(1)}, f32[3,6,24,128]{3,2,1,0:T(8,128)S(1)}, u32[]{:S(2)}, u32[]{:S(2)}) collective-permute-start(f32[3,6,24,128]{3,2,1,0:T(8,128)S(1)} %pad_maximum_fusion.1), channel_id=1, source_target_pairs={{0,480},{32,0},{64,32},{96,64},{128,96},{160,128},{192,160},{224,1... | collective-permute-start | bytes 663560 | tf_op jit(solution)/shard_map/ppermute | solution.py:514
  47.5 0.0 collective-permute-start.8
  47.5 1.8 %collective-permute-done.9.xhi = f32[3,6,24,128]{3,2,1,0:T(8,128)S(1)} collective-permute-done((f32[3,6,24,128]{3,2,1,0:T(8,128)S(1)}, f32[3,6,24,128]{3,2,1,0:T(8,128)S(1)}, u32[]{:S(2)}, u32[]{:S(2)}) %collective-permute-start.9) | collective-permute-done | bytes 221216 | tf_op jit(solution)/shard_map/ppermute | solution.py:514
  49.4 1.1 %collective-permute-done.8.xlo = f32[3,6,24,128]{3,2,1,0:T(8,128)S(1)} collective-permute-done((f32[3,6,24,128]{3,2,1,0:T(8,128)S(1)}, f32[3,6,24,128]{3,2,1,0:T(8,128)S(1)}, u32[]{:S(2)}, u32[]{:S(2)}) %collective-permute-start.8) | collective-permute-done | bytes 221216 | tf_op jit(solution)/shard_map/ppermute | solution.py:514
  50.4 2.5 %shard_map.31 = f32[32,9,2,128]{3,2,1,0:T(2,128)} custom-call(f32[3,8,8,128]{3,2,1,0:T(8,128)S(1)} %shard_map.30.own, f32[3,8,8,128]{3,2,1,0:T(8,128)S(1)} %collective-permute-done.6.ylo, f32[3,8,8,128]{3,2,1,0:T(8,128)S(1)} %collective-permute-done.7.yhi, f32[3,6,24,128]{3,2,1,0:T(8,128)S(1)} %collective-permute-done.8.xlo, ...), custom_call_target="tpu_custom_call" | custom-call | tf_op jit(solution)/shard_map/pallas_call | solution.py:498
  52.9 8.8 %all-to-all-start = ((f32[32,9,2,128]{3,2,1,0:T(2,128)}), f32[32,9,2,128]{3,2,1,0:T(2,128)S(1)}, u32[]{:S(2)}, u32[]{:S(2)}) async-start(f32[32,9,2,128]{3,2,1,0:T(2,128)} %shard_map.31), calls=%async_computation | async-start | bytes 589824 | tf_op jit(solution)/shard_map/all_to_all | solution.py:556
  61.8 3.2 %shard_map.33 = (f32[2,16,16,128]{3,2,1,0:T(8,128)S(1)}, f32[3,18,24,256]{3,2,1,0:T(8,128)S(1)}) custom-call(f32[3,22,24,128]{3,2,1,0:T(8,128)S(1)} %get-tuple-element.25.f, f32[16,1584]{1,0:T(8,128)S(1)} %collective-permute-done.4.lower, f32[16,1584]{1,0:T(8,128)S(1)} %collective-permute-done.5.upper), custom_call_target="tpu_custom_call" | custom-call | flops 62914560 | bytes 8388608 | tf_op jit(solution)/shard_map/pallas_call | solution.py:498
  65.0 0.0 copy-start
  65.0 0.7 copy-done
  65.7 1.5 %shard_map.32 = (f32[2,10,16,128]{3,2,1,0:T(8,128)S(1)}, f32[3,12,16,128]{3,2,1,0:T(8,128)S(1)}, f32[12,16,128]{2,1,0:T(8,128)S(1)}) custom-call(f32[3,8,8,128]{3,2,1,0:T(8,128)S(1)} %shard_map.30.own, f32[3,8,8,128]{3,2,1,0:T(8,128)S(1)} %collective-permute-done.6.ylo, f32[3,8,8,128]{3,2,1,0:T(8,128)S(1)} %collective-permute-done.7.yhi, ...), custom_call_target="tpu_custom_call" | custom-call | flops 8388608 | bytes 1048576 | tf_op jit(solution)/shard_map/pallas_call | solution.py:498
  67.2 0.7 copy-done.3
  67.8 0.6 copy-done.5
  68.4 4.0 %all-to-all-done.parts = f32[32,9,2,128]{3,2,1,0:T(2,128)S(1)} async-done(((f32[32,9,2,128]{3,2,1,0:T(2,128)}), f32[32,9,2,128]{3,2,1,0:T(2,128)S(1)}, u32[]{:S(2)}, u32[]{:S(2)}) %all-to-all-start) | async-done | bytes 294944 | tf_op jit(solution)/shard_map/all_to_all | solution.py:556
  72.5 0.9 shard_map.34
  73.4 10.7 %all-to-all-start.1 = ((f32[16,48,128]{2,1,0:T(8,128)}), f32[16,48,128]{2,1,0:T(8,128)S(1)}, u32[]{:S(2)}, u32[]{:S(2)}) async-start(f32[16,48,128]{2,1,0:T(8,128)} %shard_map.34), calls=%async_computation.1 | async-start | bytes 786432 | tf_op jit(solution)/shard_map/all_to_all | solution.py:573
  84.1 1.6 %collective-permute-start.10 = (f32[36,4,128]{2,1,0:T(4,128)S(1)}, f32[36,4,128]{2,1,0:T(4,128)S(1)}, u32[]{:S(2)}, u32[]{:S(2)}) collective-permute-start(f32[36,4,128]{2,1,0:T(4,128)S(1)} %shard_map.35.own), channel_id=1, source_target_pairs={{0,32},{32,64},{64,96},{96,128},{128,160},{160,192},{192,224},{224... | collective-permute-start | bytes 221192 | tf_op jit(solution)/shard_map/ppermute | solution.py:514
  85.8 0.0 collective-permute-start.11
  85.8 7.1 %collective-permute-done.10.west = f32[36,4,128]{2,1,0:T(4,128)S(1)} collective-permute-done((f32[36,4,128]{2,1,0:T(4,128)S(1)}, f32[36,4,128]{2,1,0:T(4,128)S(1)}, u32[]{:S(2)}, u32[]{:S(2)}) %collective-permute-start.10) | collective-permute-done | bytes 73760 | tf_op jit(solution)/shard_map/ppermute | solution.py:514
  92.8 3.4 %collective-permute-done.11.east = f32[36,4,128]{2,1,0:T(4,128)S(1)} collective-permute-done((f32[36,4,128]{2,1,0:T(4,128)S(1)}, f32[36,4,128]{2,1,0:T(4,128)S(1)}, u32[]{:S(2)}, u32[]{:S(2)}) %collective-permute-start.11) | collective-permute-done | bytes 73760 | tf_op jit(solution)/shard_map/ppermute | solution.py:514
  96.2 1.1 %shard_map.36.a = f32[4,12,16,128]{3,2,1,0:T(8,128)S(1)} custom-call(f32[36,4,128]{2,1,0:T(4,128)S(1)} %collective-permute-done.10.west, f32[36,4,128]{2,1,0:T(4,128)S(1)} %shard_map.35.own, f32[36,4,128]{2,1,0:T(4,128)S(1)} %collective-permute-done.11.east), custom_call_target="tpu_custom_call" | custom-call | flops 4194304 | bytes 1048576 | tf_op jit(solution)/shard_map/pallas_call | solution.py:498
  97.3 1.3 %all-to-all-done.1.parts3 = f32[16,48,128]{2,1,0:T(8,128)S(1)} async-done(((f32[16,48,128]{2,1,0:T(8,128)}), f32[16,48,128]{2,1,0:T(8,128)S(1)}, u32[]{:S(2)}, u32[]{:S(2)}) %all-to-all-start.1) | async-done | bytes 393248 | tf_op jit(solution)/shard_map/all_to_all | solution.py:573
  98.6 0.0 copy-done.1
  98.6 0.0 copy-done.4
  98.7 0.0 copy-done.6
  98.7 6.3 %shard_map.37 = f32[2,16,16,128]{3,2,1,0:T(8,128)} custom-call(f32[16,48,128]{2,1,0:T(8,128)S(1)} %all-to-all-done.1.parts3, f32[4,12,16,128]{3,2,1,0:T(8,128)S(1)} %shard_map.36.a, f32[12,16,128]{2,1,0:T(8,128)S(1)} %copy-done.6, f32[2,10,16,128]{3,2,1,0:T(8,128)S(1)} %copy-done.4, f32[3,12,16,128]{3,2,1,0:T(8,128)S(1)} %get-tuple-element.36.coef1, ...), custom_call_target="tpu_custom_call" | custom-call | tf_op jit(solution)/shard_map/pallas_call | solution.py:498
  (16 shorter events, 0.2 us)
Async XLA Ops:
  0.0 0.9 copy-start.2
  1.0 0.8 copy-start.7
  1.9 6.5 %collective-permute-start = (f32[3,16,4,128]{3,2,1,0:T(4,128)S(1)}, f32[3,16,4,128]{3,2,1,0:T(4,128)S(1)}, u32[]{:S(2)}, u32[]{:S(2)}) collective-permute-start(f32[3,16,4,128]{3,2,1,0:T(4,128)S(1)} %get-tuple-element.23), channel_id=1, source_target_pairs={{0,4},{4,8},{8,12},{12,16},{16,20},{20,24},{24,28},{1,5},{5,9},{9,... | collective-permute-start | bytes 294920 | tf_op jit(solution)/shard_map/ppermute | solution.py:514
  6.7 6.0 %collective-permute-start.1 = (f32[3,16,4,128]{3,2,1,0:T(4,128)S(1)}, f32[3,16,4,128]{3,2,1,0:T(4,128)S(1)}, u32[]{:S(2)}, u32[]{:S(2)}) collective-permute-start(f32[3,16,4,128]{3,2,1,0:T(4,128)S(1)} %get-tuple-element.24), channel_id=1, source_target_pairs={{4,0},{8,4},{12,8},{16,12},{20,16},{24,20},{28,24},{5,1},{9,5},{13... | collective-permute-start | bytes 294920 | tf_op jit(solution)/shard_map/ppermute | solution.py:514
  12.7 5.5 %collective-permute-start.3 = (f32[3,3,24,128]{3,2,1,0:T(8,128)S(1)}, f32[3,3,24,128]{3,2,1,0:T(8,128)S(1)}, u32[]{:S(2)}, u32[]{:S(2)}) collective-permute-start(f32[3,3,24,128]{3,2,1,0:T(8,128)S(1)} %pad_maximum_fusion.3), channel_id=1, source_target_pairs={{0,480},{32,0},{64,32},{96,64},{128,96},{160,128},{192,160},{224,1... | collective-permute-start | bytes 331784 | tf_op jit(solution)/shard_map/ppermute | solution.py:514
  16.6 1.8 %collective-permute-start.2 = (f32[3,3,24,128]{3,2,1,0:T(8,128)S(1)}, f32[3,3,24,128]{3,2,1,0:T(8,128)S(1)}, u32[]{:S(2)}, u32[]{:S(2)}) collective-permute-start(f32[3,3,24,128]{3,2,1,0:T(8,128)S(1)} %pad_maximum_fusion.2), channel_id=1, source_target_pairs={{0,32},{32,64},{64,96},{96,128},{128,160},{160,192},{192,224},{224... | collective-permute-start | bytes 331784 | tf_op jit(solution)/shard_map/ppermute | solution.py:514
  19.0 4.6 %collective-permute-start.4 = (f32[16,1584]{1,0:T(8,128)S(1)}, f32[16,1584]{1,0:T(8,128)S(1)}, u32[]{:S(2)}, u32[]{:S(2)}) collective-permute-start(f32[16,1584]{1,0:T(8,128)S(1)} %get-tuple-element.26), channel_id=1, source_target_pairs={{0,1},{1,2},{2,3},{4,5},{5,6},{6,7},{8,9},{9,10},{10,11},{12,13},{... | collective-permute-start | bytes 304136 | tf_op jit(solution)/shard_map/ppermute | solution.py:514
  21.9 5.4 %collective-permute-start.5 = (f32[16,1584]{1,0:T(8,128)S(1)}, f32[16,1584]{1,0:T(8,128)S(1)}, u32[]{:S(2)}, u32[]{:S(2)}) collective-permute-start(f32[16,1584]{1,0:T(8,128)S(1)} %get-tuple-element.27), channel_id=1, source_target_pairs={{1,0},{2,1},{3,2},{5,4},{6,5},{7,6},{9,8},{10,9},{11,10},{13,12},{... | collective-permute-start | bytes 304136 | tf_op jit(solution)/shard_map/ppermute | solution.py:514
  30.1 5.6 %collective-permute-start.6 = (f32[3,8,8,128]{3,2,1,0:T(8,128)S(1)}, f32[3,8,8,128]{3,2,1,0:T(8,128)S(1)}, u32[]{:S(2)}, u32[]{:S(2)}) collective-permute-start(f32[3,8,8,128]{3,2,1,0:T(8,128)S(1)} %shard_map.30.own), channel_id=1, source_target_pairs={{0,4},{4,8},{8,12},{12,16},{16,20},{20,24},{24,28},{1,5},{5,9},{9,... | collective-permute-start | bytes 294920 | tf_op jit(solution)/shard_map/ppermute | solution.py:514
  34.1 7.2 %collective-permute-start.7 = (f32[3,8,8,128]{3,2,1,0:T(8,128)S(1)}, f32[3,8,8,128]{3,2,1,0:T(8,128)S(1)}, u32[]{:S(2)}, u32[]{:S(2)}) collective-permute-start(f32[3,8,8,128]{3,2,1,0:T(8,128)S(1)} %shard_map.30.own), channel_id=1, source_target_pairs={{4,0},{8,4},{12,8},{16,12},{20,16},{24,20},{28,24},{5,1},{9,5},{13... | collective-permute-start | bytes 294920 | tf_op jit(solution)/shard_map/ppermute | solution.py:514
  41.4 8.0 %collective-permute-start.9 = (f32[3,6,24,128]{3,2,1,0:T(8,128)S(1)}, f32[3,6,24,128]{3,2,1,0:T(8,128)S(1)}, u32[]{:S(2)}, u32[]{:S(2)}) collective-permute-start(f32[3,6,24,128]{3,2,1,0:T(8,128)S(1)} %pad_maximum_fusion.1), channel_id=1, source_target_pairs={{0,480},{32,0},{64,32},{96,64},{128,96},{160,128},{192,160},{224,1... | collective-permute-start | bytes 663560 | tf_op jit(solution)/shard_map/ppermute | solution.py:514
  47.5 2.9 %collective-permute-start.8 = (f32[3,6,24,128]{3,2,1,0:T(8,128)S(1)}, f32[3,6,24,128]{3,2,1,0:T(8,128)S(1)}, u32[]{:S(2)}, u32[]{:S(2)}) collective-permute-start(f32[3,6,24,128]{3,2,1,0:T(8,128)S(1)} %pad_maximum_fusion), channel_id=1, source_target_pairs={{0,32},{32,64},{64,96},{96,128},{128,160},{160,192},{192,224},{224... | collective-permute-start | bytes 663560 | tf_op jit(solution)/shard_map/ppermute | solution.py:514
  52.9 19.6 %all-to-all-start = ((f32[32,9,2,128]{3,2,1,0:T(2,128)}), f32[32,9,2,128]{3,2,1,0:T(2,128)S(1)}, u32[]{:S(2)}, u32[]{:S(2)}) async-start(f32[32,9,2,128]{3,2,1,0:T(2,128)} %shard_map.31), calls=%async_computation | async-start | bytes 589824 | tf_op jit(solution)/shard_map/all_to_all | solution.py:556
  65.0 0.7 copy-start
  67.1 0.7 copy-start.3
  67.8 0.6 copy-start.5
  68.4 30.2 %copy-start.1 = (f32[2,16,16,128]{3,2,1,0:T(8,128)S(1)}, f32[2,16,16,128]{3,2,1,0:T(8,128)}, u32[]{:S(2)}) copy-start(f32[2,16,16,128]{3,2,1,0:T(8,128)} %copy-done) | copy-start | bytes 786436
  72.5 26.2 %copy-start.4 = (f32[2,10,16,128]{3,2,1,0:T(8,128)S(1)}, f32[2,10,16,128]{3,2,1,0:T(8,128)}, u32[]{:S(2)}) copy-start(f32[2,10,16,128]{3,2,1,0:T(8,128)} %copy-done.3) | copy-start | bytes 491524
  72.5 26.2 %copy-start.6 = (f32[12,16,128]{2,1,0:T(8,128)S(1)}, f32[12,16,128]{2,1,0:T(8,128)}, u32[]{:S(2)}) copy-start(f32[12,16,128]{2,1,0:T(8,128)} %copy-done.5) | copy-start | bytes 294916
  73.4 25.3 %all-to-all-start.1 = ((f32[16,48,128]{2,1,0:T(8,128)}), f32[16,48,128]{2,1,0:T(8,128)S(1)}, u32[]{:S(2)}, u32[]{:S(2)}) async-start(f32[16,48,128]{2,1,0:T(8,128)} %shard_map.34), calls=%async_computation.1 | async-start | bytes 786432 | tf_op jit(solution)/shard_map/all_to_all | solution.py:573
  84.1 8.7 %collective-permute-start.10 = (f32[36,4,128]{2,1,0:T(4,128)S(1)}, f32[36,4,128]{2,1,0:T(4,128)S(1)}, u32[]{:S(2)}, u32[]{:S(2)}) collective-permute-start(f32[36,4,128]{2,1,0:T(4,128)S(1)} %shard_map.35.own), channel_id=1, source_target_pairs={{0,32},{32,64},{64,96},{96,128},{128,160},{160,192},{192,224},{224... | collective-permute-start | bytes 221192 | tf_op jit(solution)/shard_map/ppermute | solution.py:514
  85.8 10.4 %collective-permute-start.11 = (f32[36,4,128]{2,1,0:T(4,128)S(1)}, f32[36,4,128]{2,1,0:T(4,128)S(1)}, u32[]{:S(2)}, u32[]{:S(2)}) collective-permute-start(f32[36,4,128]{2,1,0:T(4,128)S(1)} %shard_map.35.own), channel_id=1, source_target_pairs={{0,480},{32,0},{64,32},{96,64},{128,96},{160,128},{192,160},{224,1... | collective-permute-start | bytes 221192 | tf_op jit(solution)/shard_map/ppermute | solution.py:514
